TPU v7x, 32 devices: a whole 2x2x4 slice. The times are simulated.
32 devices in a mesh: tm: 4 (over y, x), res: 8 (over z, core).
Axes of the slice: x: 2, y: 2, z: 4, core: 2. Of those that a mesh axis runs over, the one named last changes fastest.
Arguments:
- node_feats: bfloat16 [4, 1024, 512], P('tm', 'res'), may hold values from -6 to 6
- edge_feats: bfloat16 [4, 1024, 60, 192], P('tm', 'res'), may hold values from -6 to 6
- node_cotan: bfloat16 [4, 1024, 512], P('tm', 'res'), may hold values from -6 to 6
- edge_cotan: bfloat16 [4, 1024, 60, 192], P('tm', 'res'), may hold values from -6 to 6
- neighbour: int32 [1024, 60], P('res'), may hold values from 0 to 383, as said below
- edge_mask: int32 [1024, 60], P('res'), may hold values from 0 to 1, as said below
- fetch_rows: int32 [8, 8, 32], P('res'), may hold values from 0 to 1023, as said below
- chain_ids: int32 [1024], P('res'), may hold values from 0 to 23, as said below
- complex_flag: int32 [1024], P('res'), may hold values from 0 to 1, as said below
- message_in: bfloat16 [1216, 512], replicated, may hold values from -0.15625 to 0.15625
- message_mid: bfloat16 [512, 512], replicated, may hold values from -0.25 to 0.25
- message_out: bfloat16 [512, 512], replicated, may hold values from -0.75 to 0.75
- gain_node: bfloat16 [512], replicated, may hold values from 0.5 to 1.5
- offset_node: bfloat16 [512], replicated, may hold values from -3 to 3
- expand_weight: bfloat16 [512, 2048], replicated, may hold values from -0.25 to 0.25
- contract_weight: bfloat16 [2048, 512], replicated, may hold values from -0.125 to 0.125
- gain_ffn: bfloat16 [512], replicated, may hold values from 0.5 to 1.5
- offset_ffn: bfloat16 [512], replicated, may hold values from -3 to 3
- update_in: bfloat16 [1216, 192], replicated, may hold values from -0.15625 to 0.15625
- update_mid: bfloat16 [192, 192], replicated, may hold values from -0.4375 to 0.4375
- update_out: bfloat16 [192, 192], replicated, may hold values from -0.4375 to 0.4375
- gain_edge: bfloat16 [192], replicated, may hold values from 0.5 to 1.5
- offset_edge: bfloat16 [192], replicated, may hold values from -3 to 3
Outputs:
- node_out: bfloat16 [4, 1024, 512], P('tm', 'res')
- edge_out: bfloat16 [4, 1024, 60, 192], P('tm', 'res')
- node_grad: float32 [4, 1024, 512], P('tm', 'res')
- edge_grad: float32 [4, 1024, 60, 192], P('tm', 'res')
- grad_message_in: float32 [1216, 512], replicated
- grad_message_mid: float32 [512, 512], replicated
- grad_message_out: float32 [512, 512], replicated
- grad_gain_node: float32 [512], replicated
- grad_offset_node: float32 [512], replicated
- grad_expand: float32 [512, 2048], replicated
- grad_contract: float32 [2048, 512], replicated
- grad_gain_ffn: float32 [512], replicated
- grad_offset_ffn: float32 [512], replicated
- grad_update_in: float32 [1216, 192], replicated
- grad_update_mid: float32 [192, 192], replicated
- grad_update_out: float32 [192, 192], replicated
- grad_gain_edge: float32 [192], replicated
- grad_offset_edge: float32 [192], replicated
Inputs may be any that keep to these rules, and one draw needn't show every extreme that they name: `neighbour`: below 128 an entry names a residue of the own block; an entry s of 128 or more names the residue fetch_rows[block, (s - 128) // 32, (s - 128) % 32]. fetch_rows[d, p] holds 32 distinct residues of block p, that is of p * 128 to (p + 1) * 128 - 1. `chain_ids`: never falls along residues; no chain crosses from one block of 128 residues to the next. `complex_flag`: equal for all residues of a chain; the first chain of every block is in the complex. `edge_mask`: some residues are padding with no live edge.
All inputs are finite; a program needn't handle non-finite values.
Results may differ from a plain program's by a relative error of at most 0.02.
Values may be sent and summed in bfloat16 or wider, within the bound.
A program may use at most 256 MiB of HBM per device.

v0:
```python
import jax
import jax.numpy as jnp
from jax import lax
from jax.sharding import PartitionSpec as P

EPSILON = 1e-05


def activate(values):
    return jax.nn.gelu(values, approximate=True)


def layer_norm(values, gain_vec, offset):
    centred = values - jnp.mean(values, axis=-1, keepdims=True)
    spread = jnp.mean(centred * centred, axis=-1, keepdims=True)
    return centred * lax.rsqrt(spread + EPSILON) * gain_vec + offset


def forward_dot(left_op, right_op):
    return jnp.dot(left_op, right_op, preferred_element_type=jnp.float32)


def weight_grad(inputs, grad_rows):
    return lax.dot_general(
        inputs, grad_rows, (((0,), (0,)), ((), ())), preferred_element_type=jnp.float32
    )


def input_grad(grad_rows, weight):
    return lax.dot_general(
        grad_rows, weight, (((1,), (1,)), ((), ())), preferred_element_type=jnp.float32
    )


def edge_dot(edges, weight):
    return jnp.einsum("rke,ef->rkf", edges, weight, preferred_element_type=jnp.float32)


def edge_weight_grad(edges, grads):
    return jnp.einsum("rke,rkf->ef", edges, grads, preferred_element_type=jnp.float32)


def edge_input_grad(grads, weight):
    return jnp.einsum("rkf,ef->rke", grads, weight, preferred_element_type=jnp.float32)


def through_gate(pre_act, grad_out):
    unused, pullback = jax.vjp(activate, pre_act)
    return pullback(grad_out)[0].astype(jnp.bfloat16)


def one_hot_rows(indices, table_len):
    return (indices[:, None] == jnp.arange(table_len, dtype=jnp.int32)[None, :]).astype(
        jnp.bfloat16
    )


def pick_rows(picker, table):
    upper = table.astype(jnp.bfloat16)
    lower = (table - upper.astype(jnp.float32)).astype(jnp.bfloat16)
    return jnp.einsum(
        "rkl,ld->rkd", picker, upper, preferred_element_type=jnp.float32
    ) + jnp.einsum("rkl,ld->rkd", picker, lower, preferred_element_type=jnp.float32)


def table_grad(picker, grads):
    return jnp.einsum("rkl,rkd->ld", picker, grads, preferred_element_type=jnp.float32)


def message_pass(self_proj, table_proj, picker, edge_in, edge_weight, mid_weight, out_weight):
    gathered = pick_rows(picker, table_proj)
    pre_one = self_proj[:, None, :] + gathered + edge_dot(edge_in, edge_weight)
    hidden_one = activate(pre_one).astype(jnp.bfloat16)
    pre_two = edge_dot(hidden_one, mid_weight)
    hidden_two = activate(pre_two).astype(jnp.bfloat16)
    return (pre_one, hidden_one, pre_two, hidden_two, edge_dot(hidden_two, out_weight))


def local(
    node_feats,
    edge_feats,
    node_cotan,
    edge_cotan,
    neighbour,
    edge_mask,
    fetch_rows,
    chain_ids,
    complex_flag,
    message_in,
    message_mid,
    message_out,
    gain_node,
    offset_node,
    expand_weight,
    contract_weight,
    gain_ffn,
    offset_ffn,
    update_in,
    update_mid,
    update_out,
    gain_edge,
    offset_edge,
):
    row_count, fanout = neighbour.shape
    feat_width = node_feats.shape[2]
    peer_count = fetch_rows.shape[1]
    slot_count = fetch_rows.shape[2]
    table_len = row_count + peer_count * slot_count
    node_in = node_feats[0]
    edge_in = edge_feats[0]
    wanted = fetch_rows[0].reshape(peer_count * slot_count)
    my_index = lax.axis_index("res")
    own_ids = my_index * row_count + jnp.arange(row_count, dtype=jnp.int32)
    table_ids = jnp.concatenate([own_ids, wanted], axis=0)
    tag_local = chain_ids * 2 + complex_flag
    picker = (
        neighbour[:, :, None] == jnp.arange(table_len, dtype=jnp.int32)[None, None, :]
    ).astype(jnp.bfloat16)
    all_rows, all_tags = (
        lax.all_gather(node_in, "res", axis=0, tiled=True),
        lax.all_gather(tag_local, "res", axis=0, tiled=True),
    )
    wanted_picker = one_hot_rows(wanted, peer_count * row_count)
    far_rows = forward_dot(wanted_picker, all_rows).astype(jnp.bfloat16)
    far_tags = jnp.take(all_tags, wanted)
    table_rows = jnp.concatenate([node_in, far_rows], axis=0)
    table_tags = jnp.concatenate([tag_local, far_tags], axis=0)
    other_tag = jnp.take(table_tags, neighbour, axis=0)
    joined = jnp.logical_or(
        chain_ids[:, None] == other_tag // 2, complex_flag[:, None] * (other_tag % 2) > 0
    )
    keep = edge_mask.astype(jnp.float32) * joined.astype(jnp.float32)
    counted = jnp.maximum(jnp.sum(keep, axis=1), 1.0)
    self_weight = message_in[:feat_width]
    neigh_weight = message_in[feat_width : 2 * feat_width]
    message_edge = message_in[2 * feat_width :]
    self_proj = forward_dot(node_in, self_weight)
    table_proj = forward_dot(table_rows, neigh_weight)
    kept = message_pass(
        self_proj, table_proj, picker, edge_in, message_edge, message_mid, message_out
    )
    aggregate = jnp.sum(kept[4] * keep[:, :, None], axis=1) / counted[:, None]
    first, first_pull = jax.vjp(
        layer_norm,
        node_in.astype(jnp.float32) + aggregate,
        gain_node.astype(jnp.float32),
        offset_node.astype(jnp.float32),
    )
    first_low = first.astype(jnp.bfloat16)
    inner = forward_dot(first_low, expand_weight)
    acted = activate(inner).astype(jnp.bfloat16)
    ffn_out = forward_dot(acted, contract_weight)
    updated, second_pull = jax.vjp(
        layer_norm, first + ffn_out, gain_ffn.astype(jnp.float32), offset_ffn.astype(jnp.float32)
    )
    updated_low = updated.astype(jnp.bfloat16)
    far_new = forward_dot(
        wanted_picker, lax.all_gather(updated_low, "res", axis=0, tiled=True)
    ).astype(jnp.bfloat16)
    table_new = jnp.concatenate([updated_low, far_new], axis=0)
    update_self = update_in[:feat_width]
    update_neigh = update_in[feat_width : 2 * feat_width]
    update_edge = update_in[2 * feat_width :]
    self_edge = forward_dot(updated_low, update_self)
    table_edge = forward_dot(table_new, update_neigh)
    gathered_edge = pick_rows(picker, table_edge)
    pre_three = self_edge[:, None, :] + gathered_edge + edge_dot(edge_in, update_edge)
    hidden_three = activate(pre_three).astype(jnp.bfloat16)
    pre_four = edge_dot(hidden_three, update_mid)
    hidden_four = activate(pre_four).astype(jnp.bfloat16)
    branch = edge_dot(hidden_four, update_out)
    edge_new, third_pull = jax.vjp(
        layer_norm,
        edge_in.astype(jnp.float32) + branch,
        gain_edge.astype(jnp.float32),
        offset_edge.astype(jnp.float32),
    )
    delta_resid, grad_gain_edge, grad_offset_edge = third_pull(edge_cotan[0].astype(jnp.float32))
    delta_branch = delta_resid.astype(jnp.bfloat16)
    grad_update_out = edge_weight_grad(hidden_four, delta_branch)
    delta_four = through_gate(pre_four, edge_input_grad(delta_branch, update_out))
    grad_update_mid = edge_weight_grad(hidden_three, delta_four)
    delta_three = through_gate(pre_three, edge_input_grad(delta_four, update_mid))
    grad_update_edge = edge_weight_grad(edge_in, delta_three)
    delta_edge_in = delta_resid + edge_input_grad(delta_three, update_edge)
    delta_self_edge = jnp.sum(delta_three, axis=1, dtype=jnp.float32).astype(jnp.bfloat16)
    delta_table_edge = table_grad(picker, delta_three)
    table_picker = one_hot_rows(table_ids, peer_count * row_count).astype(jnp.float32)
    spread_edge = lax.dot_general(
        table_picker, delta_table_edge, (((0,), (0,)), ((), ())), precision=lax.Precision.HIGHEST
    )
    own_edge = lax.psum_scatter(
        spread_edge.astype(jnp.bfloat16), "res", scatter_dimension=0, tiled=True
    )
    grad_update_self = weight_grad(updated_low, delta_self_edge)
    grad_update_neigh = weight_grad(updated_low, own_edge)
    delta_updated = (
        node_cotan[0].astype(jnp.float32)
        + input_grad(delta_self_edge, update_self)
        + input_grad(own_edge, update_neigh)
    )
    delta_second, grad_gain_ffn, grad_offset_ffn = second_pull(delta_updated)
    delta_ffn = delta_second.astype(jnp.bfloat16)
    grad_contract = weight_grad(acted, delta_ffn)
    delta_inner = through_gate(inner, input_grad(delta_ffn, contract_weight))
    grad_expand = weight_grad(first_low, delta_inner)
    delta_first = delta_second + input_grad(delta_inner, expand_weight)
    delta_first_in, grad_gain_node, grad_offset_node = first_pull(delta_first)
    delta_message = ((delta_first_in / counted[:, None])[:, None, :] * keep[:, :, None]).astype(
        jnp.bfloat16
    )
    pre_one, hidden_one, pre_two, hidden_two, unused_message = kept
    grad_message_out = edge_weight_grad(hidden_two, delta_message)
    delta_two = through_gate(pre_two, edge_input_grad(delta_message, message_out))
    grad_message_mid = edge_weight_grad(hidden_one, delta_two)
    delta_one = through_gate(pre_one, edge_input_grad(delta_two, message_mid))
    grad_message_edge = edge_weight_grad(edge_in, delta_one)
    delta_edge_in = delta_edge_in + edge_input_grad(delta_one, message_edge)
    delta_self = jnp.sum(delta_one, axis=1, dtype=jnp.float32).astype(jnp.bfloat16)
    delta_table = table_grad(picker, delta_one)
    spread_node = lax.dot_general(
        table_picker, delta_table, (((0,), (0,)), ((), ())), precision=lax.Precision.HIGHEST
    )
    own_node = lax.psum_scatter(
        spread_node.astype(jnp.bfloat16), "res", scatter_dimension=0, tiled=True
    )
    grad_message_self = weight_grad(node_in, delta_self)
    grad_message_neigh = weight_grad(node_in, own_node)
    delta_node_in = (
        delta_first_in + input_grad(delta_self, self_weight) + input_grad(own_node, neigh_weight)
    )
    grad_message_in = jnp.concatenate(
        [grad_message_self, grad_message_neigh, grad_message_edge], axis=0
    )
    grad_update_in = jnp.concatenate(
        [grad_update_self, grad_update_neigh, grad_update_edge], axis=0
    )
    totals = lax.psum(
        (
            grad_message_in,
            grad_message_mid,
            grad_message_out,
            grad_gain_node,
            grad_offset_node,
            grad_expand,
            grad_contract,
            grad_gain_ffn,
            grad_offset_ffn,
            grad_update_in,
            grad_update_mid,
            grad_update_out,
            grad_gain_edge,
            grad_offset_edge,
        ),
        ("tm", "res"),
    )
    return (
        updated_low[None],
        edge_new.astype(jnp.bfloat16)[None],
        delta_node_in[None],
        delta_edge_in[None],
        totals[0],
        totals[1],
        totals[2],
        totals[3],
        totals[4],
        totals[5],
        totals[6],
        totals[7],
        totals[8],
        totals[9],
        totals[10],
        totals[11],
        totals[12],
        totals[13],
    )


def solution(mesh):
    placed = (
        P("tm", "res", None),
        P("tm", "res", None, None),
        P("tm", "res", None),
        P("tm", "res", None, None),
        P("res", None),
        P("res", None),
        P("res", None, None),
        P("res"),
        P("res"),
        P(),
        P(),
        P(),
        P(),
        P(),
        P(),
        P(),
        P(),
        P(),
        P(),
        P(),
        P(),
        P(),
        P(),
    )
    return jax.shard_map(
        local,
        mesh=mesh,
        in_specs=placed,
        out_specs=(
            P("tm", "res", None),
            P("tm", "res", None, None),
            P("tm", "res", None),
            P("tm", "res", None, None),
            P(),
            P(),
            P(),
            P(),
            P(),
            P(),
            P(),
            P(),
            P(),
            P(),
            P(),
            P(),
            P(),
            P(),
        ),
        check_vma=False,
    )
```

profile of v0, /device:TPU:1, one launch (start us, length us, event | category | flops | bytes accessed | tf_op | source)
XLA Modules:
  0.0 620.5 jit_solution(12304324607836840426)
XLA Ops:
  13.0 13.2 %all-gather.1 = s32[8,1,128]{2,1,0:T(1,128)S(1)} all-gather(s32[1,1,128]{2,1,0:T(1,128)S(1)} %bitcast.183), channel_id=1, replica_groups=mesh['tm'=4,'res'=8] {'res'}, dimensions={0}, use_global_device_ids=true | all-gather | bytes 4608 | tf_op jit(solution)/shard_map/all_gather | solution.py:121
  28.6 45.2 %gather_fusion.1 = s32[7680]{0:T(1024)S(1)} fusion(s32[384]{0:T(512)S(1)} %pad_add_fusion, s32[8192]{0:T(1024)S(1)} %pad_clamp_fusion), kind=kCustom, calls=%fused_computation.1 | custom fusion | bytes 92160 | tf_op jit(solution)/shard_map/jit(_take)/gather | solution.py:128
  75.7 9.6 %fusion.58 = f32[128,60,512]{2,0,1:T(8,128)} fusion(bf16[1,128,60,192]{1,3,2,0:T(8,128)(2,1)} %param.24, bf16[1216,512]{1,0:T(8,128)(2,1)} %param.32), kind=kOutput, calls=%fused_computation.85 | convolution fusion | flops 1509949440 | bytes 18874368 | tf_op jit(solution)/shard_map/rke,ef->rkf/dot_general | solution.py:36
  88.4 7.7 %fusion.18 = f32[128,60,512]{2,0,1:T(8,128)} fusion(s32[128,60]{0,1:T(8,128)S(1)} %copy-done.24, f32[384,512]{1,0:T(8,128)S(1)} %fusion.94), kind=kOutput, calls=%fused_computation.30 | convolution fusion | flops 3023634432 | bytes 16545792 | tf_op jit(solution)/shard_map/rkl,ld->rkd/dot_general | solution.py:63
  96.1 17.7 %add_add_fusion = f32[128,60,512]{2,0,1:T(8,128)} fusion(f32[128,60,512]{2,0,1:T(8,128)} %fusion.58, f32[128,60,512]{2,0,1:T(8,128)} %fusion.18, f32[128,512]{1,0:T(8,128)S(1)} %fusion.97, s32[128,60]{0,1:T(8,128)S(1)} %copy-done.24, f32[384,512]{1,0:T(8,128)S(1)} %fusion.94), kind=kOutput, calls=%fused_computation.24 | convolution fusion | flops 3034841088 | bytes 48265216 | tf_op jit(solution)/shard_map/rkl,ld->rkd/dot_general | solution.py:61
  113.9 16.2 %multiply_convert_fusion.1 = (bf16[128,60,512]{2,0,1:T(8,128)(2,1)S(1)}, f32[128,60,512]{2,0,1:T(8,128)}) fusion(bf16[512,512]{1,0:T(8,128)(2,1)} %param.33, f32[128,60,512]{2,0,1:T(8,128)} %add_add_fusion), kind=kOutput, calls=%fused_computation.22 | convolution fusion | flops 4097310720 | bytes 39845888 | tf_op jit(solution)/shard_map/rke,ef->rkf/dot_general | solution.py:36
  130.1 4.5 multiply_reduce_fusion
  139.5 19.1 %all-gather.5.cloned.1.call-done = bf16[1024,512]{1,0:T(8,128)(2,1)} async-done(((bf16[128,512]{1,0:T(8,128)(2,1)}), bf16[1024,512]{1,0:T(8,128)(2,1)}) %all-gather.5.cloned.1.call-update) | async-done | bytes 1048592 | tf_op jit(solution)/shard_map/all_gather | solution.py:158
  177.3 6.6 %fusion.30 = (f32[192]{0:T(256)}, f32[128,60]{0,1:T(8,128)S(1)}, bf16[1,128,60,192]{1,3,2,0:T(8,128)(2,1)}) fusion(bf16[1,128,60,192]{1,3,2,0:T(8,128)(2,1)S(1)} %copy-done.3, f32[128,60,192]{0,2,1:T(8,128)S(1)} %get-tuple-element.58, f32[128,60]{0,1:T(8,128)S(1)} %get-tuple-element.52, f32[128,60]{0,1:T(8,128)S(1)} %broadcast_multiply_fusion, ...), kind=kLoop, calls=%fused_computation.49 | loop fusion | flops 20635968 | bytes 11921664 | tf_op jit(solution)/shard_map/transpose(jvp())/reduce_sum | solution.py:16
  184.0 4.3 convolution_bitcast_fusion.3
  188.3 6.4 %fusion.44 = bf16[128,60,192]{0,2,1:T(8,128)(2,1)S(1)} fusion(f32[128,60,192]{0,2,1:T(8,128)S(1)} %fusion.128, f32[128,60]{0,1:T(8,128)S(1)} %negate_multiply_fusion, bf16[192,192]{1,0:T(8,128)(2,1)S(1)} %copy-done.87, bf16[1,128,60,192]{1,3,2,0:T(8,128)(2,1)S(1)} %copy-done.3, f32[128,60,192]{0,2,1:T(8,128)S(1)} %get-tuple-element.58, ...), kind=kOutput, calls=%fused_computation.63 | convolution fusion | flops 608993280 | bytes 17892096 | tf_op jit(solution)/shard_map/rkf,ef->rke/dot_general | solution.py:44
  194.7 5.0 fusion.162
  209.7 6.2 %convolution_bitcast_fusion.4 = f32[192,192]{1,0:T(8,128)} fusion(bf16[128,60,192]{0,2,1:T(8,128)(2,1)} %copy-done.92, f32[128,60,192]{0,2,1:T(8,128)} %copy-done.9), kind=kOutput, calls=%fused_computation.113 | convolution fusion | flops 579502080 | bytes 8994816 | tf_op jit(solution)/shard_map/rke,rkf->ef/dot_general | solution.py:40
  215.9 18.5 %reduce-scatter.7.cloned.1.call-done = bf16[128,192]{1,0:T(8,128)(2,1)} async-done(((bf16[1024,192]{1,0:T(8,128)(2,1)}), bf16[128,192]{1,0:T(8,128)(2,1)}) %reduce-scatter.7.cloned.1.call-update) | async-done | bytes 49168
  241.3 8.7 %fusion.65 = f32[512,512]{1,0:T(8,128)} fusion(bf16[128,60,512]{2,0,1:T(8,128)(2,1)} %copy-done.91, f32[128,512]{1,0:T(8,128)S(1)} %add_divide_fusion, f32[128,60]{0,1:T(8,128)S(1)} %copy-done.49), kind=kOutput, calls=%fused_computation.94 | convolution fusion | flops 4034396160 | bytes 9205760 | tf_op jit(solution)/shard_map/rke,rkf->ef/dot_general | solution.py:40
  250.0 17.7 %fusion.13 = bf16[128,60,512]{2,0,1:T(8,128)(2,1)} fusion(f32[128,60,512]{2,0,1:T(8,128)} %get-tuple-element.54, f32[128,512]{1,0:T(8,128)S(1)} %add_divide_fusion, f32[128,60]{0,1:T(8,128)S(1)} %copy-done.49, bf16[512,512]{1,0:T(8,128)(2,1)S(1)} %copy-done.85), kind=kOutput, calls=%fused_computation.19 | convolution fusion | flops 4113039360 | bytes 24410112 | tf_op jit(solution)/shard_map/rkf,ef->rke/dot_general | solution.py:44
  267.7 15.9 %fusion.163 = (bf16[128,512]{1,0:T(8,128)(2,1)S(1)}, bf16[128,60,512]{2,0,1:T(8,128)(2,1)S(1)}) fusion(f32[128,60,512]{2,0,1:T(8,128)S(1)} %bitcast.180, bf16[128,60,512]{2,0,1:T(8,128)(2,1)} %fusion.13, bf16[512,512]{1,0:T(8,128)(2,1)S(1)} %copy-done.86), kind=kOutput, calls=%fused_computation.246 | convolution fusion | flops 4109041664 | bytes 32112640 | tf_op jit(solution)/shard_map/rkf,ef->rke/dot_general | solution.py:44
  283.7 6.5 %fusion.68 = f32[192,512]{1,0:T(8,128)} fusion(bf16[128,60,512]{2,0,1:T(8,128)(2,1)S(1)} %get-tuple-element.64, bf16[1,128,60,192]{1,3,2,0:T(8,128)(2,1)} %param.24), kind=kOutput, calls=%fused_computation.100 | convolution fusion | flops 1509949440 | bytes 11206656 | tf_op jit(solution)/shard_map/rke,rkf->ef/dot_general | solution.py:40
  303.7 12.2 %convolution_bitcast_fusion = f32[512,512]{1,0:T(8,128)} fusion(bf16[128,60,512]{2,0,1:T(8,128)(2,1)} %fusion.13, f32[128,60,512]{2,0,1:T(8,128)} %add_add_fusion), kind=kOutput, calls=%fused_computation.95 | convolution fusion | flops 4061921280 | bytes 24641536 | tf_op jit(solution)/shard_map/rke,rkf->ef/dot_general | solution.py:40
  315.9 16.8 %reduce-scatter.5.cloned.1.call-done = bf16[128,512]{1,0:T(8,128)(2,1)} async-done(((bf16[1024,512]{1,0:T(8,128)(2,1)}), bf16[128,512]{1,0:T(8,128)(2,1)}) %reduce-scatter.5.cloned.1.call-update) | async-done | bytes 131088 | tf_op jit(solution)/shard_map/reduce_scatter | solution.py:224
  339.1 43.9 %all-reduce = (f32[512]{0:T(512)}, f32[512]{0:T(512)}, f32[512]{0:T(512)}, f32[512]{0:T(512)}, f32[192]{0:T(256)}, /*index=5*/f32[192]{0:T(256)}) all-reduce(f32[512]{0:T(512)S(1)} %copy-done.66, f32[512]{0:T(512)S(1)} %copy-done.67, f32[512]{0:T(512)S(1)} %copy-done.64, ...), channel_id=1, replica_groups=mesh['tm'=4,'res'=8] {'tm','res'}, use_global_device_ids=true, to_apply=%region_22.23 | all-reduce | flops 2432 | bytes 19456 | tf_op jit(solution)/shard_map/psum | solution.py:238
  383.4 5.7 fusion.110
  389.4 6.5 %add_bitcast_fusion = f32[1,128,60,192]{1,3,2,0:T(8,128)} fusion(f32[128,60,192]{0,2,1:T(8,128)S(1)} %fusion.110, f32[128,60]{0,1:T(8,128)S(1)} %copy-done.41, bf16[128,60,192]{0,2,1:T(8,128)(2,1)S(1)} %copy-done.19, bf16[1216,192]{0,1:T(8,128)(2,1)} %param.41, f32[128,60]{0,1:T(8,128)S(1)} %copy-done.33, f32[128,60,192]{0,2,1:T(8,128)} %copy-done.2, ...), kind=kOutput, calls=%fused_computation.64 | convolution fusion | flops 580976640 | bytes 23814912 | tf_op jit(solution)/shard_map/rkf,ef->rke/dot_general | solution.py:44
  397.0 203.1 %all-reduce.4.cloned.1.call-done = (f32[1216,512]{1,0:T(8,128)}, f32[512,512]{1,0:T(8,128)}, f32[512,512]{1,0:T(8,128)}, f32[512,2048]{1,0:T(8,128)}, f32[2048,5...) async-done(((f32[1216,512]{1,0:T(8,128)}, f32[512,512]{1,0:T(8,128)}, f32[512,512]{1,0:T(8,128)}, f32[512,2048]{1,0:T(8,128)}, ...) | async-done | bytes 14204944 | tf_op jit(solution)/shard_map/psum | solution.py:238
  (293 shorter events, 87.3 us)
Async XLA Ops:
  7.2 127.8 %copy-start = (bf16[512,2048]{1,0:T(8,128)(2,1)S(1)}, bf16[512,2048]{1,0:T(8,128)(2,1)}, u32[]{:S(2)}) copy-start(bf16[512,2048]{1,0:T(8,128)(2,1)} %param.37) | copy-start | bytes 6291460
  7.2 78.1 %all-gather.7.cloned.1.call-start = ((), (), s32[]{:S(2)}) async-start(), calls=%async_computation.4 | async-start | bytes 1179648 | tf_op jit(solution)/shard_map/all_gather | solution.py:120
  7.9 150.7 %all-gather.5.cloned.1.call-start = ((), (), s32[]{:S(2)}) async-start(), calls=%async_computation.2 | async-start | bytes 1179648 | tf_op jit(solution)/shard_map/all_gather | solution.py:158
  10.2 125.3 %copy-start.45 = (f32[512]{0:T(512)}, f32[512]{0:T(512)S(1)}, u32[]{:S(2)}) copy-start(f32[512]{0:T(512)S(1)} %convert_element_type.134) | copy-start | bytes 6148
  10.9 126.5 %copy-start.42 = (f32[512]{0:T(512)}, f32[512]{0:T(512)S(1)}, u32[]{:S(2)}) copy-start(f32[512]{0:T(512)S(1)} %convert_element_type.138) | copy-start | bytes 6148
  11.6 124.0 %copy-start.52 = (f32[512]{0:T(512)}, f32[512]{0:T(512)S(1)}, u32[]{:S(2)}) copy-start(f32[512]{0:T(512)S(1)} %convert_element_type.135) | copy-start | bytes 6148
  12.3 125.2 %copy-start.50 = (f32[512]{0:T(512)}, f32[512]{0:T(512)S(1)}, u32[]{:S(2)}) copy-start(f32[512]{0:T(512)S(1)} %convert_element_type.139) | copy-start | bytes 6148
  28.6 45.4 %copy-start.47 = (s32[128,60]{0,1:T(8,128)S(1)}, s32[128,60]{0,1:T(8,128)}, u32[]{:S(2)}) copy-start(s32[128,60]{0,1:T(8,128)} %param.28) | copy-start | bytes 92164
  28.6 45.5 %copy-start.77 = (s32[128]{0:T(128)S(1)}, s32[128]{0:T(128)}, u32[]{:S(2)}) copy-start(s32[128]{0:T(128)} %param.31) | copy-start | bytes 1540
  28.6 45.5 %copy-start.78 = (s32[128]{0:T(128)S(1)}, s32[128]{0:T(128)}, u32[]{:S(2)}) copy-start(s32[128]{0:T(128)} %param.30) | copy-start | bytes 1540
  28.6 45.8 %copy-start.14 = (bf16[1,128,512]{2,1,0:T(8,128)(2,1)S(1)}, bf16[1,128,512]{2,1,0:T(8,128)(2,1)}, u32[]{:S(2)}) copy-start(bf16[1,128,512]{2,1,0:T(8,128)(2,1)} %param.23) | copy-start | bytes 393220
  74.4 55.7 %copy-start.48 = (f32[128,60]{0,1:T(8,128)}, f32[128,60]{0,1:T(8,128)S(1)}, u32[]{:S(2)}) copy-start(f32[128,60]{0,1:T(8,128)S(1)} %copy.62) | copy-start | bytes 92164
  74.4 60.2 %copy-start.73 = (f32[128]{0:T(128)}, f32[128]{0:T(128)S(1)}, u32[]{:S(2)}) copy-start(f32[128]{0:T(128)S(1)} %broadcast_maximum_fusion) | copy-start | bytes 1540
  137.2 99.0 %copy-start.7 = (f32[128,512]{1,0:T(8,128)}, f32[128,512]{1,0:T(8,128)S(1)}, u32[]{:S(2)}) copy-start(f32[128,512]{1,0:T(8,128)S(1)} %get-tuple-element.56) | copy-start | bytes 786436
  137.2 29.5 %copy-start.54 = (f32[128]{0:T(128)}, f32[128]{0:T(128)S(1)}, u32[]{:S(2)}) copy-start(f32[128]{0:T(128)S(1)} %broadcast_multiply_fusion.1) | copy-start | bytes 1540
  138.3 96.2 %reduce-scatter.7.cloned.1.call-start = ((), (), s32[]{:S(2)}) async-start(), calls=%async_computation.5 | async-start | bytes 589824
  138.3 50.0 %copy-start.59 = (f32[192]{0:T(256)}, f32[192]{0:T(256)S(1)}, u32[]{:S(2)}) copy-start(f32[192]{0:T(256)S(1)} %convert_element_type.148) | copy-start | bytes 2308
  138.4 65.4 %copy-start.71 = (s32[384]{0:T(512)}, s32[384]{0:T(512)S(1)}, u32[]{:S(2)}) copy-start(s32[384]{0:T(512)S(1)} %pad_add_fusion.1) | copy-start | bytes 4612
  207.6 125.2 %reduce-scatter.5.cloned.1.call-start = ((), (), s32[]{:S(2)}) async-start(), calls=%async_computation.3 | async-start | bytes 1179648 | tf_op jit(solution)/shard_map/reduce_scatter | solution.py:224
  302.0 298.1 %all-reduce.4.cloned.1.call-start = ((), (), s32[]{:S(2)}) async-start(), calls=%async_computation.6 | async-start | bytes 28704768 | tf_op jit(solution)/shard_map/psum | solution.py:238
  303.7 30.3 %copy-start.31 = (f32[192,512]{1,0:T(8,128)S(1)}, f32[192,512]{1,0:T(8,128)}, u32[]{:S(2)}) copy-start(f32[192,512]{1,0:T(8,128)} %fusion.68) | copy-start | bytes 1179652
  335.8 47.2 %copy-start.17 = (bf16[1216,512]{1,0:T(8,128)(2,1)S(1)}, bf16[1216,512]{1,0:T(8,128)(2,1)}, u32[]{:S(2)}) copy-start(bf16[1216,512]{1,0:T(8,128)(2,1)} %param.32) | copy-start | bytes 3735556
  335.8 47.2 %copy-start.21 = (f32[128,512]{1,0:T(8,128)S(1)}, f32[128,512]{1,0:T(8,128)}, u32[]{:S(2)}) copy-start(f32[128,512]{1,0:T(8,128)} %copy-done.20) | copy-start | bytes 786436
  335.8 47.2 %copy-start.76 = (f32[128]{0:T(128)S(1)}, f32[128]{0:T(128)}, u32[]{:S(2)}) copy-start(f32[128]{0:T(128)} %copy-done.75) | copy-start | bytes 1540
  (78 other events, 773.0 us)
Sparse Core Ops, SparseCore 0:
  9.6 24.5 all-gather.6
  138.4 20.2 all-gather.4
  207.7 26.6 reduce-scatter.6
  302.2 30.5 reduce-scatter.4
  341.3 258.7 all-reduce.3
where the time goes:
time: 629 us; the launch traced here: 620 us
  waiting for transfers between devices  258 us (41%)
  matrix products  202 us (32%)
  local copies, waits for them, and re-layouts  66.4 us (11%)
  blocking collectives  57.1 us (9%)
  other arithmetic  20.6 us (3%)
  between operations  15.6 us (2%)
    psum x1, waiting for transfers between devices, local(): lax.psum((grad_message_in, grad_message_mid, grad_message_out, grad_gain_...  203 us
    dot_general x6, matrix products, edge_input_grad(): jnp.einsum('rkf,ef->rke', grads, weight, preferred_element_type=jnp.float32)  57.3 us
    gather x2, local copies, waits for them, and re-layouts, local(): other_tag = jnp.take(table_tags, neighbour, axis=0)  45.3 us
    psum x1, blocking collectives, local(): lax.psum((grad_message_in, grad_message_mid, grad_message_out, grad_gain_...  43.9 us
    dot_general x6, matrix products, edge_weight_grad(): jnp.einsum('rke,rkf->ef', edges, grads, preferred_element_type=jnp.float32)  39.6 us
    dot_general x6, matrix products, edge_dot(): jnp.einsum('rke,ef->rkf', edges, weight, preferred_element_type=jnp.float32)  38.1 us
    dot_general x2, matrix products, pick_rows(): jnp.einsum('rkl,ld->rkd', picker, upper, preferred_element_type=jnp.float32)  20.2 us
    unnamed x6, waiting for transfers between devices  19.2 us
  transfers between devices with their start and end apart: 5, of which 4 were waited for; matrix products, arithmetic and copies ran while one was open for 17% of the time, Pallas kernels for 0%

commit v1 on v0

v1 whole, which is shorter than its diff:
```python
import functools
import jax
import jax.numpy as jnp
from jax import lax
from jax.experimental import pallas as pl
from jax.experimental.pallas import tpu as pltpu
from jax.sharding import PartitionSpec as P

EPSILON = 1e-05
CURVE = 0.7978845608028654
CUBIC = 0.044715
F32 = jnp.float32
BF16 = jnp.bfloat16
VMEM_LIMIT = 60 * 1024 * 1024
MESH = pl.DeviceIdType.MESH


def nn(a, b):
    return lax.dot_general(a, b, (((1,), (0,)), ((), ())), preferred_element_type=F32)


def nt(a, b):
    return lax.dot_general(a, b, (((1,), (1,)), ((), ())), preferred_element_type=F32)


def tn(a, b):
    return lax.dot_general(a, b, (((0,), (0,)), ((), ())), preferred_element_type=F32)


def gelu_parts(v):
    square = v * v
    t = jnp.tanh(v * (CURVE + (CURVE * CUBIC) * square))
    half = 0.5 + 0.5 * t
    slope = half + (half - half * half) * (v * (2.0 * CURVE + (6.0 * CURVE * CUBIC) * square))
    return v * half, slope


def tile_lanes(block, count):
    return jnp.concatenate([block] * count, axis=1) if count > 1 else block


def edge_operand(table_len, slabs, base, e_ref, nbr_ref):
    columns = []
    for j in range(slabs):
        row = nbr_ref[pl.ds(base + j, 1), :]
        ids = lax.broadcasted_iota(jnp.int32, (table_len, row.shape[1]), 0)
        hot = jnp.where(ids == row, 1.0, 0.0).astype(BF16)
        columns.append(jnp.concatenate([hot, e_ref[j]], axis=0))
    return jnp.concatenate(columns, axis=1) if slabs > 1 else columns[0]


def message_forward_body(table_len, feat, slabs, e_ref, nbr_ref, mask_ref, own_ref, lhs_ref, self_ref, mid_ref,
                         h1_ref, gp1_ref, gp2_ref, s_ref, keep_ref, cnt_ref):
    step = pl.program_id(0)
    base = step * slabs
    rows = nbr_ref.shape[1]

    @pl.when(step == 0)
    def _():
        s_ref[...] = jnp.zeros_like(s_ref)
        cnt_ref[...] = jnp.zeros_like(cnt_ref)

    own = own_ref[...]
    own_chain = own // 2
    own_flag = own % 2
    total = s_ref[...]
    count = cnt_ref[...]
    for j in range(slabs):
        row = nbr_ref[pl.ds(base + j, 1), :]
        ids = lax.broadcasted_iota(jnp.int32, (table_len, rows), 0)
        hot = jnp.where(ids == row, 1.0, 0.0).astype(BF16)
        x = jnp.concatenate([hot, e_ref[j]], axis=0)
        pre = nn(lhs_ref[...], x)
        other = pre[feat : feat + 1, :].astype(jnp.int32)
        joined = jnp.logical_or(own_chain == other // 2, own_flag * (other % 2) > 0)
        keep = jnp.where(joined, 1.0, 0.0) * mask_ref[pl.ds(base + j, 1), :].astype(F32)
        keep_ref[j] = keep
        count = count + keep
        hidden, slope = gelu_parts(pre[:feat] + self_ref[...])
        hidden = hidden.astype(BF16)
        h1_ref[j] = hidden
        gp1_ref[j] = slope.astype(BF16)
        hidden, slope = gelu_parts(nn(mid_ref[...], hidden))
        gp2_ref[j] = slope.astype(BF16)
        total = total + hidden * keep
    s_ref[...] = total
    cnt_ref[...] = count


def message_forward(e, nbr, mask, own_tag, lhs, self_t, mid_t, slabs):
    fan, edge_w, rows = e.shape
    feat = self_t.shape[0]
    table_len = lhs.shape[1] - edge_w
    whole = lambda a: pl.BlockSpec(a.shape, lambda i: (0,) * a.ndim)
    slab = lambda f: pl.BlockSpec((slabs, f, rows), lambda i: (i, 0, 0))
    big = jax.ShapeDtypeStruct((fan, feat, rows), BF16)
    return pl.pallas_call(
        functools.partial(message_forward_body, table_len, feat, slabs),
        grid=(fan // slabs,),
        in_specs=[slab(edge_w), whole(nbr), whole(mask), whole(own_tag), whole(lhs), whole(self_t), whole(mid_t)],
        out_specs=[slab(feat), slab(feat), slab(feat), pl.BlockSpec((feat, rows), lambda i: (0, 0)), slab(1),
                   pl.BlockSpec((1, rows), lambda i: (0, 0))],
        out_shape=[big, big, big, jax.ShapeDtypeStruct((feat, rows), F32), jax.ShapeDtypeStruct((fan, 1, rows), F32),
                   jax.ShapeDtypeStruct((1, rows), F32)],
        compiler_params=pltpu.CompilerParams(vmem_limit_bytes=VMEM_LIMIT),
        name="message_forward",
    )(e, nbr, mask, own_tag, lhs, self_t, mid_t)


def edge_body(table_len, slabs, e_ref, cot_ref, nbr_ref, lhs_ref, self_ref, mid_t_ref, out_t_ref, mid_ref, out_ref, edge_ref,
              gain_ref, offset_ref,
              new_ref, part_ref, gout_ref, gmid_ref, gin_ref, dself_ref, ggain_ref, goff_ref):
    step = pl.program_id(0)
    base = step * slabs
    rows = nbr_ref.shape[1]

    @pl.when(step == 0)
    def _():
        for ref in (gout_ref, gmid_ref, gin_ref, dself_ref, ggain_ref, goff_ref):
            ref[...] = jnp.zeros_like(ref)

    x = edge_operand(table_len, slabs, base, e_ref, nbr_ref)
    self_t = tile_lanes(self_ref[...], slabs)
    hidden_three, slope_three = gelu_parts(nn(lhs_ref[...], x) + self_t)
    hidden_three = hidden_three.astype(BF16)
    hidden_four, slope_four = gelu_parts(nn(mid_t_ref[...], hidden_three))
    hidden_four = hidden_four.astype(BF16)
    branch = nn(out_t_ref[...], hidden_four)
    gain = gain_ref[...]
    offset = offset_ref[...]
    scale = 1.0 / e_ref.shape[1]
    resid = []
    ggain = ggain_ref[...]
    goff = goff_ref[...]
    for j in range(slabs):
        z = e_ref[j].astype(F32) + branch[:, j * rows : (j + 1) * rows]
        z = z - jnp.sum(z, axis=0, keepdims=True) * scale
        r = lax.rsqrt(jnp.sum(z * z, axis=0, keepdims=True) * scale + EPSILON)
        h = z * r
        new_ref[j] = (h * gain + offset).astype(BF16)
        dy = cot_ref[j].astype(F32)
        ggain = ggain + dy * h
        goff = goff + dy
        dh = dy * gain
        one = jnp.sum(dh, axis=0, keepdims=True) * scale
        two = jnp.sum(dh * h, axis=0, keepdims=True) * scale
        resid.append(r * (dh - one - h * two))
    ggain_ref[...] = ggain
    goff_ref[...] = goff
    resid = jnp.concatenate(resid, axis=1) if slabs > 1 else resid[0]
    delta = resid.astype(BF16)
    gout_ref[...] += nt(hidden_four, delta)
    delta_four = (nn(out_ref[...], delta) * slope_four).astype(BF16)
    gmid_ref[...] += nt(hidden_three, delta_four)
    delta_three = nn(mid_ref[...], delta_four) * slope_three
    low = delta_three.astype(BF16)
    gin_ref[...] += nt(x, low)
    part = resid + nn(edge_ref[...], low)
    dself = dself_ref[...]
    for j in range(slabs):
        cut = slice(j * rows, (j + 1) * rows)
        part_ref[j] = part[:, cut]
        dself = dself + low[:, cut].astype(F32)
    dself_ref[...] = dself


def edge_pass(e, cot, nbr, lhs, self_t, mid_t, out_t, mid, out, edge, gain, offset, slabs):
    fan, edge_w, rows = e.shape
    table_len = lhs.shape[1] - edge_w
    whole = lambda a: pl.BlockSpec(a.shape, lambda i: (0,) * a.ndim)
    slab = pl.BlockSpec((slabs, edge_w, rows), lambda i: (i, 0, 0))
    keep = lambda *s: (pl.BlockSpec(s, lambda i: (0,) * len(s)), jax.ShapeDtypeStruct(s, F32))
    sums = [keep(edge_w, edge_w), keep(edge_w, edge_w), keep(table_len + edge_w, edge_w), keep(edge_w, rows), keep(edge_w, rows),
            keep(edge_w, rows)]
    consts = (nbr, lhs, self_t, mid_t, out_t, mid, out, edge, gain, offset)
    return pl.pallas_call(
        functools.partial(edge_body, table_len, slabs),
        grid=(fan // slabs,),
        in_specs=[slab, slab] + [whole(a) for a in consts],
        out_specs=[slab, slab] + [s for s, _ in sums],
        out_shape=[jax.ShapeDtypeStruct(e.shape, BF16), jax.ShapeDtypeStruct(e.shape, F32)] + [s for _, s in sums],
        compiler_params=pltpu.CompilerParams(vmem_limit_bytes=VMEM_LIMIT),
        name="edge_pass",
    )(e, cot, *consts)


def message_backward_body(table_len, slabs, e_ref, h1_ref, gp1_ref, gp2_ref, part_ref, keep_ref, nbr_ref, d2_ref, mid_ref, edge_ref,
                          egrad_ref, gmid_ref, gin_ref, dself_ref):
    step = pl.program_id(0)
    base = step * slabs
    rows = nbr_ref.shape[1]

    @pl.when(step == 0)
    def _():
        for ref in (gmid_ref, gin_ref, dself_ref):
            ref[...] = jnp.zeros_like(ref)

    x = edge_operand(table_len, slabs, base, e_ref, nbr_ref)
    back = d2_ref[...]
    wide = lambda ref: jnp.concatenate([ref[j] for j in range(slabs)], axis=1)
    two = jnp.concatenate([(back * keep_ref[j] * gp2_ref[j].astype(F32)).astype(BF16) for j in range(slabs)], axis=1)
    gmid_ref[...] += nt(wide(h1_ref), two)
    one = (nn(mid_ref[...], two) * wide(gp1_ref).astype(F32)).astype(BF16)
    gin_ref[...] += nt(x, one)
    part = nn(edge_ref[...], one)
    dself = dself_ref[...]
    for j in range(slabs):
        cut = slice(j * rows, (j + 1) * rows)
        egrad_ref[j] = part_ref[j] + part[:, cut]
        dself = dself + one[:, cut].astype(F32)
    dself_ref[...] = dself


def message_backward(e, h1, gp1, gp2, part, keep, nbr, d2, mid, edge, table_len, slabs):
    fan, edge_w, rows = e.shape
    feat = d2.shape[0]
    whole = lambda a: pl.BlockSpec(a.shape, lambda i: (0,) * a.ndim)
    slab = lambda f: pl.BlockSpec((slabs, f, rows), lambda i: (i, 0, 0))
    fixed = lambda *s: (pl.BlockSpec(s, lambda i: (0,) * len(s)), jax.ShapeDtypeStruct(s, F32))
    sums = [fixed(feat, feat), fixed(table_len + edge_w, feat), fixed(feat, rows)]
    consts = (nbr, d2, mid, edge)
    return pl.pallas_call(
        functools.partial(message_backward_body, table_len, slabs),
        grid=(fan // slabs,),
        in_specs=[slab(edge_w), slab(feat), slab(feat), slab(feat), slab(edge_w), slab(1)] + [whole(a) for a in consts],
        out_specs=[slab(edge_w)] + [s for s, _ in sums],
        out_shape=[jax.ShapeDtypeStruct(e.shape, F32)] + [s for _, s in sums],
        compiler_params=pltpu.CompilerParams(vmem_limit_bytes=VMEM_LIMIT),
        name="message_backward",
    )(e, h1, gp1, gp2, part, keep, *consts)


def ring_place(n):
    me = lax.axis_index("res")
    return me, [lax.rem(me + s, n) for s in range(n)]


def greet(peers):
    barrier = pltpu.get_barrier_semaphore()
    for peer in peers[1:]:
        pl.semaphore_signal(barrier, inc=1, device_id={"res": peer}, device_id_type=MESH)
    pl.semaphore_wait(barrier, len(peers) - 1)


def copy_to(peer, source, target, send, recv):
    return pltpu.make_async_remote_copy(
        src_ref=source, dst_ref=target, send_sem=send, recv_sem=recv, device_id={"res": peer}, device_id_type=MESH
    )


def swap(n, me, peers, source, target, send, recv):
    sent = [copy_to(peers[s], source.at[s], target.at[me], send.at[s], recv.at[me]) for s in range(1, n)]
    back = [copy_to(peers[s], source.at[s], target.at[peers[s]], send.at[s], recv.at[peers[s]]) for s in range(1, n)]
    return sent, back


def row_norm(values):
    values = values - jnp.mean(values, axis=1, keepdims=True)
    r = lax.rsqrt(jnp.mean(values * values, axis=1, keepdims=True) + EPSILON)
    return values * r, r


def row_norm_back(dh, h, r):
    return r * (dh - jnp.mean(dh, axis=1, keepdims=True) - h * jnp.mean(dh * h, axis=1, keepdims=True))


def table_rows_body(n, fetch_ref, x_ref, chain_ref, flag_ref, win_ref, mid_ref, umid_ref, uout_ref, uin_ref,
                    lhs_ref, self_ref, midt_ref, umidt_ref, uoutt_ref, uedge_ref, sel_ref, tag_ref,
                    idx_out, idx_in, row_out, far, send_a, recv_a, send_b, recv_b):
    me, peers = ring_place(n)
    rows, feat = x_ref.shape
    cap = fetch_ref.shape[1]
    edge_w = win_ref.shape[0] - 2 * feat
    idx_out[...] = jnp.full(idx_out.shape, -1, jnp.int32)
    for s in range(n):
        idx_out[s, 0:1, 0:cap] = fetch_ref[pl.ds(peers[s], 1), :]
    greet(peers)
    sent, back = swap(n, me, peers, idx_out, idx_in, send_a, recv_a)
    for copy in sent:
        copy.start()
    tag = chain_ref[...] * 2 + flag_ref[...]
    tag_ref[...] = tag
    x = x_ref[...]
    wide_tag = jnp.transpose(jnp.broadcast_to(tag.astype(F32), (rows, rows)))
    rich = jnp.concatenate([x, wide_tag.astype(BF16)], axis=1)
    self_ref[...] = jnp.transpose(nn(x, win_ref[:feat, :]))

    def choose(row):
        ids = lax.broadcasted_iota(jnp.int32, (rows, row.shape[1]), 0) + me * rows
        hot = jnp.transpose(jnp.where(ids == row, 1.0, 0.0))[:cap].astype(BF16)
        return hot, nn(hot, rich).astype(BF16)

    hot, block = choose(idx_out[0, 0:1, :])
    sel_ref[me] = hot
    far[me] = block
    copies, backs = swap(n, me, peers, row_out, far, send_b, recv_b)
    for s in range(1, n):
        back[s - 1].wait_recv()
        hot, block = choose(idx_in[peers[s], 0:1, :])
        sel_ref[peers[s]] = hot
        row_out[s] = block
        copies[s - 1].start()
    midt_ref[...] = jnp.transpose(mid_ref[...])
    umidt_ref[...] = jnp.transpose(umid_ref[...])
    uoutt_ref[...] = jnp.transpose(uout_ref[...])
    uedge_ref[...] = jnp.transpose(uin_ref[:, 2 * feat :])
    neigh = win_ref[feat : 2 * feat, :]
    extra = lhs_ref.shape[0] - feat
    table_len = rows + n * cap
    lhs_ref[feat:, table_len:] = jnp.zeros((extra, edge_w), BF16)
    lhs_ref[:feat, table_len:] = jnp.transpose(win_ref[2 * feat :, :])
    lhs_ref[:feat, :rows] = jnp.transpose(nn(x, neigh)).astype(BF16)
    lhs_ref[feat:, :rows] = jnp.broadcast_to(tag.astype(F32), (extra, rows)).astype(BF16)
    for copy in backs:
        copy.wait_recv()
    got = far[...].reshape(n * cap, far.shape[2])
    lhs_ref[:feat, rows:table_len] = jnp.transpose(nn(got[:, :feat], neigh)).astype(BF16)
    lhs_ref[feat:, rows:table_len] = jnp.transpose(got[:, feat:].astype(F32))[:extra].astype(BF16)
    for copy in sent + copies:
        copy.wait_send()


def vmem_call(body, args, outs, scratch, collective, name):
    whole = pl.BlockSpec(memory_space=pltpu.VMEM)
    return pl.pallas_call(
        body,
        out_shape=[jax.ShapeDtypeStruct(s, d) for s, d in outs],
        in_specs=[whole] * len(args),
        out_specs=[whole] * len(outs),
        scratch_shapes=scratch,
        compiler_params=pltpu.CompilerParams(vmem_limit_bytes=VMEM_LIMIT, collective_id=collective, has_side_effects=True),
        name=name,
    )(*args)


def table_rows(n, fetch, x, chain, flag, win, mid, umid, uout, uin):
    rows, feat = x.shape
    cap = fetch.shape[1]
    edge_w = win.shape[0] - 2 * feat
    table_len = rows + n * cap
    outs = [((feat + 16, table_len + edge_w), BF16), ((feat, rows), F32), (mid.shape, BF16), (umid.shape, BF16), (uout.shape, BF16),
            ((edge_w, edge_w), BF16), ((n, cap, rows), BF16), ((1, rows), jnp.int32)]
    sems = [pltpu.SemaphoreType.DMA((n,))] * 4
    scratch = [pltpu.VMEM((n, 8, 128), jnp.int32)] * 2 + [pltpu.VMEM((n, cap, feat + rows), BF16)] * 2 + sems
    return vmem_call(functools.partial(table_rows_body, n), (fetch, x, chain, flag, win, mid, umid, uout, uin), outs, scratch, 0,
                     "table_rows")


def node_forward_body(n, s_ref, cnt_ref, x_ref, mout_ref, gain_ref, off_ref, exp_ref, con_ref, gain2_ref, off2_ref, sel_ref, uin_ref,
                      node_ref, lhs_ref, self_ref, h1_ref, r1_ref, h2_ref, r2_ref, acted_ref, slope_ref,
                      row_out, far, send_a, recv_a):
    me, peers = ring_place(n)
    rows, feat = x_ref.shape
    cap = sel_ref.shape[1]
    edge_w = uin_ref.shape[0]
    mean = jnp.transpose(s_ref[...] / jnp.maximum(cnt_ref[...], 1.0))
    upper = mean.astype(BF16)
    lower = (mean - upper.astype(F32)).astype(BF16)
    aggregate = nn(upper, mout_ref[...]) + nn(lower, mout_ref[...])
    h, r = row_norm(x_ref[...].astype(F32) + aggregate)
    h1_ref[...] = h
    r1_ref[...] = r
    first = h * gain_ref[...].astype(F32) + off_ref[...].astype(F32)
    hidden, slope = gelu_parts(nn(first.astype(BF16), exp_ref[...]))
    acted = hidden.astype(BF16)
    acted_ref[...] = acted
    slope_ref[...] = slope
    h, r = row_norm(first + nn(acted, con_ref[...]))
    h2_ref[...] = h
    r2_ref[...] = r
    low = (h * gain2_ref[...].astype(F32) + off2_ref[...].astype(F32)).astype(BF16)
    node_ref[...] = low
    neigh = nt(low, uin_ref[:, feat : 2 * feat])
    packed = neigh.astype(BF16)
    greet(peers)
    copies, backs = swap(n, me, peers, row_out, far, send_a, recv_a)
    for s in range(1, n):
        row_out[s] = nn(sel_ref[peers[s]], packed).astype(BF16)
        copies[s - 1].start()
    far[me] = nn(sel_ref[me], packed).astype(BF16)
    self_ref[...] = nt(uin_ref[:, :feat], low)
    table_len = rows + n * cap
    lhs_ref[:, :rows] = jnp.transpose(neigh).astype(BF16)
    lhs_ref[:, table_len:] = uin_ref[:, 2 * feat :]
    for copy in backs:
        copy.wait_recv()
    lhs_ref[:, rows:table_len] = jnp.transpose(far[...].reshape(n * cap, edge_w))
    for copy in copies:
        copy.wait_send()


def node_forward(n, s, cnt, x, mout, gain, off, expand, contract, gain2, off2, sel, uin):
    rows, feat = x.shape
    cap = sel.shape[1]
    edge_w = uin.shape[0]
    table_len = rows + n * cap
    hidden = expand.shape[1]
    outs = [(x.shape, BF16), ((edge_w, table_len + edge_w), BF16), ((edge_w, rows), F32), (x.shape, F32), ((rows, 1), F32),
            (x.shape, F32), ((rows, 1), F32), ((rows, hidden), BF16), ((rows, hidden), F32)]
    scratch = [pltpu.VMEM((n, cap, edge_w), BF16)] * 2 + [pltpu.SemaphoreType.DMA((n,))] * 2
    return vmem_call(functools.partial(node_forward_body, n),
                     (s, cnt, x, mout, gain, off, expand, contract, gain2, off2, sel, uin), outs, scratch, 1, "node_forward")


def gather_back(n, me, peers, gin_ref, sel_ref, row_out, far, send, recv, rows):
    cap = sel_ref.shape[1]
    width = gin_ref.shape[1]
    greet(peers)
    copies, backs = swap(n, me, peers, row_out, far, send, recv)
    for s in range(1, n):
        start = pl.multiple_of(rows + peers[s] * cap, cap)
        row_out[s] = gin_ref[pl.ds(start, cap), :].astype(BF16)
        copies[s - 1].start()
    far[me] = gin_ref[pl.ds(pl.multiple_of(rows + me * cap, cap), cap), :].astype(BF16)
    for copy in backs:
        copy.wait_recv()
    picked = tn(sel_ref[...].reshape(n * cap, rows), far[...].reshape(n * cap, width))
    total = gin_ref[:rows, :] + picked
    for copy in copies:
        copy.wait_send()
    return total.astype(BF16)


def node_backward_body(n, gin_ref, dself_ref, sel_ref, node_ref, cot_ref, uin_ref, h1_ref, r1_ref, h2_ref, r2_ref, acted_ref, slope_ref,
                       gain_ref, off_ref, gain2_ref, exp_ref, con_ref, s_ref, cnt_ref, mout_ref, ggain_ref, goff_ref,
                       dfirst_ref, d2_ref, guin_ref, gmout_ref, gexp_ref, gcon_ref, gv_ref, ge_ref,
                       row_out, far, send_a, recv_a):
    me, peers = ring_place(n)
    rows, feat = node_ref.shape
    edge_w = uin_ref.shape[0]
    own = gather_back(n, me, peers, gin_ref, sel_ref, row_out, far, send_a, recv_a, rows)
    table_len = gin_ref.shape[0] - edge_w
    dself_t = dself_ref[...].astype(BF16)
    dself = jnp.transpose(dself_ref[...]).astype(BF16)
    node = node_ref[...]
    guin_ref[:, :feat] = nn(dself_t, node)
    guin_ref[:, feat : 2 * feat] = tn(own, node)
    guin_ref[:, 2 * feat :] = jnp.transpose(gin_ref[table_len:, :])
    dy = cot_ref[...].astype(F32) + nn(dself, uin_ref[:, :feat]) + nn(own, uin_ref[:, feat : 2 * feat])
    h2 = h2_ref[...]
    gv_ref[2:3, :] = jnp.sum(dy * h2, axis=0, keepdims=True)
    gv_ref[3:4, :] = jnp.sum(dy, axis=0, keepdims=True)
    second = row_norm_back(dy * gain2_ref[...].astype(F32), h2, r2_ref[...])
    dffn = second.astype(BF16)
    gcon_ref[...] = tn(acted_ref[...], dffn)
    dinner = (nt(dffn, con_ref[...]) * slope_ref[...]).astype(BF16)
    h1 = h1_ref[...]
    gain = gain_ref[...].astype(F32)
    first_low = (h1 * gain + off_ref[...].astype(F32)).astype(BF16)
    gexp_ref[...] = tn(first_low, dinner)
    dy = second + nt(dinner, exp_ref[...])
    gv_ref[0:1, :] = jnp.sum(dy * h1, axis=0, keepdims=True)
    gv_ref[1:2, :] = jnp.sum(dy, axis=0, keepdims=True)
    dfirst = row_norm_back(dy * gain, h1, r1_ref[...])
    dfirst_ref[...] = dfirst
    back = (jnp.transpose(dfirst) / jnp.maximum(cnt_ref[...], 1.0)).astype(BF16)
    d2_ref[...] = nn(mout_ref[...], back)
    gmout_ref[...] = nt(s_ref[...].astype(BF16), back)
    ge_ref[0:1, :] = jnp.sum(jnp.transpose(ggain_ref[...]), axis=0, keepdims=True)
    ge_ref[1:2, :] = jnp.sum(jnp.transpose(goff_ref[...]), axis=0, keepdims=True)


def node_backward(n, gin, dself, sel, node, cot, uin, h1, r1, h2, r2, acted, slope, gain, off, gain2, expand, contract, s, cnt, mout,
                  ggain, goff):
    rows, feat = node.shape
    cap = sel.shape[1]
    edge_w = uin.shape[0]
    outs = [(node.shape, F32), ((feat, rows), F32), (uin.shape, F32), (mout.shape, F32), (expand.shape, F32), (contract.shape, F32),
            ((4, feat), F32), ((2, edge_w), F32)]
    scratch = [pltpu.VMEM((n, cap, edge_w), BF16)] * 2 + [pltpu.SemaphoreType.DMA((n,))] * 2
    return vmem_call(functools.partial(node_backward_body, n),
                     (gin, dself, sel, node, cot, uin, h1, r1, h2, r2, acted, slope, gain, off, gain2, expand, contract, s, cnt, mout,
                      ggain, goff), outs, scratch, 2, "node_backward")


def node_finish_body(n, gin_ref, dself_ref, sel_ref, x_ref, dfirst_ref, win_ref, grad_ref, gwin_ref, row_out, far, send_a, recv_a):
    me, peers = ring_place(n)
    rows, feat = x_ref.shape
    own = gather_back(n, me, peers, gin_ref, sel_ref, row_out, far, send_a, recv_a, rows)
    table_len = gin_ref.shape[0] - (win_ref.shape[0] - 2 * feat)
    dself = jnp.transpose(dself_ref[...]).astype(BF16)
    x = x_ref[...]
    grad_ref[...] = dfirst_ref[...] + nt(dself, win_ref[:feat, :]) + nt(own, win_ref[feat : 2 * feat, :])
    gwin_ref[:feat, :] = tn(x, dself)
    gwin_ref[feat : 2 * feat, :] = tn(x, own)
    gwin_ref[2 * feat :, :] = gin_ref[table_len:, :]


def node_finish(n, gin, dself, sel, x, dfirst, win):
    cap = sel.shape[1]
    outs = [(x.shape, F32), (win.shape, F32)]
    scratch = [pltpu.VMEM((n, cap, x.shape[1]), BF16)] * 2 + [pltpu.SemaphoreType.DMA((n,))] * 2
    return vmem_call(functools.partial(node_finish_body, n), (gin, dself, sel, x, dfirst, win), outs, scratch, 3, "node_finish")


def local(n, node_feats, edge_feats, node_cotan, edge_cotan, neighbour, edge_mask, fetch_rows, chain_ids, complex_flag, message_in,
          message_mid, message_out, gain_node, offset_node, expand_weight, contract_weight, gain_ffn, offset_ffn, update_in, update_mid,
          update_out, gain_edge, offset_edge):
    x = node_feats[0]
    rows, feat = x.shape
    fan = neighbour.shape[1]
    edge_w = edge_feats.shape[3]
    e = jnp.transpose(edge_feats[0], (1, 2, 0))
    cot = jnp.transpose(edge_cotan[0], (1, 2, 0))
    nbr = jnp.transpose(neighbour)
    mask = jnp.transpose(edge_mask)
    uin = jnp.transpose(update_in)
    line = lambda v: v.reshape(1, -1)
    lhs, self_t, mid_t, umid_t, uout_t, uedge, sel, tag = table_rows(
        n, fetch_rows[0], x, line(chain_ids), line(complex_flag), message_in, message_mid, update_mid, update_out, uin
    )
    table_len = lhs.shape[1] - edge_w
    slabs = next(c for c in (10, 6, 4, 2, 1) if fan % c == 0)
    h1, gp1, gp2, s, keep, cnt = message_forward(e, nbr, mask, tag, lhs, self_t, mid_t, slabs)
    node, lhs3, self3, n1, r1, n2, r2, acted, slope = node_forward(
        n, s, cnt, x, message_out, line(gain_node), line(offset_node), expand_weight, contract_weight, line(gain_ffn), line(offset_ffn),
        sel, uin
    )
    column = lambda v: v.astype(F32).reshape(-1, 1)
    edge_new, part, guout, gumid, gin3, dself3, ggain, goff = edge_pass(
        e, cot, nbr, lhs3, self3, umid_t, uout_t, update_mid, update_out, uedge, column(gain_edge), column(offset_edge), slabs
    )
    dfirst, d2, guin, gmout, gexp, gcon, gv, ge = node_backward(
        n, gin3, dself3, sel, node, node_cotan[0], uin, n1, r1, n2, r2, acted, slope, line(gain_node), line(offset_node), line(gain_ffn),
        expand_weight, contract_weight, s, cnt, message_out, ggain, goff
    )
    egrad, gmid, gin1, dself1 = message_backward(
        e, h1, gp1, gp2, part, keep, nbr, d2, message_mid, message_in[2 * feat :], table_len, slabs
    )
    ngrad, gwin = node_finish(n, gin1, dself1, sel, x, dfirst, message_in)
    gwin, gmid, gmout, gv, gexp, gcon, guin, gumid, guout, ge = lax.psum(
        (gwin, gmid, gmout, gv, gexp, gcon, guin, gumid, guout, ge), ("tm", "res")
    )
    native = lambda a: jnp.transpose(a, (2, 0, 1))[None]
    return (node[None], native(edge_new), ngrad[None], native(egrad), gwin, gmid, gmout, gv[0], gv[1], gexp, gcon, gv[2], gv[3],
            jnp.transpose(guin), gumid, guout, ge[0], ge[1])


def solution(mesh):
    grouped, placed, copied = P("tm", "res", None), P("res", None), P()
    wide = P("tm", "res", None, None)
    arguments = (grouped, wide, grouped, wide, placed, placed, P("res", None, None), P("res"), P("res")) + (copied,) * 14
    return jax.shard_map(
        functools.partial(local, mesh.shape["res"]),
        mesh=mesh,
        in_specs=arguments,
        out_specs=(grouped, wide, grouped, wide) + (copied,) * 14,
        check_vma=False,
    )
```

time: 629 us -> 456 us (0.72); the launches traced: 620 us -> 454 us
  matrix products: 202 us -> 0 us
  Pallas kernels: 0 us -> 157 us
  waiting for transfers between devices: 258 us -> 214 us
  local copies, waits for them, and re-layouts: 66.4 us -> 24.9 us
  other arithmetic: 20.6 us -> 1.32 us
  blocking collectives: 57.1 us -> 41.9 us
    dot_general x46 -> x0, matrix products: 202 us -> none  [the longest x6 57.3 us: edge_input_grad(): jnp.einsum('rkf,ef->rke', grads, weight, preferred_element_type=jnp.float32)]
    pallas_call x0 -> x7, Pallas kernels: none -> 157 us  [the longest x4 62.2 us: vmem_call(): pl.pallas_call(body, out_shape=[jax.ShapeDtypeStruct(s, d) for s, d in ou...]
    gather x3 -> x0, local copies, waits for them, and re-layouts: 46.7 us -> none  [the longest x2 45.3 us: local(): other_tag = jnp.take(table_tags, neighbour, axis=0)]
    unnamed x6 -> x1, waiting for transfers between devices: 19.2 us -> 0.02 us
    all_gather x2 -> x0, waiting for transfers between devices: 19.1 us -> none  [the longest x1 19.1 us: local(): lax.all_gather(updated_low, 'res', axis=0, tiled=True)]
    reduce_scatter x1 -> x0, waiting for transfers between devices: 16.8 us -> none  [local(): lax.psum_scatter(spread_node.astype(jnp.bfloat16), 'res', scatter_dimensi...]
    all_gather x1 -> x0, blocking collectives: 13.2 us -> none  [local(): lax.all_gather(tag_local, 'res', axis=0, tiled=True)]
    reduce_sum x9 -> x0, other arithmetic: 12.7 us -> none  [the longest x3 11.6 us: layer_norm(): return centred * lax.rsqrt(spread + EPSILON) * gain_vec + offset]
  transfers between devices with their start and end apart: 5 -> 1, of which waited for: 4 -> 1; matrix products, arithmetic and copies ran while one was open for 17% -> 0% of each run, Pallas kernels for 0% -> 0%
where the time goes in v1:
time: 456 us; the launch traced here: 454 us
  waiting for transfers between devices  214 us (47%)
  Pallas kernels  157 us (34%)
  blocking collectives  41.9 us (9%)
  local copies, waits for them, and re-layouts  24.9 us (5%)
  between operations  14.2 us (3%)
    psum x1, waiting for transfers between devices, local(): lax.psum((gwin, gmid, gmout, gv, gexp, gcon, guin, gumid, guout, ge), ('t...  214 us
    pallas_call x4, Pallas kernels, vmem_call(): pl.pallas_call(body, out_shape=[jax.ShapeDtypeStruct(s, d) for s, d in ou...  62.2 us
    pallas_call x1, Pallas kernels, message_forward(): pl.pallas_call(functools.partial(message_forward_body, table_len, feat, s...  50.8 us
    psum x1, blocking collectives, local(): lax.psum((gwin, gmid, gmout, gv, gexp, gcon, guin, gumid, guout, ge), ('t...  41.9 us
    pallas_call x1, Pallas kernels, edge_pass(): pl.pallas_call(functools.partial(edge_body, table_len, slabs), grid=(fan...  22.8 us
    pallas_call x1, Pallas kernels, message_backward(): pl.pallas_call(functools.partial(message_backward_body, table_len, slabs)...  21.6 us
    unnamed x32, local copies, waits for them, and re-layouts  15.5 us
  transfers between devices with their start and end apart: 1, of which 1 were waited for; matrix products, arithmetic and copies ran while one was open for 0% of the time, Pallas kernels for 0%

profile of v1, /device:TPU:1, one launch (start us, length us, event | category | flops | bytes accessed | tf_op | source)
XLA Modules:
  0.0 454.1 jit_solution(13463277216152937091)
XLA Ops:
  8.6 1.3 reshape.69.gain_ref
  9.8 1.3 reshape.70.off_ref
  11.1 1.3 reshape.71.gain2_ref
  12.3 1.3 reshape.72.off2_ref
  13.6 0.8 copy.42.offset_ref
  14.4 0.8 copy.41.gain_ref
  15.1 1.6 slice.21.edge_ref
  16.7 19.7 %table_rows.1 = (bf16[528,576]{1,0:T(8,128)(2,1)}, f32[512,128]{1,0:T(8,128)}, bf16[512,512]{1,0:T(8,128)(2,1)}, bf16[192,192]{1,0:T(8,128)(2,1)}, bf16[192,192]...) custom-call(s32[8,32]{1,0:T(8,128)} %bitcast.49, ...), custom_call_target="tpu_custom_call" | custom-call | tf_op jit(solution)/shard_map/table_rows/pallas_call | solution.py:325
  36.5 50.8 %message_forward.1 = (bf16[60,512,128]{2,1,0:T(8,128)(2,1)}, bf16[60,512,128]{2,1,0:T(8,128)(2,1)}, bf16[60,512,128]{2,1,0:T(8,128)(2,1)}, f32[512,128]{1,0:T(8,...) custom-call(bf16[60,192,128]{2,1,0:T(8,128)(2,1)} %bitcast.31, s32[60,128]{1,0:T(8,128)} %bitcast.43, s32[60,128]{1,0:T(8,128)} %bitcast.48, ...), custom_call_target="tpu_custom_call" | custom-call | tf_op jit(solution)/shard_map/message_forward/pallas_call | solution.py:97
  87.3 13.2 %node_forward.1 = (bf16[128,512]{1,0:T(8,128)(2,1)}, bf16[192,576]{1,0:T(8,128)(2,1)}, f32[192,128]{1,0:T(8,128)}, f32[128,512]{1,0:T(8,128)}, f32[128,1]{1,0:T(...) custom-call(f32[512,128]{1,0:T(8,128)} %get-tuple-element.67.s_ref, ...), custom_call_target="tpu_custom_call" | custom-call | tf_op jit(solution)/shard_map/node_forward/pallas_call | solution.py:325
  100.4 22.8 %edge_pass.1 = (bf16[60,192,128]{2,1,0:T(8,128)(2,1)}, f32[60,192,128]{2,1,0:T(8,128)}, f32[192,192]{1,0:T(8,128)}, f32[192,192]{1,0:T(8,128)}, f32[576,192]{1,0...) custom-call(bf16[60,192,128]{2,1,0:T(8,128)(2,1)} %bitcast.32, ...), custom_call_target="tpu_custom_call" | custom-call | tf_op jit(solution)/shard_map/edge_pass/pallas_call | solution.py:176
  123.3 15.9 %node_backward.1 = (f32[128,512]{1,0:T(8,128)}, f32[512,128]{1,0:T(8,128)}, f32[192,1216]{1,0:T(8,128)}, f32[512,512]{1,0:T(8,128)}, f32[512,2048]{1,0:T(8,128)}...) custom-call(f32[576,192]{1,0:T(8,128)} %get-tuple-element.82.gin_ref, ...), custom_call_target="tpu_custom_call" | custom-call | tf_op jit(solution)/shard_map/node_backward/pallas_call | solution.py:325
  139.2 21.6 %message_backward.1 = (f32[60,192,128]{2,1,0:T(8,128)}, f32[512,512]{1,0:T(8,128)}, f32[576,512]{1,0:T(8,128)}, f32[512,128]{1,0:T(8,128)}) custom-call(bf16[60,192,128]{2,1,0:T(8,128)(2,1)} %bitcast.33, bf16[60,512,128]{2,1,0:T(8,128)(2,1)} %get-tuple-element.77.h1_ref, bf16[60,512,128]{2,1,0:T(8,128)(2,1)} %get-tuple-element.78.gp1_ref, ...), custom_call_target="tpu_custom_call" | custom-call | tf_op jit(solution)/shard_map/message_backward/pallas_call | solution.py:222
  160.8 13.4 %node_finish.1 = (f32[128,512]{1,0:T(8,128)}, f32[1216,512]{1,0:T(8,128)}) custom-call(f32[576,512]{1,0:T(8,128)} %get-tuple-element.93.gin_ref, f32[512,128]{1,0:T(8,128)} %get-tuple-element.94.dself_ref, bf16[8,32,128]{2,1,0:T(8,128)(2,1)} %get-tuple-element.69.sel_ref, bf16[128,512]{1,0:T(8,128)(2,1)} %bitcast.40, ...), custom_call_target="tpu_custom_call" | custom-call | tf_op jit(solution)/shard_map/node_finish/pallas_call | solution.py:325
  174.9 41.9 %all-reduce = (f32[4,512]{1,0:T(4,128)S(1)}, f32[2,192]{1,0:T(2,128)S(1)}) all-reduce(f32[4,512]{1,0:T(4,128)S(1)} %copy-done.9, f32[2,192]{1,0:T(2,128)S(1)} %copy-done.10), channel_id=1, replica_groups=mesh['tm'=4,'res'=8] {'tm','res'}, use_global_device_ids=true, to_apply=%region_3.0 | all-reduce | flops 2432 | bytes 19456 | tf_op jit(solution)/shard_map/psum | solution.py:531
  218.0 214.4 %all-reduce.4.cloned.1.call-done = (f32[1216,512]{1,0:T(8,128)}, f32[512,512]{1,0:T(8,128)}, f32[512,512]{1,0:T(8,128)}, f32[512,2048]{1,0:T(8,128)}, f32[2048,5...) async-done(((f32[1216,512]{1,0:T(8,128)}, f32[512,512]{1,0:T(8,128)}, f32[512,512]{1,0:T(8,128)}, f32[512,2048]{1,0:T(8,128)}, ...) | async-done | bytes 14204944 | tf_op jit(solution)/shard_map/psum | solution.py:531
  433.0 0.7 copy.59
  433.8 3.5 copy.60
  437.3 1.0 copy.61
  438.3 1.0 copy.62
  439.2 2.1 copy.63
  441.4 1.6 copy-done
  442.9 2.0 copy.64
  445.0 0.9 copy.65
  (30 shorter events, 5.2 us)
Async XLA Ops:
  7.2 425.2 %all-reduce.4.cloned.1.call-start = ((), (), s32[]{:S(2)}) async-start(), calls=%async_computation | async-start | bytes 28704768 | tf_op jit(solution)/shard_map/psum | solution.py:531
  174.2 0.7 copy-start.9
  174.3 0.7 copy-start.10
  174.3 258.1 %copy-start.5 = (bf16[128,512]{1,0:T(8,128)(2,1)S(1)}, bf16[128,512]{1,0:T(8,128)(2,1)}, u32[]{:S(2)}) copy-start(bf16[128,512]{1,0:T(8,128)(2,1)} %get-tuple-element.70.node_ref) | copy-start | bytes 393220
  174.3 258.8 %copy-start.6 = (f32[128,512]{1,0:T(8,128)S(1)}, f32[128,512]{1,0:T(8,128)}, u32[]{:S(2)}) copy-start(f32[128,512]{1,0:T(8,128)} %get-tuple-element.96) | copy-start | bytes 786436
  432.4 4.9 %copy-start.3 = (f32[512,512]{1,0:T(8,128)S(1)}, f32[512,512]{1,0:T(8,128)}, u32[]{:S(2)}) copy-start(f32[512,512]{1,0:T(8,128)} %get-tuple-element.147) | copy-start | bytes 3145732
  432.4 5.9 %copy-start.2 = (f32[512,512]{1,0:T(8,128)S(1)}, f32[512,512]{1,0:T(8,128)}, u32[]{:S(2)}) copy-start(f32[512,512]{1,0:T(8,128)} %get-tuple-element.148) | copy-start | bytes 3145732
  433.8 5.5 %copy-start.1 = (f32[512,2048]{1,0:T(8,128)S(1)}, f32[512,2048]{1,0:T(8,128)}, u32[]{:S(2)}) copy-start(f32[512,2048]{1,0:T(8,128)} %get-tuple-element.151) | copy-start | bytes 12582916
  439.2 3.7 copy-start
  442.9 2.0 copy-start.4
  442.9 3.0 copy-start.8
  442.9 3.6 copy-start.7
Sparse Core Ops, SparseCore 0:
  174.4 257.9 all-reduce.3

commit v2 on v1

--- a/solution.py
+++ b/solution.py
@@ -63,26 +63,29 @@
     own = own_ref[...]
     own_chain = own // 2
     own_flag = own % 2
+    pre = nn(lhs_ref[...], edge_operand(table_len, slabs, base, e_ref, nbr_ref))
+    hidden, slope = gelu_parts(pre[:feat] + tile_lanes(self_ref[...], slabs))
+    hidden = hidden.astype(BF16)
+    slope = slope.astype(BF16)
     total = s_ref[...]
     count = cnt_ref[...]
+    keeps = []
     for j in range(slabs):
-        row = nbr_ref[pl.ds(base + j, 1), :]
-        ids = lax.broadcasted_iota(jnp.int32, (table_len, rows), 0)
-        hot = jnp.where(ids == row, 1.0, 0.0).astype(BF16)
-        x = jnp.concatenate([hot, e_ref[j]], axis=0)
-        pre = nn(lhs_ref[...], x)
-        other = pre[feat : feat + 1, :].astype(jnp.int32)
+        cut = slice(j * rows, (j + 1) * rows)
+        h1_ref[j] = hidden[:, cut]
+        gp1_ref[j] = slope[:, cut]
+        other = pre[feat : feat + 1, cut].astype(jnp.int32)
         joined = jnp.logical_or(own_chain == other // 2, own_flag * (other % 2) > 0)
         keep = jnp.where(joined, 1.0, 0.0) * mask_ref[pl.ds(base + j, 1), :].astype(F32)
         keep_ref[j] = keep
+        keeps.append(keep)
         count = count + keep
-        hidden, slope = gelu_parts(pre[:feat] + self_ref[...])
-        hidden = hidden.astype(BF16)
-        h1_ref[j] = hidden
-        gp1_ref[j] = slope.astype(BF16)
-        hidden, slope = gelu_parts(nn(mid_ref[...], hidden))
-        gp2_ref[j] = slope.astype(BF16)
-        total = total + hidden * keep
+    hidden, slope = gelu_parts(nn(mid_ref[...], hidden))
+    slope = slope.astype(BF16)
+    for j in range(slabs):
+        cut = slice(j * rows, (j + 1) * rows)
+        gp2_ref[j] = slope[:, cut]
+        total = total + hidden[:, cut] * keeps[j]
     s_ref[...] = total
     cnt_ref[...] = count
 
@@ -184,50 +187,297 @@
     )(e, cot, *consts)
 
 
-def message_backward_body(table_len, slabs, e_ref, h1_ref, gp1_ref, gp2_ref, part_ref, keep_ref, nbr_ref, d2_ref, mid_ref, edge_ref,
-                          egrad_ref, gmid_ref, gin_ref, dself_ref):
-    step = pl.program_id(0)
-    base = step * slabs
-    rows = nbr_ref.shape[1]
-
-    @pl.when(step == 0)
-    def _():
-        for ref in (gmid_ref, gin_ref, dself_ref):
-            ref[...] = jnp.zeros_like(ref)
-
-    x = edge_operand(table_len, slabs, base, e_ref, nbr_ref)
-    back = d2_ref[...]
-    wide = lambda ref: jnp.concatenate([ref[j] for j in range(slabs)], axis=1)
-    two = jnp.concatenate([(back * keep_ref[j] * gp2_ref[j].astype(F32)).astype(BF16) for j in range(slabs)], axis=1)
-    gmid_ref[...] += nt(wide(h1_ref), two)
-    one = (nn(mid_ref[...], two) * wide(gp1_ref).astype(F32)).astype(BF16)
-    gin_ref[...] += nt(x, one)
-    part = nn(edge_ref[...], one)
-    dself = dself_ref[...]
-    for j in range(slabs):
-        cut = slice(j * rows, (j + 1) * rows)
-        egrad_ref[j] = part_ref[j] + part[:, cut]
-        dself = dself + one[:, cut].astype(F32)
-    dself_ref[...] = dself
-
-
-def message_backward(e, h1, gp1, gp2, part, keep, nbr, d2, mid, edge, table_len, slabs):
-    fan, edge_w, rows = e.shape
-    feat = d2.shape[0]
-    whole = lambda a: pl.BlockSpec(a.shape, lambda i: (0,) * a.ndim)
-    slab = lambda f: pl.BlockSpec((slabs, f, rows), lambda i: (i, 0, 0))
-    fixed = lambda *s: (pl.BlockSpec(s, lambda i: (0,) * len(s)), jax.ShapeDtypeStruct(s, F32))
-    sums = [fixed(feat, feat), fixed(table_len + edge_w, feat), fixed(feat, rows)]
-    consts = (nbr, d2, mid, edge)
-    return pl.pallas_call(
-        functools.partial(message_backward_body, table_len, slabs),
-        grid=(fan // slabs,),
-        in_specs=[slab(edge_w), slab(feat), slab(feat), slab(feat), slab(edge_w), slab(1)] + [whole(a) for a in consts],
-        out_specs=[slab(edge_w)] + [s for s, _ in sums],
-        out_shape=[jax.ShapeDtypeStruct(e.shape, F32)] + [s for _, s in sums],
-        compiler_params=pltpu.CompilerParams(vmem_limit_bytes=VMEM_LIMIT),
-        name="message_backward",
-    )(e, h1, gp1, gp2, part, keep, *consts)
+LANES = 512
+
+
+def spot():
+    group, place = lax.axis_index("tm"), lax.axis_index("res")
+    return group, place, lax.rem(place, 2), place // 2, lax.rem(group, 2), group // 2
+
+
+def grain(places):
+    return 16 * max(1, places // 4)
+
+
+def piece(places, depth, index):
+    across = min(places, 4)
+    rows, wide = piece_shape(places, depth)
+    top = pl.multiple_of((index // across) * rows, rows)
+    left = pl.multiple_of(lax.rem(index, across) * wide, wide)
+    return pl.ds(top, rows), pl.ds(left, wide)
+
+
+def piece_shape(places, depth):
+    across = min(places, 4)
+    return depth // (places // across), LANES // across
+
+
+def remote(source, target, send, recv, group, place):
+    return pltpu.make_async_remote_copy(
+        src_ref=source, dst_ref=target, send_sem=send, recv_sem=recv, device_id={"tm": group, "res": place}, device_id_type=MESH
+    )
+
+
+class Chunk:
+    def __init__(self, places, source, result, acc, from_core, from_first, from_second, from_line, stage, out, sends, recvs, local):
+        self.places, self.source, self.result, self.acc = places, source, result, acc
+        self.from_core, self.from_first, self.from_second = from_core, from_first, from_second
+        self.from_line, self.stage, self.out = from_line, stage, out
+        self.sends, self.recvs, self.local = sends, recvs, local
+        self.depth = acc.shape[1]
+        self.at = 0
+
+    def advance(self):
+        parts = (self.spread, self.halve, self.quarter, self.scatter, self.settle, self.gather, self.widen, self.share, self.store,
+                 self.close)
+        if self.at < len(parts):
+            parts[self.at]()
+            self.at += 1
+        return self.at < len(parts)
+
+    def link(self, slot, source, target, group, place):
+        return functools.partial(remote, source, target, self.sends.at[slot], self.recvs.at[slot], group, place)
+
+    def core_copy(self):
+        group, place, core, lane, x, y = spot()
+        theirs = pl.multiple_of((1 - core) * 8, 8)
+        return self.link(0, self.source.at[pl.ds(theirs, 8)], self.from_core, group, place + 1 - 2 * core)
+
+    def load_copy(self):
+        core = spot()[2]
+        return pltpu.make_async_copy(self.source.at[pl.ds(pl.multiple_of(core * 8, 8), 8)], self.acc, self.local.at[0])
+
+    def half_copies(self):
+        group, place, core, lane, x, y = spot()
+        return [
+            self.link(1, self.acc.at[pl.ds((1 - x) * 2, 2)], self.from_first.at[pl.ds(0, 2)], group + 1 - 2 * x, place),
+            self.link(2, self.acc.at[pl.ds(4 + (1 - y) * 2, 2)], self.from_first.at[pl.ds(2, 2)], group + 2 - 4 * y, place),
+        ]
+
+    def quarter_copies(self):
+        group, place, core, lane, x, y = spot()
+        return [
+            self.link(3, self.acc.at[x * 2 + 1 - y], self.from_second.at[0], group + 2 - 4 * y, place),
+            self.link(4, self.acc.at[4 + y * 2 + 1 - x], self.from_second.at[1], group + 1 - 2 * x, place),
+        ]
+
+    def line_copies(self):
+        group, place, core, lane, x, y = spot()
+        copies = []
+        for s in range(1, self.places):
+            ahead, behind = lax.rem(lane + s, self.places), lax.rem(lane + self.places - s, self.places)
+            rows, wide = piece(self.places, self.depth, ahead)
+            view = self.stage.at[:, rows, wide]
+            copies.append((self.link(4 + s, view, self.from_line.at[lane], group, ahead * 2 + core),
+                           self.link(4 + s, view, self.from_line.at[behind], group, behind * 2 + core)))
+        return copies
+
+    def own(self):
+        group, place, core, lane, x, y = spot()
+        return core * 8 + x * 2 + y, core * 8 + 4 + y * 2 + x
+
+    def spread_copies(self):
+        group, place, core, lane, x, y = spot()
+        copies = []
+        slot = 4 + self.places
+        for own in self.own():
+            for s in range(1, self.places):
+                ahead, behind = lax.rem(lane + s, self.places), lax.rem(lane + self.places - s, self.places)
+                rows, wide = piece(self.places, self.depth, lane)
+                back_rows, back_wide = piece(self.places, self.depth, behind)
+                view, back = self.out.at[own, rows, wide], self.out.at[own, back_rows, back_wide]
+                copies.append((self.link(slot, view, view, group, ahead * 2 + core), self.link(slot, back, back, group, behind * 2 + core)))
+                slot += 1
+        return copies
+
+    def both(self, slot, view, back, group, place):
+        return self.link(slot, view, view, group, place), self.link(slot, back, back, group, place)
+
+    def gather_copies(self):
+        group, place, core, lane, x, y = spot()
+        slot = 2 + 3 * self.places
+        first, second = self.own()
+        return [
+            self.both(slot, self.out.at[first], self.out.at[core * 8 + x * 2 + 1 - y], group + 2 - 4 * y, place),
+            self.both(slot + 1, self.out.at[second], self.out.at[core * 8 + 4 + y * 2 + 1 - x], group + 1 - 2 * x, place),
+        ]
+
+    def widen_copies(self):
+        group, place, core, lane, x, y = spot()
+        slot = 4 + 3 * self.places
+        two = lambda start: self.out.at[pl.ds(start, 2)]
+        return [
+            self.both(slot, two(core * 8 + x * 2), two(core * 8 + 2 - x * 2), group + 1 - 2 * x, place),
+            self.both(slot + 1, two(core * 8 + 4 + y * 2), two(core * 8 + 6 - y * 2), group + 2 - 4 * y, place),
+        ]
+
+    def share_copy(self):
+        group, place, core, lane, x, y = spot()
+        eight = lambda which: self.out.at[pl.ds(pl.multiple_of(which * 8, 8), 8)]
+        return self.both(6 + 3 * self.places, eight(core), eight(1 - core), group, place + 1 - 2 * core)
+
+    def store_copy(self, which, slot):
+        eight = pl.ds(pl.multiple_of(which * 8, 8), 8)
+        return pltpu.make_async_copy(self.out.at[eight], self.result.at[eight], self.local.at[slot])
+
+    def spread(self):
+        self.core_copy()().start()
+        self.load_copy().start()
+
+    def halve(self):
+        group, place, core, lane, x, y = spot()
+        self.load_copy().wait()
+        self.core_copy()().wait()
+        acc, extra = self.acc, self.from_core
+        give = [(1 - x) * 2, 4 + (1 - y) * 2]
+        keep = [x * 2, 4 + y * 2]
+        for start in give:
+            for i in range(2):
+                acc[start + i] = acc[start + i] + extra[start + i]
+        for copy in self.half_copies():
+            copy().start()
+        for start in keep:
+            for i in range(2):
+                acc[start + i] = acc[start + i] + extra[start + i]
+
+    def quarter(self):
+        group, place, core, lane, x, y = spot()
+        for copy in self.half_copies():
+            copy().wait()
+        acc, extra = self.acc, self.from_first
+        acc[x * 2 + 1 - y] = acc[x * 2 + 1 - y] + extra[1 - y]
+        acc[4 + y * 2 + 1 - x] = acc[4 + y * 2 + 1 - x] + extra[3 - x]
+        for copy in self.quarter_copies():
+            copy().start()
+        self.stage[0] = acc[x * 2 + y] + extra[y]
+        self.stage[1] = acc[4 + y * 2 + x] + extra[2 + x]
+
+    def scatter(self):
+        for copy in self.quarter_copies():
+            copy().wait()
+        for s in range(2):
+            self.stage[s] = self.stage[s] + self.from_second[s]
+        for send, arrive in self.line_copies():
+            send().start()
+
+    def settle(self):
+        group, place, core, lane, x, y = spot()
+        rows, wide = piece(self.places, self.depth, lane)
+        total = self.stage[:, rows, wide].astype(F32)
+        pairs = self.line_copies()
+        for s in range(1, self.places):
+            pairs[s - 1][1]().wait_recv()
+            total = total + self.from_line[lax.rem(lane + self.places - s, self.places)].astype(F32)
+        first, second = self.own()
+        total = total.astype(BF16)
+        self.out[first, rows, wide] = total[0]
+        self.out[second, rows, wide] = total[1]
+        for send, arrive in self.spread_copies():
+            send().start()
+        for send, arrive in pairs:
+            send().wait_send()
+
+    def finish(self, pairs):
+        for send, arrive in pairs:
+            arrive().wait_recv()
+        for send, arrive in pairs:
+            send().wait_send()
+
+    def gather(self):
+        self.finish(self.spread_copies())
+        for send, arrive in self.gather_copies():
+            send().start()
+
+    def widen(self):
+        self.finish(self.gather_copies())
+        for send, arrive in self.widen_copies():
+            send().start()
+
+    def share(self):
+        core = spot()[2]
+        self.finish(self.widen_copies())
+        self.share_copy()[0]().start()
+        self.store_copy(core, 1).start()
+
+    def store(self):
+        core = spot()[2]
+        self.share_copy()[1]().wait_recv()
+        self.store_copy(1 - core, 2).start()
+
+    def close(self):
+        core = spot()[2]
+        self.share_copy()[0]().wait_send()
+        self.store_copy(core, 1).wait()
+        self.store_copy(1 - core, 2).wait()
+
+
+CHUNK_REFS = 10
+
+
+def chunk_scratch(places, depth):
+    rows, wide = piece_shape(places, depth)
+    shapes = [(8, depth, LANES), (8, depth, LANES), (4, depth, LANES), (2, depth, LANES), (places, 2, rows, wide), (2, depth, LANES),
+              (16, depth, LANES)]
+    links = 7 + 3 * places
+    return [pltpu.VMEM(s, BF16) for s in shapes] + [pltpu.SemaphoreType.DMA((links,))] * 2 + [pltpu.SemaphoreType.DMA((3,))]
+
+
+def greet_all(n):
+    group, place, core, lane, x, y = spot()
+    barrier = pltpu.get_barrier_semaphore()
+    partners = [(group + 1 - 2 * x, place), (group + 2 - 4 * y, place)]
+    partners += [(group, lax.rem(place + s, n)) for s in range(1, n)]
+    for near, far in partners:
+        pl.semaphore_signal(barrier, inc=1, device_id={"tm": near, "res": far}, device_id_type=MESH)
+    pl.semaphore_wait(barrier, len(partners))
+
+
+def run_rounds(active, waiting=()):
+    waiting = list(waiting)
+    active = list(active)
+    while active or waiting:
+        if waiting:
+            active.append(waiting.pop(0))
+        active = [chunk for chunk in active if chunk.advance()]
+
+
+def chunk_plan(places, early_rows, late_first, late_second):
+    unit = grain(places)
+    depth = lambda rows: -(-rows // (16 * unit)) * unit
+    total = depth(early_rows)
+    third = total // 3 // unit * unit
+    return [third, third, total - 2 * third], [depth(late_first), depth(late_second)]
+
+
+def pack(bufs, row, value):
+    start = 0
+    value = value.astype(BF16)
+    for buf in bufs:
+        size = buf.shape[0] * buf.shape[1]
+        depth = buf.shape[1]
+        low, high = max(row, start), min(row + value.shape[0], start + size)
+        while low < high:
+            slot, inner = divmod(low - start, depth)
+            step = min(high - low, depth - inner)
+            buf[slot, inner : inner + step, : value.shape[1]] = value[low - row : low - row + step]
+            low += step
+        start += size
+
+
+def unpack(bufs, row, count, width):
+    pieces = []
+    start = 0
+    for buf in bufs:
+        depth = buf.shape[1]
+        size = buf.shape[0] * depth
+        low, high = max(row, start), min(row + count, start + size)
+        while low < high:
+            slot, inner = divmod(low - start, depth)
+            step = min(high - low, depth - inner)
+            pieces.append((buf[slot, inner : inner + step, : width], low - row))
+            low += step
+        start += size
+    return pieces
 
 
 def ring_place(n):
@@ -402,95 +652,277 @@
                      (s, cnt, x, mout, gain, off, expand, contract, gain2, off2, sel, uin), outs, scratch, 1, "node_forward")
 
 
-def gather_back(n, me, peers, gin_ref, sel_ref, row_out, far, send, recv, rows):
+def swap_back_start(n, me, peers, gin, sel_ref, row_out, far, send, recv, rows):
     cap = sel_ref.shape[1]
-    width = gin_ref.shape[1]
-    greet(peers)
     copies, backs = swap(n, me, peers, row_out, far, send, recv)
     for s in range(1, n):
         start = pl.multiple_of(rows + peers[s] * cap, cap)
-        row_out[s] = gin_ref[pl.ds(start, cap), :].astype(BF16)
+        row_out[s] = gin[pl.ds(start, cap), :].astype(BF16)
         copies[s - 1].start()
-    far[me] = gin_ref[pl.ds(pl.multiple_of(rows + me * cap, cap), cap), :].astype(BF16)
-    for copy in backs:
+    far[me] = gin[pl.ds(pl.multiple_of(rows + me * cap, cap), cap), :].astype(BF16)
+    return copies, backs
+
+
+def swap_back_finish(n, copies, gin, sel_ref, far, rows):
+    cap = sel_ref.shape[1]
+    width = gin.shape[1]
+    for copy in copies[1]:
         copy.wait_recv()
-    picked = tn(sel_ref[...].reshape(n * cap, rows), far[...].reshape(n * cap, width))
-    total = gin_ref[:rows, :] + picked
-    for copy in copies:
+    total = gin[:rows, :] + tn(sel_ref[...].reshape(n * cap, rows), far[...].reshape(n * cap, width))
+    for copy in copies[0]:
         copy.wait_send()
     return total.astype(BF16)
 
 
 def node_backward_body(n, gin_ref, dself_ref, sel_ref, node_ref, cot_ref, uin_ref, h1_ref, r1_ref, h2_ref, r2_ref, acted_ref, slope_ref,
                        gain_ref, off_ref, gain2_ref, exp_ref, con_ref, s_ref, cnt_ref, mout_ref, ggain_ref, goff_ref,
-                       dfirst_ref, d2_ref, guin_ref, gmout_ref, gexp_ref, gcon_ref, gv_ref, ge_ref,
-                       row_out, far, send_a, recv_a):
+                       gumid_ref, guout_ref, dfirst_ref, d2_ref, *rest):
+    chunks, (row_out, far, send_a, recv_a) = rest[:-4], rest[-4:]
     me, peers = ring_place(n)
     rows, feat = node_ref.shape
     edge_w = uin_ref.shape[0]
-    own = gather_back(n, me, peers, gin_ref, sel_ref, row_out, far, send_a, recv_a, rows)
+    greet(peers)
+    copies = swap_back_start(n, me, peers, gin_ref, sel_ref, row_out, far, send_a, recv_a, rows)
+    own = swap_back_finish(n, copies, gin_ref, sel_ref, far, rows)
     table_len = gin_ref.shape[0] - edge_w
     dself_t = dself_ref[...].astype(BF16)
     dself = jnp.transpose(dself_ref[...]).astype(BF16)
     node = node_ref[...]
-    guin_ref[:, :feat] = nn(dself_t, node)
-    guin_ref[:, feat : 2 * feat] = tn(own, node)
-    guin_ref[:, 2 * feat :] = jnp.transpose(gin_ref[table_len:, :])
+    at = early_rows(feat, acted_ref.shape[1], edge_w)
+    pack(chunks, at["update_self"], nn(dself_t, node))
+    pack(chunks, at["update_neigh"], tn(own, node))
+    gap = jnp.zeros((edge_w, 256 - edge_w), F32)
+    pack(chunks, at["update_edge"], jnp.concatenate([jnp.transpose(gin_ref[table_len:, :]), gap, gumid_ref[...], gap], axis=1))
+    pack(chunks, at["update_out"], jnp.concatenate([guout_ref[...], jnp.zeros((edge_w, feat - edge_w), F32)], axis=1))
     dy = cot_ref[...].astype(F32) + nn(dself, uin_ref[:, :feat]) + nn(own, uin_ref[:, feat : 2 * feat])
     h2 = h2_ref[...]
-    gv_ref[2:3, :] = jnp.sum(dy * h2, axis=0, keepdims=True)
-    gv_ref[3:4, :] = jnp.sum(dy, axis=0, keepdims=True)
+    ffn_sums = [jnp.sum(dy * h2, axis=0, keepdims=True), jnp.sum(dy, axis=0, keepdims=True)]
     second = row_norm_back(dy * gain2_ref[...].astype(F32), h2, r2_ref[...])
     dffn = second.astype(BF16)
-    gcon_ref[...] = tn(acted_ref[...], dffn)
+    for b in range(acted_ref.shape[1] // feat):
+        pack(chunks, at["contract"] + b * feat, tn(acted_ref[:, b * feat : (b + 1) * feat], dffn))
     dinner = (nt(dffn, con_ref[...]) * slope_ref[...]).astype(BF16)
     h1 = h1_ref[...]
     gain = gain_ref[...].astype(F32)
     first_low = (h1 * gain + off_ref[...].astype(F32)).astype(BF16)
-    gexp_ref[...] = tn(first_low, dinner)
+    for b in range(acted_ref.shape[1] // feat):
+        pack(chunks, at["expand"] + b * feat, tn(first_low, dinner[:, b * feat : (b + 1) * feat]))
     dy = second + nt(dinner, exp_ref[...])
-    gv_ref[0:1, :] = jnp.sum(dy * h1, axis=0, keepdims=True)
-    gv_ref[1:2, :] = jnp.sum(dy, axis=0, keepdims=True)
+    sums = [jnp.sum(dy * h1, axis=0, keepdims=True), jnp.sum(dy, axis=0, keepdims=True)] + ffn_sums
     dfirst = row_norm_back(dy * gain, h1, r1_ref[...])
     dfirst_ref[...] = dfirst
     back = (jnp.transpose(dfirst) / jnp.maximum(cnt_ref[...], 1.0)).astype(BF16)
     d2_ref[...] = nn(mout_ref[...], back)
-    gmout_ref[...] = nt(s_ref[...].astype(BF16), back)
-    ge_ref[0:1, :] = jnp.sum(jnp.transpose(ggain_ref[...]), axis=0, keepdims=True)
-    ge_ref[1:2, :] = jnp.sum(jnp.transpose(goff_ref[...]), axis=0, keepdims=True)
+    pack(chunks, at["message_out"], nt(s_ref[...].astype(BF16), back))
+    side = jnp.zeros((1, feat - edge_w), F32)
+    for ref in (ggain_ref, goff_ref):
+        sums.append(jnp.concatenate([jnp.sum(jnp.transpose(ref[...]), axis=0, keepdims=True), side], axis=1))
+    pack(chunks, at["vectors"], jnp.concatenate(sums + [jnp.zeros((10, feat), F32)], axis=0))
+    used = at["end"]
+    spare = sum(c.shape[0] * c.shape[1] for c in chunks) - used
+    if spare:
+        pack(chunks, used, jnp.zeros((spare, feat), F32))
+
+
+def early_rows(feat, hidden, edge_w):
+    at, row = {}, 0
+    for name, count in (("contract", hidden), ("expand", hidden), ("message_out", feat), ("update_self", edge_w),
+                        ("update_neigh", edge_w), ("update_edge", edge_w), ("update_out", edge_w), ("vectors", 16)):
+        at[name] = row
+        row += count
+    at["end"] = row
+    return at
 
 
 def node_backward(n, gin, dself, sel, node, cot, uin, h1, r1, h2, r2, acted, slope, gain, off, gain2, expand, contract, s, cnt, mout,
-                  ggain, goff):
+                  ggain, goff, gumid, guout, depths):
     rows, feat = node.shape
     cap = sel.shape[1]
     edge_w = uin.shape[0]
-    outs = [(node.shape, F32), ((feat, rows), F32), (uin.shape, F32), (mout.shape, F32), (expand.shape, F32), (contract.shape, F32),
-            ((4, feat), F32), ((2, edge_w), F32)]
+    outs = [(node.shape, F32), ((feat, rows), F32)] + [((16, d, LANES), BF16) for d in depths]
     scratch = [pltpu.VMEM((n, cap, edge_w), BF16)] * 2 + [pltpu.SemaphoreType.DMA((n,))] * 2
     return vmem_call(functools.partial(node_backward_body, n),
                      (gin, dself, sel, node, cot, uin, h1, r1, h2, r2, acted, slope, gain, off, gain2, expand, contract, s, cnt, mout,
-                      ggain, goff), outs, scratch, 2, "node_backward")
-
-
-def node_finish_body(n, gin_ref, dself_ref, sel_ref, x_ref, dfirst_ref, win_ref, grad_ref, gwin_ref, row_out, far, send_a, recv_a):
-    me, peers = ring_place(n)
-    rows, feat = x_ref.shape
-    own = gather_back(n, me, peers, gin_ref, sel_ref, row_out, far, send_a, recv_a, rows)
-    table_len = gin_ref.shape[0] - (win_ref.shape[0] - 2 * feat)
-    dself = jnp.transpose(dself_ref[...]).astype(BF16)
-    x = x_ref[...]
-    grad_ref[...] = dfirst_ref[...] + nt(dself, win_ref[:feat, :]) + nt(own, win_ref[feat : 2 * feat, :])
-    gwin_ref[:feat, :] = tn(x, dself)
-    gwin_ref[feat : 2 * feat, :] = tn(x, own)
-    gwin_ref[2 * feat :, :] = gin_ref[table_len:, :]
-
-
-def node_finish(n, gin, dself, sel, x, dfirst, win):
+                      ggain, goff, gumid, guout), outs, scratch, 2, "node_backward")
+
+
+EARLY_STEPS = {0: (0, 1, 2), 1: (0, 1), 3: (0, 2), 4: (1,), 5: (0,)}
+
+
+def message_backward_body(n, table_len, slabs, early, late, *refs):
+    (e_ref, h1_ref, gp1_ref, gp2_ref, part_ref, keep_ref, nbr_ref, d2_ref, mid_ref, win_ref, x_ref, dfirst_ref, sel_ref) = refs[:13]
+    refs = refs[13:]
+    sources, refs = refs[:early], refs[early:]
+    egrad_ref, grad_ref, results, refs = refs[0], refs[1], refs[2 : 2 + early + late], refs[2 + early + late :]
+    (gmid, gin, dself_sum, row_out, far, send_a, recv_a), refs = refs[:7], refs[7:]
+    late_sources, refs = refs[:late], refs[late:]
+    places = n // 2
+    chunks = [Chunk(places, (list(sources) + list(late_sources))[i], results[i], *refs[CHUNK_REFS * i : CHUNK_REFS * (i + 1)])
+              for i in range(early + late)]
+    step = pl.program_id(0)
+    base = step * slabs
+    steps = pl.num_programs(0)
+    rows = nbr_ref.shape[1]
+    feat = d2_ref.shape[0]
+
+    @pl.when(step == 0)
+    def _():
+        greet_all(n)
+        for ref in (gmid, gin, dself_sum):
+            ref[...] = jnp.zeros_like(ref)
+
+    for at, which in EARLY_STEPS.items():
+
+        @pl.when(step == at)
+        def _(which=which):
+            for i in which:
+                chunks[i].advance()
+
+    x = edge_operand(table_len, slabs, base, e_ref, nbr_ref)
+    back = d2_ref[...]
+    wide = lambda ref: jnp.concatenate([ref[j] for j in range(slabs)], axis=1)
+    two = jnp.concatenate([(back * keep_ref[j] * gp2_ref[j].astype(F32)).astype(BF16) for j in range(slabs)], axis=1)
+    gmid[...] += nt(wide(h1_ref), two)
+    one = (nn(mid_ref[...], two) * wide(gp1_ref).astype(F32)).astype(BF16)
+    gin[...] += nt(x, one)
+    part = nn(win_ref[2 * feat :, :], one)
+    total = dself_sum[...]
+    for j in range(slabs):
+        cut = slice(j * rows, (j + 1) * rows)
+        egrad_ref[j] = part_ref[j] + part[:, cut]
+        total = total + one[:, cut].astype(F32)
+    dself_sum[...] = total
+
+    @pl.when(step == steps - 1)
+    def _():
+        me, peers = ring_place(n)
+        copies = swap_back_start(n, me, peers, gin, sel_ref, row_out, far, send_a, recv_a, rows)
+        first, second = late_sources
+        pack([first], 0, gmid[...])
+        pack([first], feat, gin[table_len:, :])
+        end = feat + gin.shape[0] - table_len
+        spare = first.shape[0] * first.shape[1] - end
+        if spare:
+            pack([first], end, jnp.zeros((spare, feat), F32))
+        chunks[early].advance()
+        dself = jnp.transpose(dself_sum[...]).astype(BF16)
+        nodes = x_ref[...]
+        pack([second], 0, tn(nodes, dself))
+        own = swap_back_finish(n, copies, gin, sel_ref, far, rows)
+        pack([second], feat, tn(nodes, own))
+        spare = second.shape[0] * second.shape[1] - 2 * feat
+        if spare:
+            pack([second], 2 * feat, jnp.zeros((spare, feat), F32))
+        chunks[early + 1].advance()
+        grad_ref[...] = dfirst_ref[...] + nt(dself, win_ref[:feat, :]) + nt(own, win_ref[feat : 2 * feat, :])
+        run_rounds(chunks)
+
+
+def message_backward(n, e, h1, gp1, gp2, part, keep, nbr, d2, mid, win, x, dfirst, sel, sources, late_depths, table_len, slabs):
+    fan, edge_w, rows = e.shape
+    feat = d2.shape[0]
     cap = sel.shape[1]
-    outs = [(x.shape, F32), (win.shape, F32)]
-    scratch = [pltpu.VMEM((n, cap, x.shape[1]), BF16)] * 2 + [pltpu.SemaphoreType.DMA((n,))] * 2
-    return vmem_call(functools.partial(node_finish_body, n), (gin, dself, sel, x, dfirst, win), outs, scratch, 3, "node_finish")
+    places = n // 2
+    whole = lambda a: pl.BlockSpec(a.shape, lambda i: (0,) * a.ndim)
+    slab = lambda f: pl.BlockSpec((slabs, f, rows), lambda i: (i, 0, 0))
+    anywhere = pl.BlockSpec(memory_space=pl.ANY)
+    consts = (nbr, d2, mid, win, x, dfirst, sel)
+    depths = [s.shape[1] for s in sources] + list(late_depths)
+    scratch = [pltpu.VMEM((feat, feat), F32), pltpu.VMEM((table_len + edge_w, feat), F32), pltpu.VMEM((feat, rows), F32)]
+    scratch += [pltpu.VMEM((n, cap, feat), BF16)] * 2 + [pltpu.SemaphoreType.DMA((n,))] * 2
+    scratch += [pltpu.VMEM((16, d, LANES), BF16) for d in late_depths]
+    for d in depths:
+        scratch += chunk_scratch(places, d)
+    return pl.pallas_call(
+        functools.partial(message_backward_body, n, table_len, slabs, len(sources), len(late_depths)),
+        grid=(fan // slabs,),
+        in_specs=[slab(edge_w), slab(feat), slab(feat), slab(feat), slab(edge_w), slab(1)] + [whole(a) for a in consts]
+        + [anywhere] * len(sources),
+        out_specs=[slab(edge_w), whole(x)] + [anywhere] * len(depths),
+        out_shape=[jax.ShapeDtypeStruct(e.shape, F32), jax.ShapeDtypeStruct(x.shape, F32)]
+        + [jax.ShapeDtypeStruct((16, d, LANES), BF16) for d in depths],
+        scratch_shapes=scratch,
+        compiler_params=pltpu.CompilerParams(vmem_limit_bytes=VMEM_LIMIT, collective_id=3, has_side_effects=True),
+        name="message_backward",
+    )(e, h1, gp1, gp2, part, keep, *consts, *sources)
+
+
+def unpack_body(early, late, feat, hidden, edge_w, *refs):
+    count = early + late
+    sources, refs = refs[:count], refs[count:]
+    (gwin, gmid, gmout, gexp, gcon, guin, gumid, guout, gv, ge), refs = refs[:10], refs[10:]
+    held, refs = refs[:count], refs[count:]
+    (swin, smid, smout, sexp, scon, suin), load, send = refs[:6], refs[6], refs[7]
+    loads = [pltpu.make_async_copy(sources[i], held[i], load.at[i]) for i in range(count)]
+    for copy in loads:
+        copy.start()
+    at = early_rows(feat, hidden, edge_w)
+    sent = []
+
+    def push(source, target):
+        copy = pltpu.make_async_copy(source, target, send.at[len(sent)])
+        copy.start()
+        sent.append(copy)
+
+    ready = [0]
+
+    def section(bufs, row, size, width, target, top=0, left=0, lane=0):
+        for value, offset in unpack(bufs, row, size, LANES):
+            target[top + offset : top + offset + value.shape[0], left : left + width] = value[:, lane : lane + width].astype(F32)
+
+    def need(rows, first):
+        start = 0
+        for i in range(first, count):
+            if start < rows and i >= ready[0]:
+                loads[i].wait()
+                ready[0] = i + 1
+            start += held[i].shape[0] * held[i].shape[1]
+
+    front, back = held[:early], held[early:]
+    for b in range(hidden // feat):
+        need(at["contract"] + (b + 1) * feat, 0)
+        section(front, at["contract"] + b * feat, feat, feat, scon, top=b * feat)
+        push(scon.at[pl.ds(b * feat, feat)], gcon.at[pl.ds(b * feat, feat)])
+    for b in range(hidden // feat):
+        need(at["expand"] + (b + 1) * feat, 0)
+        section(front, at["expand"] + b * feat, feat, feat, sexp, left=b * feat)
+        push(sexp.at[:, pl.ds(b * feat, feat)], gexp.at[:, pl.ds(b * feat, feat)])
+    for copy in loads[ready[0]:]:
+        copy.wait()
+    section(front, at["message_out"], feat, feat, smout)
+    push(smout, gmout)
+    section(front, at["update_self"], edge_w, feat, suin)
+    section(front, at["update_neigh"], edge_w, feat, suin, left=feat)
+    section(front, at["update_edge"], edge_w, edge_w, suin, left=2 * feat)
+    push(suin, guin)
+    section(front, at["update_edge"], edge_w, edge_w, gumid, lane=256)
+    section(front, at["update_out"], edge_w, edge_w, guout)
+    vectors = unpack(front, at["vectors"], 16, LANES)[0][0].astype(F32)
+    gv[...] = vectors[:4]
+    ge[...] = vectors[4:6, :edge_w]
+    section(back[:1], 0, feat, feat, smid)
+    push(smid, gmid)
+    section(back[:1], feat, edge_w, feat, swin, top=2 * feat)
+    section(back[1:], 0, 2 * feat, feat, swin)
+    push(swin, gwin)
+    for copy in sent:
+        copy.wait()
+
+
+def unpack_all(chunks, early, feat, hidden, edge_w):
+    whole, anywhere = pl.BlockSpec(memory_space=pltpu.VMEM), pl.BlockSpec(memory_space=pl.ANY)
+    big = [(2 * feat + edge_w, feat), (feat, feat), (feat, feat), (feat, hidden), (hidden, feat), (edge_w, 2 * feat + edge_w)]
+    small = [(edge_w, edge_w), (edge_w, edge_w), (4, feat), (2, edge_w)]
+    return pl.pallas_call(
+        functools.partial(unpack_body, early, len(chunks) - early, feat, hidden, edge_w),
+        in_specs=[anywhere] * len(chunks),
+        out_specs=[anywhere] * 6 + [whole] * 4,
+        out_shape=[jax.ShapeDtypeStruct(s, F32) for s in big + small],
+        scratch_shapes=[pltpu.VMEM(c.shape, BF16) for c in chunks] + [pltpu.VMEM(s, F32) for s in big]
+        + [pltpu.SemaphoreType.DMA((len(chunks),)), pltpu.SemaphoreType.DMA((16,))],
+        compiler_params=pltpu.CompilerParams(vmem_limit_bytes=VMEM_LIMIT),
+        name="unpack_all",
+    )(*chunks)
 
 
 def local(n, node_feats, edge_feats, node_cotan, edge_cotan, neighbour, edge_mask, fetch_rows, chain_ids, complex_flag, message_in,
@@ -520,17 +952,16 @@
     edge_new, part, guout, gumid, gin3, dself3, ggain, goff = edge_pass(
         e, cot, nbr, lhs3, self3, umid_t, uout_t, update_mid, update_out, uedge, column(gain_edge), column(offset_edge), slabs
     )
-    dfirst, d2, guin, gmout, gexp, gcon, gv, ge = node_backward(
+    hidden = expand_weight.shape[1]
+    early_depths, late_depths = chunk_plan(n // 2, early_rows(feat, hidden, edge_w)["end"], feat + edge_w, 2 * feat)
+    dfirst, d2, *sources = node_backward(
         n, gin3, dself3, sel, node, node_cotan[0], uin, n1, r1, n2, r2, acted, slope, line(gain_node), line(offset_node), line(gain_ffn),
-        expand_weight, contract_weight, s, cnt, message_out, ggain, goff
+        expand_weight, contract_weight, s, cnt, message_out, ggain, goff, gumid, guout, early_depths
     )
-    egrad, gmid, gin1, dself1 = message_backward(
-        e, h1, gp1, gp2, part, keep, nbr, d2, message_mid, message_in[2 * feat :], table_len, slabs
+    egrad, ngrad, *sums = message_backward(
+        n, e, h1, gp1, gp2, part, keep, nbr, d2, message_mid, message_in, x, dfirst, sel, sources, late_depths, table_len, slabs
     )
-    ngrad, gwin = node_finish(n, gin1, dself1, sel, x, dfirst, message_in)
-    gwin, gmid, gmout, gv, gexp, gcon, guin, gumid, guout, ge = lax.psum(
-        (gwin, gmid, gmout, gv, gexp, gcon, guin, gumid, guout, ge), ("tm", "res")
-    )
+    gwin, gmid, gmout, gexp, gcon, guin, gumid, guout, gv, ge = unpack_all(sums, len(sources), feat, hidden, edge_w)
     native = lambda a: jnp.transpose(a, (2, 0, 1))[None]
     return (node[None], native(edge_new), ngrad[None], native(egrad), gwin, gmid, gmout, gv[0], gv[1], gexp, gcon, gv[2], gv[3],
             jnp.transpose(guin), gumid, guout, ge[0], ge[1])

time: 456 us -> 219 us (0.48)
  waiting for transfers between devices: 214 us -> 0 us
  Pallas kernels: 157 us -> 200 us
  blocking collectives: 41.9 us -> 0 us
  between operations: 14.2 us -> 0.73 us
  local copies, waits for them, and re-layouts: 24.9 us -> 16.6 us
    psum x1 -> x0, waiting for transfers between devices: 214 us -> none  [local(): lax.psum((gwin, gmid, gmout, gv, gexp, gcon, guin, gumid, guout, ge), ('t...]
    pallas_call x1 -> x2, Pallas kernels: 21.6 us -> 105 us  [the longest x1 97.2 us: message_backward(): pl.pallas_call(functools.partial(message_backward_body, n, table_len, sla...]
    psum x1 -> x0, blocking collectives: 41.9 us -> none  [local(): lax.psum((gwin, gmid, gmout, gv, gexp, gcon, guin, gumid, guout, ge), ('t...]
    pallas_call x1, Pallas kernels: 50.8 us -> 24 us  [message_forward(): pl.pallas_call(functools.partial(message_forward_body, table_len, feat, s...]
    pallas_call x4 -> x3, Pallas kernels: 62.2 us -> 47.8 us  [vmem_call(): pl.pallas_call(body, out_shape=[jax.ShapeDtypeStruct(s, d) for s, d in ou...]
    unnamed x32 -> x7, local copies, waits for them, and re-layouts: 15.5 us -> 7.29 us
  transfers between devices with their start and end apart: 1 -> 0, of which waited for: 1 -> 0; matrix products, arithmetic and copies ran while one was open for 0% -> 0% of each run, Pallas kernels for 0% -> 0%
where the time goes in v2:
time: 219 us
  Pallas kernels  200 us (91%)
  local copies, waits for them, and re-layouts  16.6 us (8%)
    pallas_call x1, Pallas kernels, message_backward(): pl.pallas_call(functools.partial(message_backward_body, n, table_len, sla...  97.2 us
    pallas_call x3, Pallas kernels, vmem_call(): pl.pallas_call(body, out_shape=[jax.ShapeDtypeStruct(s, d) for s, d in ou...  47.8 us
    pallas_call x1, Pallas kernels, message_forward(): pl.pallas_call(functools.partial(message_forward_body, table_len, feat, s...  24 us
    pallas_call x1, Pallas kernels, edge_pass(): pl.pallas_call(functools.partial(edge_body, table_len, slabs), grid=(fan...  22.8 us
    pallas_call x1, Pallas kernels, unpack_all(): pl.pallas_call(functools.partial(unpack_body, early, len(chunks) - early,...  8.22 us
    unnamed x7, local copies, waits for them, and re-layouts  7.29 us
    reshape x4, local copies, waits for them, and re-layouts, local(): line = lambda v: v.reshape(1, -1)  5.03 us

profile of v2, /device:TPU:1, one launch (start us, length us, event | category | flops | bytes accessed | tf_op | source)
XLA Modules:
  0.0 218.8 jit_solution(8435291749817387795)
XLA Ops:
  0.7 0.7 reshape.77
  1.3 0.7 reshape.79
  2.0 1.3 reshape.69.gain_ref
  3.2 1.3 reshape.70.off_ref
  4.5 1.3 reshape.71.gain2_ref
  5.7 1.3 reshape.72.off2_ref
  7.0 0.8 copy.42.offset_ref
  7.8 0.8 copy.41.gain_ref
  8.5 19.7 %table_rows.1 = (bf16[528,576]{1,0:T(8,128)(2,1)}, f32[512,128]{1,0:T(8,128)}, bf16[512,512]{1,0:T(8,128)(2,1)}, bf16[192,192]{1,0:T(8,128)(2,1)}, bf16[192,192]...) custom-call(s32[8,32]{1,0:T(8,128)} %bitcast.49, ...), custom_call_target="tpu_custom_call" | custom-call | tf_op jit(solution)/shard_map/table_rows/pallas_call | solution.py:575
  28.3 24.0 %message_forward.1 = (bf16[60,512,128]{2,1,0:T(8,128)(2,1)}, bf16[60,512,128]{2,1,0:T(8,128)(2,1)}, bf16[60,512,128]{2,1,0:T(8,128)(2,1)}, f32[512,128]{1,0:T(8,...) custom-call(bf16[60,192,128]{2,1,0:T(8,128)(2,1)} %bitcast.31, s32[60,128]{1,0:T(8,128)} %bitcast.43, s32[60,128]{1,0:T(8,128)} %bitcast.48, ...), custom_call_target="tpu_custom_call" | custom-call | tf_op jit(solution)/shard_map/message_forward/pallas_call | solution.py:100
  52.3 13.0 %node_forward.1 = (bf16[128,512]{1,0:T(8,128)(2,1)}, bf16[192,576]{1,0:T(8,128)(2,1)}, f32[192,128]{1,0:T(8,128)}, f32[128,512]{1,0:T(8,128)}, f32[128,1]{1,0:T(...) custom-call(f32[512,128]{1,0:T(8,128)} %get-tuple-element.75.s_ref, ...), custom_call_target="tpu_custom_call" | custom-call | tf_op jit(solution)/shard_map/node_forward/pallas_call | solution.py:575
  65.3 22.8 %edge_pass.1 = (bf16[60,192,128]{2,1,0:T(8,128)(2,1)}, f32[60,192,128]{2,1,0:T(8,128)}, f32[192,192]{1,0:T(8,128)}, f32[192,192]{1,0:T(8,128)}, f32[576,192]{1,0...) custom-call(bf16[60,192,128]{2,1,0:T(8,128)(2,1)} %bitcast.32, ...), custom_call_target="tpu_custom_call" | custom-call | tf_op jit(solution)/shard_map/edge_pass/pallas_call | solution.py:179
  88.1 15.1 %node_backward.1 = (f32[128,512]{1,0:T(8,128)}, f32[512,128]{1,0:T(8,128)}, bf16[16,112,512]{2,1,0:T(8,128)(2,1)}, bf16[16,112,512]{2,1,0:T(8,128)(2,1)}, bf16[16,128,512]{2,1,0:T(8,128)(2,1)}) custom-call(f32[576,192]{1,0:T(8,128)} %get-tuple-element.90.gin_ref, f32[192,128]{1,0:T(8,128)} %get-tuple-element.91.dself_ref, ...), custom_call_target="tpu_custom_call" | custom-call | tf_op jit(solution)/shard_map/node_backward/pallas_call | solution.py:575
  103.3 97.2 %message_backward.1 = (f32[60,192,128]{2,1,0:T(8,128)}, f32[128,512]{1,0:T(8,128)}, bf16[16,112,512]{2,1,0:T(8,128)(2,1)}, bf16[16,112,512]{2,1,0:T(8,128)(2,1)}...) custom-call(bf16[60,192,128]{2,1,0:T(8,128)(2,1)} %bitcast.33, ...), custom_call_target="tpu_custom_call" | custom-call | tf_op jit(solution)/shard_map/message_backward/pallas_call | solution.py:836
  200.5 0.0 copy-start
  200.5 0.0 copy-start.1
  200.5 8.2 %unpack_all.1 = (f32[1216,512]{1,0:T(8,128)}, f32[512,512]{1,0:T(8,128)}, f32[512,512]{1,0:T(8,128)}, f32[512,2048]{1,0:T(8,128)}, f32[2048,512]{1,0:T(8,128)}, ...) custom-call(bf16[16,112,512]{2,1,0:T(8,128)(2,1)} %get-tuple-element., ...), custom_call_target="tpu_custom_call" | custom-call | tf_op jit(solution)/shard_map/unpack_all/pallas_call | solution.py:916
  208.7 1.3 fusion.1
  210.0 1.4 fusion
  211.5 0.0 copy-done
  211.5 0.7 copy.46
  212.1 0.0 copy-done.1
  212.1 0.7 copy.47
  212.8 5.9 %copy.48 = f32[1,128,60,192]{1,3,2,0:T(8,128)} copy(f32[1,128,60,192]{1,3,2,0:T(8,128)} %bitcast.34) | data formatting | bytes 11796480
Async XLA Ops:
  200.5 11.0 %copy-start = (bf16[128,512]{1,0:T(8,128)(2,1)S(1)}, bf16[128,512]{1,0:T(8,128)(2,1)}, u32[]{:S(2)}) copy-start(bf16[128,512]{1,0:T(8,128)(2,1)} %get-tuple-element.78.node_ref) | copy-start | bytes 393220
  200.5 11.7 %copy-start.1 = (f32[128,512]{1,0:T(8,128)S(1)}, f32[128,512]{1,0:T(8,128)}, u32[]{:S(2)}) copy-start(f32[128,512]{1,0:T(8,128)} %get-tuple-element.107) | copy-start | bytes 786436

commit v3 on v2

--- a/solution.py
+++ b/solution.py
@@ -96,16 +96,17 @@
     table_len = lhs.shape[1] - edge_w
     whole = lambda a: pl.BlockSpec(a.shape, lambda i: (0,) * a.ndim)
     slab = lambda f: pl.BlockSpec((slabs, f, rows), lambda i: (i, 0, 0))
-    big = jax.ShapeDtypeStruct((fan, feat, rows), BF16)
+    big = pltpu.HBM((fan, feat, rows), BF16)
+    e, nbr, mask = far_off(e, nbr, mask)
     return pl.pallas_call(
         functools.partial(message_forward_body, table_len, feat, slabs),
         grid=(fan // slabs,),
         in_specs=[slab(edge_w), whole(nbr), whole(mask), whole(own_tag), whole(lhs), whole(self_t), whole(mid_t)],
         out_specs=[slab(feat), slab(feat), slab(feat), pl.BlockSpec((feat, rows), lambda i: (0, 0)), slab(1),
                    pl.BlockSpec((1, rows), lambda i: (0, 0))],
-        out_shape=[big, big, big, jax.ShapeDtypeStruct((feat, rows), F32), jax.ShapeDtypeStruct((fan, 1, rows), F32),
+        out_shape=[big, big, big, jax.ShapeDtypeStruct((feat, rows), F32), pltpu.HBM((fan, 1, rows), F32),
                    jax.ShapeDtypeStruct((1, rows), F32)],
-        compiler_params=pltpu.CompilerParams(vmem_limit_bytes=VMEM_LIMIT),
+        compiler_params=pltpu.CompilerParams(vmem_limit_bytes=30 * 1024 * 1024),
         name="message_forward",
     )(e, nbr, mask, own_tag, lhs, self_t, mid_t)
 
@@ -175,14 +176,15 @@
     keep = lambda *s: (pl.BlockSpec(s, lambda i: (0,) * len(s)), jax.ShapeDtypeStruct(s, F32))
     sums = [keep(edge_w, edge_w), keep(edge_w, edge_w), keep(table_len + edge_w, edge_w), keep(edge_w, rows), keep(edge_w, rows),
             keep(edge_w, rows)]
+    e, cot, nbr, mid, out = far_off(e, cot, nbr, mid, out)
     consts = (nbr, lhs, self_t, mid_t, out_t, mid, out, edge, gain, offset)
     return pl.pallas_call(
         functools.partial(edge_body, table_len, slabs),
         grid=(fan // slabs,),
         in_specs=[slab, slab] + [whole(a) for a in consts],
         out_specs=[slab, slab] + [s for s, _ in sums],
-        out_shape=[jax.ShapeDtypeStruct(e.shape, BF16), jax.ShapeDtypeStruct(e.shape, F32)] + [s for _, s in sums],
-        compiler_params=pltpu.CompilerParams(vmem_limit_bytes=VMEM_LIMIT),
+        out_shape=[pltpu.HBM(e.shape, BF16), pltpu.HBM(e.shape, F32)] + [s for _, s in sums],
+        compiler_params=pltpu.CompilerParams(vmem_limit_bytes=30 * 1024 * 1024),
         name="edge_pass",
     )(e, cot, *consts)
 
@@ -225,15 +227,10 @@
         self.from_line, self.stage, self.out = from_line, stage, out
         self.sends, self.recvs, self.local = sends, recvs, local
         self.depth = acc.shape[1]
-        self.at = 0
-
-    def advance(self):
-        parts = (self.spread, self.halve, self.quarter, self.scatter, self.settle, self.gather, self.widen, self.share, self.store,
-                 self.close)
-        if self.at < len(parts):
-            parts[self.at]()
-            self.at += 1
-        return self.at < len(parts)
+
+    def run(self, stage):
+        (self.spread, self.halve, self.quarter, self.scatter, self.settle, self.gather, self.widen, self.share, self.store,
+         self.close)[stage]()
 
     def link(self, slot, source, target, group, place):
         return functools.partial(remote, source, target, self.sends.at[slot], self.recvs.at[slot], group, place)
@@ -429,24 +426,16 @@
     partners += [(group, lax.rem(place + s, n)) for s in range(1, n)]
     for near, far in partners:
         pl.semaphore_signal(barrier, inc=1, device_id={"tm": near, "res": far}, device_id_type=MESH)
-    pl.semaphore_wait(barrier, len(partners))
-
-
-def run_rounds(active, waiting=()):
-    waiting = list(waiting)
-    active = list(active)
-    while active or waiting:
-        if waiting:
-            active.append(waiting.pop(0))
-        active = [chunk for chunk in active if chunk.advance()]
-
-
-def chunk_plan(places, early_rows, late_first, late_second):
+
+
+def chunk_plan(places, early_rows, late_rows):
     unit = grain(places)
     depth = lambda rows: -(-rows // (16 * unit)) * unit
     total = depth(early_rows)
-    third = total // 3 // unit * unit
-    return [third, third, total - 2 * third], [depth(late_first), depth(late_second)]
+    size = min(-(-total // (4 * unit)) * unit, (total - unit) // (3 * unit) * unit)
+    late = depth(late_rows)
+    half = late // 2 // unit * unit
+    return [size, size, size, total - 3 * size], [half, late - half]
 
 
 def pack(bufs, row, value):
@@ -462,6 +451,15 @@
             buf[slot, inner : inner + step, : value.shape[1]] = value[low - row : low - row + step]
             low += step
         start += size
+
+
+def fill(bufs, row, values):
+    for value in values:
+        pack(bufs, row, value)
+        row += value.shape[0]
+    spare = sum(b.shape[0] * b.shape[1] for b in bufs) - row
+    if spare:
+        pack(bufs, row, jnp.zeros((spare, bufs[0].shape[2]), F32))
 
 
 def unpack(bufs, row, count, width):
@@ -485,11 +483,14 @@
     return me, [lax.rem(me + s, n) for s in range(n)]
 
 
-def greet(peers):
+def greet_start(peers):
     barrier = pltpu.get_barrier_semaphore()
     for peer in peers[1:]:
         pl.semaphore_signal(barrier, inc=1, device_id={"res": peer}, device_id_type=MESH)
-    pl.semaphore_wait(barrier, len(peers) - 1)
+
+
+def greet_end(peers):
+    pl.semaphore_wait(pltpu.get_barrier_semaphore(), len(peers) - 1)
 
 
 def copy_to(peer, source, target, send, recv):
@@ -498,9 +499,10 @@
     )
 
 
-def swap(n, me, peers, source, target, send, recv):
-    sent = [copy_to(peers[s], source.at[s], target.at[me], send.at[s], recv.at[me]) for s in range(1, n)]
-    back = [copy_to(peers[s], source.at[s], target.at[peers[s]], send.at[s], recv.at[peers[s]]) for s in range(1, n)]
+def swap(n, me, peers, source, target, send, recv, placed=False):
+    view = lambda s: source.at[peers[s] if placed else s]
+    sent = [copy_to(peers[s], view(s), target.at[me], send.at[s], recv.at[me]) for s in range(1, n)]
+    back = [copy_to(peers[s], view(s), target.at[peers[s]], send.at[s], recv.at[peers[s]]) for s in range(1, n)]
     return sent, back
 
 
@@ -514,46 +516,48 @@
     return r * (dh - jnp.mean(dh, axis=1, keepdims=True) - h * jnp.mean(dh * h, axis=1, keepdims=True))
 
 
-def table_rows_body(n, fetch_ref, x_ref, chain_ref, flag_ref, win_ref, mid_ref, umid_ref, uout_ref, uin_ref,
-                    lhs_ref, self_ref, midt_ref, umidt_ref, uoutt_ref, uedge_ref, sel_ref, tag_ref,
-                    idx_out, idx_in, row_out, far, send_a, recv_a, send_b, recv_b):
+def table_rows_body(n, fetch_ref, x_ref, chain_ref, flag_ref, win_ref, mid_ref, umid_ref, uout_ref, uin_ref, gain_ref, off_ref,
+                    lhs_ref, self_ref, midt_ref, umidt_ref, uoutt_ref, uedge_ref, sel_ref, tag_ref, gaint_ref, offt_ref, far_ref,
+                    idx_out, idx_in, row_out, far, wants, asked, send_a, recv_a, send_b, recv_b):
     me, peers = ring_place(n)
+    greet_start(peers)
     rows, feat = x_ref.shape
     cap = fetch_ref.shape[1]
     edge_w = win_ref.shape[0] - 2 * feat
-    idx_out[...] = jnp.full(idx_out.shape, -1, jnp.int32)
+    tag = chain_ref[...].reshape(1, rows) * 2 + flag_ref[...].reshape(1, rows)
+    tag_ref[...] = tag
     for s in range(n):
+        idx_out[s] = jnp.full((8, 128), -1, jnp.int32)
         idx_out[s, 0:1, 0:cap] = fetch_ref[pl.ds(peers[s], 1), :]
-    greet(peers)
+        idx_out[s, 1:2, 0:rows] = tag
+    greet_end(peers)
     sent, back = swap(n, me, peers, idx_out, idx_in, send_a, recv_a)
     for copy in sent:
         copy.start()
-    tag = chain_ref[...] * 2 + flag_ref[...]
-    tag_ref[...] = tag
+    idx_in[me] = idx_out[0]
     x = x_ref[...]
-    wide_tag = jnp.transpose(jnp.broadcast_to(tag.astype(F32), (rows, rows)))
-    rich = jnp.concatenate([x, wide_tag.astype(BF16)], axis=1)
+    for p in range(n):
+        wants[0:1, p * cap : (p + 1) * cap] = fetch_ref[p : p + 1, :]
     self_ref[...] = jnp.transpose(nn(x, win_ref[:feat, :]))
 
-    def choose(row):
-        ids = lax.broadcasted_iota(jnp.int32, (rows, row.shape[1]), 0) + me * rows
-        hot = jnp.transpose(jnp.where(ids == row, 1.0, 0.0))[:cap].astype(BF16)
-        return hot, nn(hot, rich).astype(BF16)
-
-    hot, block = choose(idx_out[0, 0:1, :])
-    sel_ref[me] = hot
-    far[me] = block
-    copies, backs = swap(n, me, peers, row_out, far, send_b, recv_b)
-    for s in range(1, n):
-        back[s - 1].wait_recv()
-        hot, block = choose(idx_in[peers[s], 0:1, :])
-        sel_ref[peers[s]] = hot
-        row_out[s] = block
-        copies[s - 1].start()
+    copies, backs = swap(n, me, peers, row_out, far, send_b, recv_b, True)
+    for copy in back:
+        copy.wait_recv()
+    for p in range(n):
+        asked[0:1, p * cap : (p + 1) * cap] = idx_in[p, 0:1, 0:cap]
+    spots = lax.broadcasted_iota(jnp.int32, (rows, n * cap), 0)
+    hot = jnp.where(spots + me * rows == asked[...], 1.0, 0.0).astype(BF16)
+    row_out[...] = tn(hot, x).astype(BF16).reshape(n, cap, feat)
+    for copy in copies:
+        copy.start()
+    sel_ref[...] = hot
+    far[me] = row_out[me]
     midt_ref[...] = jnp.transpose(mid_ref[...])
     umidt_ref[...] = jnp.transpose(umid_ref[...])
     uoutt_ref[...] = jnp.transpose(uout_ref[...])
     uedge_ref[...] = jnp.transpose(uin_ref[:, 2 * feat :])
+    for source, target in ((gain_ref, gaint_ref), (off_ref, offt_ref)):
+        target[...] = jnp.transpose(jnp.broadcast_to(source[...].astype(F32).reshape(1, edge_w), (rows, edge_w)))
     neigh = win_ref[feat : 2 * feat, :]
     extra = lhs_ref.shape[0] - feat
     table_len = rows + n * cap
@@ -561,48 +565,61 @@
     lhs_ref[:feat, table_len:] = jnp.transpose(win_ref[2 * feat :, :])
     lhs_ref[:feat, :rows] = jnp.transpose(nn(x, neigh)).astype(BF16)
     lhs_ref[feat:, :rows] = jnp.broadcast_to(tag.astype(F32), (extra, rows)).astype(BF16)
+    tags = jnp.concatenate([idx_in[p, 1:2, 0:rows] for p in range(n)] + [jnp.zeros((-n % 16, rows), jnp.int32)] * (n % 16 > 0), axis=0)
+    want = wants[...]
+    picked = nn(tags.astype(F32).astype(BF16), jnp.where(spots == lax.rem(want, rows), 1.0, 0.0).astype(BF16))
+    owner = lax.broadcasted_iota(jnp.int32, picked.shape, 0) == want // rows
+    far_tag = jnp.sum(jnp.where(owner, picked, 0.0), axis=0, keepdims=True)
+    lhs_ref[feat:, rows:table_len] = jnp.broadcast_to(far_tag, (extra, n * cap)).astype(BF16)
     for copy in backs:
         copy.wait_recv()
-    got = far[...].reshape(n * cap, far.shape[2])
-    lhs_ref[:feat, rows:table_len] = jnp.transpose(nn(got[:, :feat], neigh)).astype(BF16)
-    lhs_ref[feat:, rows:table_len] = jnp.transpose(got[:, feat:].astype(F32))[:extra].astype(BF16)
+    got = far[...].reshape(n * cap, feat)
+    lhs_ref[:feat, rows:table_len] = jnp.transpose(nn(got, neigh)).astype(BF16)
+    far_ref[...] = got
     for copy in sent + copies:
         copy.wait_send()
 
 
-def vmem_call(body, args, outs, scratch, collective, name):
+def far_off(*arrays):
+    return [pltpu.with_memory_space_constraint(a, pltpu.HBM) for a in arrays]
+
+
+def vmem_call(body, args, outs, scratch, collective, name, outside=()):
     whole = pl.BlockSpec(memory_space=pltpu.VMEM)
     return pl.pallas_call(
         body,
-        out_shape=[jax.ShapeDtypeStruct(s, d) for s, d in outs],
+        out_shape=[pltpu.HBM(s, d) if i in outside else jax.ShapeDtypeStruct(s, d) for i, (s, d) in enumerate(outs)],
         in_specs=[whole] * len(args),
         out_specs=[whole] * len(outs),
         scratch_shapes=scratch,
-        compiler_params=pltpu.CompilerParams(vmem_limit_bytes=VMEM_LIMIT, collective_id=collective, has_side_effects=True),
+        compiler_params=pltpu.CompilerParams(vmem_limit_bytes=30 * 1024 * 1024, collective_id=collective, has_side_effects=True),
         name=name,
     )(*args)
 
 
-def table_rows(n, fetch, x, chain, flag, win, mid, umid, uout, uin):
+def table_rows(n, fetch, x, chain, flag, win, mid, umid, uout, uin, gain, off):
     rows, feat = x.shape
     cap = fetch.shape[1]
     edge_w = win.shape[0] - 2 * feat
     table_len = rows + n * cap
     outs = [((feat + 16, table_len + edge_w), BF16), ((feat, rows), F32), (mid.shape, BF16), (umid.shape, BF16), (uout.shape, BF16),
-            ((edge_w, edge_w), BF16), ((n, cap, rows), BF16), ((1, rows), jnp.int32)]
+            ((edge_w, edge_w), BF16), ((rows, n * cap), BF16), ((1, rows), jnp.int32), ((edge_w, rows), F32), ((edge_w, rows), F32),
+            ((n * cap, feat), BF16)]
     sems = [pltpu.SemaphoreType.DMA((n,))] * 4
-    scratch = [pltpu.VMEM((n, 8, 128), jnp.int32)] * 2 + [pltpu.VMEM((n, cap, feat + rows), BF16)] * 2 + sems
-    return vmem_call(functools.partial(table_rows_body, n), (fetch, x, chain, flag, win, mid, umid, uout, uin), outs, scratch, 0,
-                     "table_rows")
+    scratch = [pltpu.VMEM((n, 8, 128), jnp.int32)] * 2 + [pltpu.VMEM((n, cap, feat), BF16)] * 2 + [pltpu.VMEM((1, n * cap), jnp.int32)] * 2
+    return vmem_call(functools.partial(table_rows_body, n), far_off(fetch, x, chain, flag, win, mid, umid, uout, uin, gain, off), outs,
+                     scratch + sems, 0, "table_rows", (10,))
 
 
 def node_forward_body(n, s_ref, cnt_ref, x_ref, mout_ref, gain_ref, off_ref, exp_ref, con_ref, gain2_ref, off2_ref, sel_ref, uin_ref,
                       node_ref, lhs_ref, self_ref, h1_ref, r1_ref, h2_ref, r2_ref, acted_ref, slope_ref,
                       row_out, far, send_a, recv_a):
     me, peers = ring_place(n)
+    greet_start(peers)
     rows, feat = x_ref.shape
-    cap = sel_ref.shape[1]
+    cap = sel_ref.shape[1] // n
     edge_w = uin_ref.shape[0]
+    line = lambda ref: ref[...].astype(F32).reshape(1, feat)
     mean = jnp.transpose(s_ref[...] / jnp.maximum(cnt_ref[...], 1.0))
     upper = mean.astype(BF16)
     lower = (mean - upper.astype(F32)).astype(BF16)
@@ -610,7 +627,7 @@
     h, r = row_norm(x_ref[...].astype(F32) + aggregate)
     h1_ref[...] = h
     r1_ref[...] = r
-    first = h * gain_ref[...].astype(F32) + off_ref[...].astype(F32)
+    first = h * line(gain_ref) + line(off_ref)
     hidden, slope = gelu_parts(nn(first.astype(BF16), exp_ref[...]))
     acted = hidden.astype(BF16)
     acted_ref[...] = acted
@@ -618,16 +635,16 @@
     h, r = row_norm(first + nn(acted, con_ref[...]))
     h2_ref[...] = h
     r2_ref[...] = r
-    low = (h * gain2_ref[...].astype(F32) + off2_ref[...].astype(F32)).astype(BF16)
+    low = (h * line(gain2_ref) + line(off2_ref)).astype(BF16)
     node_ref[...] = low
     neigh = nt(low, uin_ref[:, feat : 2 * feat])
     packed = neigh.astype(BF16)
-    greet(peers)
-    copies, backs = swap(n, me, peers, row_out, far, send_a, recv_a)
-    for s in range(1, n):
-        row_out[s] = nn(sel_ref[peers[s]], packed).astype(BF16)
-        copies[s - 1].start()
-    far[me] = nn(sel_ref[me], packed).astype(BF16)
+    greet_end(peers)
+    copies, backs = swap(n, me, peers, row_out, far, send_a, recv_a, True)
+    row_out[...] = tn(sel_ref[...], packed).astype(BF16).reshape(n, cap, edge_w)
+    for copy in copies:
+        copy.start()
+    far[me] = row_out[me]
     self_ref[...] = nt(uin_ref[:, :feat], low)
     table_len = rows + n * cap
     lhs_ref[:, :rows] = jnp.transpose(neigh).astype(BF16)
@@ -641,7 +658,7 @@
 
 def node_forward(n, s, cnt, x, mout, gain, off, expand, contract, gain2, off2, sel, uin):
     rows, feat = x.shape
-    cap = sel.shape[1]
+    cap = sel.shape[1] // n
     edge_w = uin.shape[0]
     table_len = rows + n * cap
     hidden = expand.shape[1]
@@ -649,26 +666,24 @@
             (x.shape, F32), ((rows, 1), F32), ((rows, hidden), BF16), ((rows, hidden), F32)]
     scratch = [pltpu.VMEM((n, cap, edge_w), BF16)] * 2 + [pltpu.SemaphoreType.DMA((n,))] * 2
     return vmem_call(functools.partial(node_forward_body, n),
-                     (s, cnt, x, mout, gain, off, expand, contract, gain2, off2, sel, uin), outs, scratch, 1, "node_forward")
+                     [s, cnt] + far_off(x, mout, gain, off) + [expand, contract] + far_off(gain2, off2) + [sel, uin], outs, scratch, 1,
+                     "node_forward")
 
 
 def swap_back_start(n, me, peers, gin, sel_ref, row_out, far, send, recv, rows):
-    cap = sel_ref.shape[1]
-    copies, backs = swap(n, me, peers, row_out, far, send, recv)
-    for s in range(1, n):
-        start = pl.multiple_of(rows + peers[s] * cap, cap)
-        row_out[s] = gin[pl.ds(start, cap), :].astype(BF16)
-        copies[s - 1].start()
-    far[me] = gin[pl.ds(pl.multiple_of(rows + me * cap, cap), cap), :].astype(BF16)
+    cap = sel_ref.shape[1] // n
+    copies, backs = swap(n, me, peers, row_out, far, send, recv, True)
+    row_out[...] = gin[pl.ds(rows, n * cap), :].astype(BF16).reshape(n, cap, gin.shape[1])
+    for copy in copies:
+        copy.start()
+    far[me] = row_out[me]
     return copies, backs
 
 
 def swap_back_finish(n, copies, gin, sel_ref, far, rows):
-    cap = sel_ref.shape[1]
-    width = gin.shape[1]
     for copy in copies[1]:
         copy.wait_recv()
-    total = gin[:rows, :] + tn(sel_ref[...].reshape(n * cap, rows), far[...].reshape(n * cap, width))
+    total = gin[:rows, :] + nn(sel_ref[...], far[...].reshape(sel_ref.shape[1], gin.shape[1]))
     for copy in copies[0]:
         copy.wait_send()
     return total.astype(BF16)
@@ -681,30 +696,39 @@
     me, peers = ring_place(n)
     rows, feat = node_ref.shape
     edge_w = uin_ref.shape[0]
-    greet(peers)
-    copies = swap_back_start(n, me, peers, gin_ref, sel_ref, row_out, far, send_a, recv_a, rows)
-    own = swap_back_finish(n, copies, gin_ref, sel_ref, far, rows)
+    greet_start(peers)
+    line = lambda ref: ref[...].astype(F32).reshape(1, feat)
     table_len = gin_ref.shape[0] - edge_w
     dself_t = dself_ref[...].astype(BF16)
     dself = jnp.transpose(dself_ref[...]).astype(BF16)
+    greet_end(peers)
+    copies = swap_back_start(n, me, peers, gin_ref, sel_ref, row_out, far, send_a, recv_a, rows)
     node = node_ref[...]
     at = early_rows(feat, acted_ref.shape[1], edge_w)
     pack(chunks, at["update_self"], nn(dself_t, node))
-    pack(chunks, at["update_neigh"], tn(own, node))
     gap = jnp.zeros((edge_w, 256 - edge_w), F32)
     pack(chunks, at["update_edge"], jnp.concatenate([jnp.transpose(gin_ref[table_len:, :]), gap, gumid_ref[...], gap], axis=1))
     pack(chunks, at["update_out"], jnp.concatenate([guout_ref[...], jnp.zeros((edge_w, feat - edge_w), F32)], axis=1))
-    dy = cot_ref[...].astype(F32) + nn(dself, uin_ref[:, :feat]) + nn(own, uin_ref[:, feat : 2 * feat])
+    side = jnp.zeros((1, feat - edge_w), F32)
+    edge_sums = [jnp.concatenate([jnp.sum(jnp.transpose(ref[...]), axis=0, keepdims=True), side], axis=1) for ref in (ggain_ref, goff_ref)]
+    used = at["end"]
+    spare = sum(c.shape[0] * c.shape[1] for c in chunks) - used
+    if spare:
+        pack(chunks, used, jnp.zeros((spare, feat), F32))
+    dy = cot_ref[...].astype(F32) + nn(dself, uin_ref[:, :feat])
+    own = swap_back_finish(n, copies, gin_ref, sel_ref, far, rows)
+    dy = dy + nn(own, uin_ref[:, feat : 2 * feat])
+    pack(chunks, at["update_neigh"], tn(own, node))
     h2 = h2_ref[...]
     ffn_sums = [jnp.sum(dy * h2, axis=0, keepdims=True), jnp.sum(dy, axis=0, keepdims=True)]
-    second = row_norm_back(dy * gain2_ref[...].astype(F32), h2, r2_ref[...])
+    second = row_norm_back(dy * line(gain2_ref), h2, r2_ref[...])
     dffn = second.astype(BF16)
     for b in range(acted_ref.shape[1] // feat):
         pack(chunks, at["contract"] + b * feat, tn(acted_ref[:, b * feat : (b + 1) * feat], dffn))
     dinner = (nt(dffn, con_ref[...]) * slope_ref[...]).astype(BF16)
     h1 = h1_ref[...]
-    gain = gain_ref[...].astype(F32)
-    first_low = (h1 * gain + off_ref[...].astype(F32)).astype(BF16)
+    gain = line(gain_ref)
+    first_low = (h1 * gain + line(off_ref)).astype(BF16)
     for b in range(acted_ref.shape[1] // feat):
         pack(chunks, at["expand"] + b * feat, tn(first_low, dinner[:, b * feat : (b + 1) * feat]))
     dy = second + nt(dinner, exp_ref[...])
@@ -714,14 +738,7 @@
     back = (jnp.transpose(dfirst) / jnp.maximum(cnt_ref[...], 1.0)).astype(BF16)
     d2_ref[...] = nn(mout_ref[...], back)
     pack(chunks, at["message_out"], nt(s_ref[...].astype(BF16), back))
-    side = jnp.zeros((1, feat - edge_w), F32)
-    for ref in (ggain_ref, goff_ref):
-        sums.append(jnp.concatenate([jnp.sum(jnp.transpose(ref[...]), axis=0, keepdims=True), side], axis=1))
-    pack(chunks, at["vectors"], jnp.concatenate(sums + [jnp.zeros((10, feat), F32)], axis=0))
-    used = at["end"]
-    spare = sum(c.shape[0] * c.shape[1] for c in chunks) - used
-    if spare:
-        pack(chunks, used, jnp.zeros((spare, feat), F32))
+    pack(chunks, at["vectors"], jnp.concatenate(sums + edge_sums + [jnp.zeros((10, feat), F32)], axis=0))
 
 
 def early_rows(feat, hidden, edge_w):
@@ -737,21 +754,41 @@
 def node_backward(n, gin, dself, sel, node, cot, uin, h1, r1, h2, r2, acted, slope, gain, off, gain2, expand, contract, s, cnt, mout,
                   ggain, goff, gumid, guout, depths):
     rows, feat = node.shape
-    cap = sel.shape[1]
+    cap = sel.shape[1] // n
     edge_w = uin.shape[0]
     outs = [(node.shape, F32), ((feat, rows), F32)] + [((16, d, LANES), BF16) for d in depths]
     scratch = [pltpu.VMEM((n, cap, edge_w), BF16)] * 2 + [pltpu.SemaphoreType.DMA((n,))] * 2
     return vmem_call(functools.partial(node_backward_body, n),
-                     (gin, dself, sel, node, cot, uin, h1, r1, h2, r2, acted, slope, gain, off, gain2, expand, contract, s, cnt, mout,
-                      ggain, goff, gumid, guout), outs, scratch, 2, "node_backward")
-
-
-EARLY_STEPS = {0: (0, 1, 2), 1: (0, 1), 3: (0, 2), 4: (1,), 5: (0,)}
+                     [gin, dself, sel, node] + far_off(cot) + [uin, h1, r1, h2, r2, acted, slope] + far_off(gain, off, gain2)
+                     + [expand, contract, s, cnt] + far_off(mout) + [ggain, goff, gumid, guout], outs, scratch, 2, "node_backward",
+                     (0, 1))
+
+
+EARLY_ORDER = (
+    ((0, 0),),
+    ((3, 0), (0, 1)),
+    (),
+    ((2, 0), (3, 1), (1, 0)),
+    ((0, 2), (1, 1)),
+    ((3, 2),),
+    ((0, 3), (2, 1)),
+    (),
+    ((3, 3), (1, 2)),
+    ((0, 4),),
+    ((2, 2),),
+    (),
+)
+LATE_ORDER = (
+    (1, 3), (5, 0), (0, 5), (2, 3), (5, 1), (3, 4), (4, 0), (4, 1), (5, 2), (1, 4), (0, 6), (3, 5), (4, 2), (2, 4), (1, 5),
+    (5, 3), (3, 6), (2, 5), (4, 3), (5, 4), (1, 6), (2, 6), (4, 4), (5, 5), (0, 7), (3, 7), (0, 8), (4, 5), (1, 7), (5, 6),
+    (2, 7), (4, 6), (-1, 0), (3, 8), (2, 8), (0, 9), (5, 7), (3, 9), (4, 7), (1, 8), (2, 9), (5, 8), (4, 8), (5, 9), (1, 9),
+    (4, 9),
+)
 
 
 def message_backward_body(n, table_len, slabs, early, late, *refs):
-    (e_ref, h1_ref, gp1_ref, gp2_ref, part_ref, keep_ref, nbr_ref, d2_ref, mid_ref, win_ref, x_ref, dfirst_ref, sel_ref) = refs[:13]
-    refs = refs[13:]
+    (e_ref, h1_ref, gp1_ref, gp2_ref, part_ref, keep_ref, nbr_ref, d2_ref, mid_ref, win_ref, x_ref, far_ref, dfirst_ref, sel_ref) = refs[:14]
+    refs = refs[14:]
     sources, refs = refs[:early], refs[early:]
     egrad_ref, grad_ref, results, refs = refs[0], refs[1], refs[2 : 2 + early + late], refs[2 + early + late :]
     (gmid, gin, dself_sum, row_out, far, send_a, recv_a), refs = refs[:7], refs[7:]
@@ -771,62 +808,68 @@
         for ref in (gmid, gin, dself_sum):
             ref[...] = jnp.zeros_like(ref)
 
-    for at, which in EARLY_STEPS.items():
-
-        @pl.when(step == at)
-        def _(which=which):
-            for i in which:
-                chunks[i].advance()
+    count = nbr_ref.shape[0] // slabs
+    def slot(half):
+        for at in range(count):
+            which = EARLY_ORDER[2 * at + half]
+            if which:
+
+                @pl.when(step == at)
+                def _(which=which):
+                    for i, stage in which:
+                        chunks[i].run(stage)
 
     x = edge_operand(table_len, slabs, base, e_ref, nbr_ref)
     back = d2_ref[...]
     wide = lambda ref: jnp.concatenate([ref[j] for j in range(slabs)], axis=1)
     two = jnp.concatenate([(back * keep_ref[j] * gp2_ref[j].astype(F32)).astype(BF16) for j in range(slabs)], axis=1)
     gmid[...] += nt(wide(h1_ref), two)
+
+    @pl.when(step == 0)
+    def _():
+        pl.semaphore_wait(pltpu.get_barrier_semaphore(), n + 1)
+
+    slot(0)
     one = (nn(mid_ref[...], two) * wide(gp1_ref).astype(F32)).astype(BF16)
     gin[...] += nt(x, one)
     part = nn(win_ref[2 * feat :, :], one)
     total = dself_sum[...]
     for j in range(slabs):
         cut = slice(j * rows, (j + 1) * rows)
-        egrad_ref[j] = part_ref[j] + part[:, cut]
+        egrad_ref[j] = (part_ref[j] + part[:, cut]).astype(BF16)
         total = total + one[:, cut].astype(F32)
     dself_sum[...] = total
+    slot(1)
 
     @pl.when(step == steps - 1)
     def _():
+        nodes = x_ref[...]
+        dself = jnp.transpose(dself_sum[...]).astype(BF16)
+        near = gin[:rows, :].astype(BF16)
+        beyond = gin[rows:table_len, :].astype(BF16)
+        fill(late_sources, 0, [gmid[...], gin[table_len:, :], tn(nodes, dself), tn(nodes, near) + tn(far_ref[...], beyond)])
         me, peers = ring_place(n)
         copies = swap_back_start(n, me, peers, gin, sel_ref, row_out, far, send_a, recv_a, rows)
-        first, second = late_sources
-        pack([first], 0, gmid[...])
-        pack([first], feat, gin[table_len:, :])
-        end = feat + gin.shape[0] - table_len
-        spare = first.shape[0] * first.shape[1] - end
-        if spare:
-            pack([first], end, jnp.zeros((spare, feat), F32))
-        chunks[early].advance()
-        dself = jnp.transpose(dself_sum[...]).astype(BF16)
-        nodes = x_ref[...]
-        pack([second], 0, tn(nodes, dself))
-        own = swap_back_finish(n, copies, gin, sel_ref, far, rows)
-        pack([second], feat, tn(nodes, own))
-        spare = second.shape[0] * second.shape[1] - 2 * feat
-        if spare:
-            pack([second], 2 * feat, jnp.zeros((spare, feat), F32))
-        chunks[early + 1].advance()
-        grad_ref[...] = dfirst_ref[...] + nt(dself, win_ref[:feat, :]) + nt(own, win_ref[feat : 2 * feat, :])
-        run_rounds(chunks)
-
-
-def message_backward(n, e, h1, gp1, gp2, part, keep, nbr, d2, mid, win, x, dfirst, sel, sources, late_depths, table_len, slabs):
+        for i, stage in LATE_ORDER:
+            if i < 0:
+                own = swap_back_finish(n, copies, gin, sel_ref, far, rows)
+                grad_ref[...] = dfirst_ref[...] + nt(dself, win_ref[:feat, :]) + nt(own, win_ref[feat : 2 * feat, :])
+            else:
+                chunks[i].run(stage)
+
+
+def message_backward(n, e, h1, gp1, gp2, part, keep, nbr, d2, mid, win, x, far_x, dfirst, sel, sources, late_depths, table_len, slabs):
     fan, edge_w, rows = e.shape
     feat = d2.shape[0]
-    cap = sel.shape[1]
+    cap = sel.shape[1] // n
     places = n // 2
     whole = lambda a: pl.BlockSpec(a.shape, lambda i: (0,) * a.ndim)
     slab = lambda f: pl.BlockSpec((slabs, f, rows), lambda i: (i, 0, 0))
     anywhere = pl.BlockSpec(memory_space=pl.ANY)
-    consts = (nbr, d2, mid, win, x, dfirst, sel)
+    consts = (nbr, d2, mid, win, x, far_x, dfirst, sel)
+    roomy = table_len <= 512
+    place = pltpu.VMEM if roomy else pltpu.HBM
+    sources = [pltpu.with_memory_space_constraint(c, place) for c in sources]
     depths = [s.shape[1] for s in sources] + list(late_depths)
     scratch = [pltpu.VMEM((feat, feat), F32), pltpu.VMEM((table_len + edge_w, feat), F32), pltpu.VMEM((feat, rows), F32)]
     scratch += [pltpu.VMEM((n, cap, feat), BF16)] * 2 + [pltpu.SemaphoreType.DMA((n,))] * 2
@@ -839,10 +882,10 @@
         in_specs=[slab(edge_w), slab(feat), slab(feat), slab(feat), slab(edge_w), slab(1)] + [whole(a) for a in consts]
         + [anywhere] * len(sources),
         out_specs=[slab(edge_w), whole(x)] + [anywhere] * len(depths),
-        out_shape=[jax.ShapeDtypeStruct(e.shape, F32), jax.ShapeDtypeStruct(x.shape, F32)]
-        + [jax.ShapeDtypeStruct((16, d, LANES), BF16) for d in depths],
+        out_shape=[pltpu.HBM(e.shape, BF16), pltpu.HBM(x.shape, F32)]
+        + [place((16, d, LANES), BF16) for d in depths],
         scratch_shapes=scratch,
-        compiler_params=pltpu.CompilerParams(vmem_limit_bytes=VMEM_LIMIT, collective_id=3, has_side_effects=True),
+        compiler_params=pltpu.CompilerParams(vmem_limit_bytes=(42 if roomy else 58) * 1024 * 1024, collective_id=3, has_side_effects=True),
         name="message_backward",
     )(e, h1, gp1, gp2, part, keep, *consts, *sources)
 
@@ -850,11 +893,14 @@
 def unpack_body(early, late, feat, hidden, edge_w, *refs):
     count = early + late
     sources, refs = refs[:count], refs[count:]
-    (gwin, gmid, gmout, gexp, gcon, guin, gumid, guout, gv, ge), refs = refs[:10], refs[10:]
-    held, refs = refs[:count], refs[count:]
-    (swin, smid, smout, sexp, scon, suin), load, send = refs[:6], refs[6], refs[7]
-    loads = [pltpu.make_async_copy(sources[i], held[i], load.at[i]) for i in range(count)]
-    for copy in loads:
+    (egrad, grad, node), refs = refs[:3], refs[3:]
+    (gwin, gmid, gmout, gexp, gcon, guin, egrad_out, grad_out, node_out, gumid, guout), refs = refs[:11], refs[11:]
+    vectors_out, refs = refs[:6], refs[6:]
+    held = sources
+    (swin, smid, smout, sexp, scon, suin, segrad, narrow), load, send = refs[:8], refs[8], refs[9]
+    slab = narrow.shape[0] // 4
+    edges = [pltpu.make_async_copy(egrad.at[pl.ds(b * slab, slab)], narrow.at[pl.ds(b * slab, slab)], load.at[b]) for b in range(4)]
+    for copy in edges:
         copy.start()
     at = early_rows(feat, hidden, edge_w)
     sent = []
@@ -864,31 +910,25 @@
         copy.start()
         sent.append(copy)
 
-    ready = [0]
+    push(grad, grad_out)
+    push(node, node_out)
 
     def section(bufs, row, size, width, target, top=0, left=0, lane=0):
         for value, offset in unpack(bufs, row, size, LANES):
             target[top + offset : top + offset + value.shape[0], left : left + width] = value[:, lane : lane + width].astype(F32)
 
-    def need(rows, first):
-        start = 0
-        for i in range(first, count):
-            if start < rows and i >= ready[0]:
-                loads[i].wait()
-                ready[0] = i + 1
-            start += held[i].shape[0] * held[i].shape[1]
-
+    for b in range(4):
+        edges[b].wait()
+        for k in range(b * slab, (b + 1) * slab):
+            segrad[k] = narrow[k].astype(F32)
+        push(segrad.at[pl.ds(b * slab, slab)], egrad_out.at[pl.ds(b * slab, slab)])
     front, back = held[:early], held[early:]
     for b in range(hidden // feat):
-        need(at["contract"] + (b + 1) * feat, 0)
         section(front, at["contract"] + b * feat, feat, feat, scon, top=b * feat)
         push(scon.at[pl.ds(b * feat, feat)], gcon.at[pl.ds(b * feat, feat)])
     for b in range(hidden // feat):
-        need(at["expand"] + (b + 1) * feat, 0)
         section(front, at["expand"] + b * feat, feat, feat, sexp, left=b * feat)
         push(sexp.at[:, pl.ds(b * feat, feat)], gexp.at[:, pl.ds(b * feat, feat)])
-    for copy in loads[ready[0]:]:
-        copy.wait()
     section(front, at["message_out"], feat, feat, smout)
     push(smout, gmout)
     section(front, at["update_self"], edge_w, feat, suin)
@@ -898,31 +938,33 @@
     section(front, at["update_edge"], edge_w, edge_w, gumid, lane=256)
     section(front, at["update_out"], edge_w, edge_w, guout)
     vectors = unpack(front, at["vectors"], 16, LANES)[0][0].astype(F32)
-    gv[...] = vectors[:4]
-    ge[...] = vectors[4:6, :edge_w]
-    section(back[:1], 0, feat, feat, smid)
+    for k in range(6):
+        size = vectors_out[k].shape[0]
+        vectors_out[k][...] = vectors[k : k + 1, :size].reshape(size)
+    section(back, 0, feat, feat, smid)
     push(smid, gmid)
-    section(back[:1], feat, edge_w, feat, swin, top=2 * feat)
-    section(back[1:], 0, 2 * feat, feat, swin)
+    section(back, feat, edge_w, feat, swin, top=2 * feat)
+    section(back, feat + edge_w, 2 * feat, feat, swin)
     push(swin, gwin)
     for copy in sent:
         copy.wait()
 
 
-def unpack_all(chunks, early, feat, hidden, edge_w):
+def unpack_all(chunks, egrad, grad, node, early, feat, hidden, edge_w):
     whole, anywhere = pl.BlockSpec(memory_space=pltpu.VMEM), pl.BlockSpec(memory_space=pl.ANY)
-    big = [(2 * feat + edge_w, feat), (feat, feat), (feat, feat), (feat, hidden), (hidden, feat), (edge_w, 2 * feat + edge_w)]
-    small = [(edge_w, edge_w), (edge_w, edge_w), (4, feat), (2, edge_w)]
+    big = [(2 * feat + edge_w, feat), (feat, feat), (feat, feat), (feat, hidden), (hidden, feat), (edge_w, 2 * feat + edge_w), egrad.shape]
+    small = [(edge_w, edge_w), (edge_w, edge_w), (feat,), (feat,), (feat,), (feat,), (edge_w,), (edge_w,)]
+    shapes = [jax.ShapeDtypeStruct(s, F32) for s in big] + [jax.ShapeDtypeStruct(grad.shape, F32), jax.ShapeDtypeStruct(node.shape, BF16)]
     return pl.pallas_call(
         functools.partial(unpack_body, early, len(chunks) - early, feat, hidden, edge_w),
-        in_specs=[anywhere] * len(chunks),
-        out_specs=[anywhere] * 6 + [whole] * 4,
-        out_shape=[jax.ShapeDtypeStruct(s, F32) for s in big + small],
-        scratch_shapes=[pltpu.VMEM(c.shape, BF16) for c in chunks] + [pltpu.VMEM(s, F32) for s in big]
-        + [pltpu.SemaphoreType.DMA((len(chunks),)), pltpu.SemaphoreType.DMA((16,))],
-        compiler_params=pltpu.CompilerParams(vmem_limit_bytes=VMEM_LIMIT),
+        in_specs=[whole] * len(chunks) + [anywhere] * 3,
+        out_specs=[anywhere] * 9 + [whole] * 8,
+        out_shape=shapes + [jax.ShapeDtypeStruct(s, F32) for s in small],
+        scratch_shapes=[pltpu.VMEM(s, F32) for s in big]
+        + [pltpu.VMEM(egrad.shape, BF16), pltpu.SemaphoreType.DMA((4,)), pltpu.SemaphoreType.DMA((24,))],
+        compiler_params=pltpu.CompilerParams(vmem_limit_bytes=46 * 1024 * 1024),
         name="unpack_all",
-    )(*chunks)
+    )(*chunks, *far_off(egrad, grad, node))
 
 
 def local(n, node_feats, edge_feats, node_cotan, edge_cotan, neighbour, edge_mask, fetch_rows, chain_ids, complex_flag, message_in,
@@ -937,34 +979,34 @@
     nbr = jnp.transpose(neighbour)
     mask = jnp.transpose(edge_mask)
     uin = jnp.transpose(update_in)
-    line = lambda v: v.reshape(1, -1)
-    lhs, self_t, mid_t, umid_t, uout_t, uedge, sel, tag = table_rows(
-        n, fetch_rows[0], x, line(chain_ids), line(complex_flag), message_in, message_mid, update_mid, update_out, uin
+    lhs, self_t, mid_t, umid_t, uout_t, uedge, sel, tag, gain_t, offset_t, far_x = table_rows(
+        n, fetch_rows[0], x, chain_ids, complex_flag, message_in, message_mid, update_mid, update_out, uin, gain_edge, offset_edge
     )
     table_len = lhs.shape[1] - edge_w
     slabs = next(c for c in (10, 6, 4, 2, 1) if fan % c == 0)
     h1, gp1, gp2, s, keep, cnt = message_forward(e, nbr, mask, tag, lhs, self_t, mid_t, slabs)
     node, lhs3, self3, n1, r1, n2, r2, acted, slope = node_forward(
-        n, s, cnt, x, message_out, line(gain_node), line(offset_node), expand_weight, contract_weight, line(gain_ffn), line(offset_ffn),
+        n, s, cnt, x, message_out, gain_node, offset_node, expand_weight, contract_weight, gain_ffn, offset_ffn,
         sel, uin
     )
-    column = lambda v: v.astype(F32).reshape(-1, 1)
     edge_new, part, guout, gumid, gin3, dself3, ggain, goff = edge_pass(
-        e, cot, nbr, lhs3, self3, umid_t, uout_t, update_mid, update_out, uedge, column(gain_edge), column(offset_edge), slabs
+        e, cot, nbr, lhs3, self3, umid_t, uout_t, update_mid, update_out, uedge, gain_t, offset_t, slabs
     )
     hidden = expand_weight.shape[1]
-    early_depths, late_depths = chunk_plan(n // 2, early_rows(feat, hidden, edge_w)["end"], feat + edge_w, 2 * feat)
+    early_depths, late_depths = chunk_plan(n // 2, early_rows(feat, hidden, edge_w)["end"], 3 * feat + edge_w)
     dfirst, d2, *sources = node_backward(
-        n, gin3, dself3, sel, node, node_cotan[0], uin, n1, r1, n2, r2, acted, slope, line(gain_node), line(offset_node), line(gain_ffn),
+        n, gin3, dself3, sel, node, node_cotan[0], uin, n1, r1, n2, r2, acted, slope, gain_node, offset_node, gain_ffn,
         expand_weight, contract_weight, s, cnt, message_out, ggain, goff, gumid, guout, early_depths
     )
     egrad, ngrad, *sums = message_backward(
-        n, e, h1, gp1, gp2, part, keep, nbr, d2, message_mid, message_in, x, dfirst, sel, sources, late_depths, table_len, slabs
+        n, e, h1, gp1, gp2, part, keep, nbr, d2, message_mid, message_in, x, far_x, dfirst, sel, sources, late_depths, table_len, slabs
     )
-    gwin, gmid, gmout, gexp, gcon, guin, gumid, guout, gv, ge = unpack_all(sums, len(sources), feat, hidden, edge_w)
+    gwin, gmid, gmout, gexp, gcon, guin, egrad, ngrad, node, gumid, guout, gnode, onode, gffn, offn, gedge, oedge = unpack_all(
+        sums, egrad, ngrad, node, len(sources), feat, hidden, edge_w
+    )
     native = lambda a: jnp.transpose(a, (2, 0, 1))[None]
-    return (node[None], native(edge_new), ngrad[None], native(egrad), gwin, gmid, gmout, gv[0], gv[1], gexp, gcon, gv[2], gv[3],
-            jnp.transpose(guin), gumid, guout, ge[0], ge[1])
+    return (node[None], native(edge_new), ngrad[None], native(egrad), gwin, gmid, gmout, gnode, onode, gexp, gcon, gffn, offn,
+            jnp.transpose(guin), gumid, guout, gedge, oedge)
 
 
 def solution(mesh):

time: 219 us -> 188 us (0.86)
  local copies, waits for them, and re-layouts: 16.6 us -> 0.02 us
  Pallas kernels: 200 us -> 186 us
    pallas_call x1, Pallas kernels: 97.2 us -> 87.2 us  [message_backward(): pl.pallas_call(functools.partial(message_backward_body, n, table_len, sla...]
    pallas_call x3, Pallas kernels: 47.8 us -> 38.7 us  [vmem_call(): pl.pallas_call(body, out_shape=[pltpu.HBM(s, d) if i in outside else jax....]
    unnamed x7 -> x10, local copies, waits for them, and re-layouts: 7.29 us -> 0.02 us
    reshape x6 -> x0, local copies, waits for them, and re-layouts: 6.57 us -> none  [the longest x4 5.03 us: local(): line = lambda v: v.reshape(1, -1)]
    pallas_call x1, Pallas kernels: 8.22 us -> 14.1 us  [unpack_all(): pl.pallas_call(functools.partial(unpack_body, early, len(chunks) - early,...]
    slice x2 -> x0, local copies, waits for them, and re-layouts: 2.77 us -> none  [the longest x1 1.44 us: local(): gv[3]]
where the time goes in v3:
time: 188 us; the launch traced here: 187 us
  Pallas kernels  186 us (99%)
    pallas_call x1, Pallas kernels, message_backward(): pl.pallas_call(functools.partial(message_backward_body, n, table_len, sla...  87.2 us
    pallas_call x3, Pallas kernels, vmem_call(): pl.pallas_call(body, out_shape=[pltpu.HBM(s, d) if i in outside else jax....  38.7 us
    pallas_call x1, Pallas kernels, message_forward(): pl.pallas_call(functools.partial(message_forward_body, table_len, feat, s...  23.8 us
    pallas_call x1, Pallas kernels, edge_pass(): pl.pallas_call(functools.partial(edge_body, table_len, slabs), grid=(fan...  22.4 us
    pallas_call x1, Pallas kernels, unpack_all(): pl.pallas_call(functools.partial(unpack_body, early, len(chunks) - early,...  14.1 us

profile of v3, /device:TPU:1, one launch (start us, length us, event | category | flops | bytes accessed | tf_op | source)
XLA Modules:
  0.0 187.0 jit_solution(10021621587426710123)
XLA Ops:
  0.7 0.0 copy-start
  0.7 0.0 copy-start.1
  0.7 0.0 copy-start.2
  0.7 18.4 %table_rows.1 = (bf16[528,576]{1,0:T(8,128)(2,1)S(1)}, f32[512,128]{1,0:T(8,128)S(1)}, bf16[512,512]{1,0:T(8,128)(2,1)S(1)}, bf16[192,192]{1,0:T(8,128)(2,1)S(1)...) custom-call(s32[8,32]{1,0:T(8,128)} %bitcast.36, ...), custom_call_target="tpu_custom_call" | custom-call | tf_op jit(solution)/shard_map/table_rows/pallas_call | solution.py:589
  19.1 0.0 copy-start.3
  19.1 23.8 %message_forward.1 = (bf16[60,512,128]{2,1,0:T(8,128)(2,1)}, bf16[60,512,128]{2,1,0:T(8,128)(2,1)}, bf16[60,512,128]{2,1,0:T(8,128)(2,1)}, f32[512,128]{1,0:T(8,...) custom-call(bf16[60,192,128]{2,1,0:T(8,128)(2,1)} %bitcast.24, s32[60,128]{1,0:T(8,128)} %bitcast.31, ...), custom_call_target="tpu_custom_call" | custom-call | tf_op jit(solution)/shard_map/message_forward/pallas_call | solution.py:101
  42.9 0.0 copy-done
  42.9 0.0 copy-done.1
  42.9 0.0 copy-done.2
  42.9 7.8 %node_forward.1 = (bf16[128,512]{1,0:T(8,128)(2,1)S(1)}, bf16[192,576]{1,0:T(8,128)(2,1)S(1)}, f32[192,128]{1,0:T(8,128)S(1)}, f32[128,512]{1,0:T(8,128)S(1)}, f...) custom-call(f32[512,128]{1,0:T(8,128)S(1)} %get-tuple-element.90.s_r, ...), custom_call_target="tpu_custom_call" | custom-call | tf_op jit(solution)/shard_map/node_forward/pallas_call | solution.py:589
  50.7 0.0 copy-start.4
  50.7 22.4 %edge_pass.1 = (bf16[60,192,128]{2,1,0:T(8,128)(2,1)}, f32[60,192,128]{2,1,0:T(8,128)}, f32[192,192]{1,0:T(8,128)S(1)}, f32[192,192]{1,0:T(8,128)S(1)}, f32[576,...) custom-call(bf16[60,192,128]{2,1,0:T(8,128)(2,1)} %bitcast.25, ...), custom_call_target="tpu_custom_call" | custom-call | tf_op jit(solution)/shard_map/edge_pass/pallas_call | solution.py:181
  73.1 0.0 copy-done.3
  73.1 0.0 copy-done.4
  73.1 12.5 %node_backward.1 = (f32[128,512]{1,0:T(8,128)}, f32[512,128]{1,0:T(8,128)}, bf16[16,96,512]{2,1,0:T(8,128)(2,1)S(1)}, bf16[16,96,512]{2,1,0:T(8,128)(2,1)S(1)}, ...) custom-call(f32[576,192]{1,0:T(8,128)S(1)} %get-tuple-element.102.gin_ref, ...), custom_call_target="tpu_custom_call" | custom-call | tf_op jit(solution)/shard_map/node_backward/pallas_call | solution.py:589
  85.6 87.2 %message_backward.1 = (bf16[60,192,128]{2,1,0:T(8,128)(2,1)}, f32[128,512]{1,0:T(8,128)}, bf16[16,96,512]{2,1,0:T(8,128)(2,1)S(1)}, bf16[16,96,512]{2,1,0:T(8,12...) custom-call(bf16[60,192,128]{2,1,0:T(8,128)(2,1)} %bitcast.26, ...), custom_call_target="tpu_custom_call" | custom-call | tf_op jit(solution)/shard_map/message_backward/pallas_call | solution.py:879
  172.8 14.1 %unpack_all.1 = (f32[1216,512]{1,0:T(8,128)}, f32[512,512]{1,0:T(8,128)}, f32[512,512]{1,0:T(8,128)}, f32[512,2048]{1,0:T(8,128)}, f32[2048,512]{1,0:T(8,128)}, ...) custom-call(bf16[16,96,512]{2,1,0:T(8,128)(2,1)S(1)} %get-tuple-elem, ...), custom_call_target="tpu_custom_call" | custom-call | tf_op jit(solution)/shard_map/unpack_all/pallas_call | solution.py:958
Async XLA Ops:
  0.7 42.2 %copy-start = (bf16[512,2048]{1,0:T(8,128)(2,1)S(1)}, bf16[512,2048]{1,0:T(8,128)(2,1)}, u32[]{:S(2)}) copy-start(bf16[512,2048]{1,0:T(8,128)(2,1)} %exp_ref.3) | copy-start | bytes 6291460
  0.7 42.2 %copy-start.1 = (bf16[2048,512]{1,0:T(8,128)(2,1)S(1)}, bf16[2048,512]{1,0:T(8,128)(2,1)}, u32[]{:S(2)}) copy-start(bf16[2048,512]{1,0:T(8,128)(2,1)} %con_ref.3) | copy-start | bytes 6291460
  0.7 42.2 %copy-start.2 = (bf16[1216,192]{0,1:T(8,128)(2,1)S(1)}, bf16[1216,192]{0,1:T(8,128)(2,1)}, u32[]{:S(2)}) copy-start(bf16[1216,192]{0,1:T(8,128)(2,1)} %param.41) | copy-start | bytes 1400836
  19.1 54.0 %copy-start.3 = (bf16[128,256]{1,0:T(8,128)(2,1)}, bf16[128,256]{1,0:T(8,128)(2,1)S(1)}, u32[]{:S(2)}) copy-start(bf16[128,256]{1,0:T(8,128)(2,1)S(1)} %get-tuple-element.92.sel_ref.refs_13_) | copy-start | bytes 196612
  50.7 22.4 %copy-start.4 = (bf16[128,512]{1,0:T(8,128)(2,1)}, bf16[128,512]{1,0:T(8,128)(2,1)S(1)}, u32[]{:S(2)}) copy-start(bf16[128,512]{1,0:T(8,128)(2,1)S(1)} %get-tuple-element.104.node_ref.refs_8_) | copy-start | bytes 393220

commit v4 on v3

--- a/solution.py
+++ b/solution.py
@@ -25,6 +25,15 @@
 
 def tn(a, b):
     return lax.dot_general(a, b, (((0,), (0,)), ((), ())), preferred_element_type=F32)
+
+
+def narrow_gelu(v):
+    v = v.astype(BF16)
+    square = v * v
+    t = jnp.tanh(v * (BF16(CURVE) + BF16(CURVE * CUBIC) * square))
+    half = BF16(0.5) + BF16(0.5) * t
+    slope = half + (half - half * half) * (v * (BF16(2.0 * CURVE) + BF16(6.0 * CURVE * CUBIC) * square))
+    return v * half, slope
 
 
 def gelu_parts(v):
@@ -64,9 +73,7 @@
     own_chain = own // 2
     own_flag = own % 2
     pre = nn(lhs_ref[...], edge_operand(table_len, slabs, base, e_ref, nbr_ref))
-    hidden, slope = gelu_parts(pre[:feat] + tile_lanes(self_ref[...], slabs))
-    hidden = hidden.astype(BF16)
-    slope = slope.astype(BF16)
+    hidden, slope = narrow_gelu(pre[:feat] + tile_lanes(self_ref[...], slabs))
     total = s_ref[...]
     count = cnt_ref[...]
     keeps = []
@@ -80,8 +87,8 @@
         keep_ref[j] = keep
         keeps.append(keep)
         count = count + keep
-    hidden, slope = gelu_parts(nn(mid_ref[...], hidden))
-    slope = slope.astype(BF16)
+    hidden, slope = narrow_gelu(nn(mid_ref[...], hidden))
+    hidden = hidden.astype(F32)
     for j in range(slabs):
         cut = slice(j * rows, (j + 1) * rows)
         gp2_ref[j] = slope[:, cut]
@@ -125,10 +132,8 @@
 
     x = edge_operand(table_len, slabs, base, e_ref, nbr_ref)
     self_t = tile_lanes(self_ref[...], slabs)
-    hidden_three, slope_three = gelu_parts(nn(lhs_ref[...], x) + self_t)
-    hidden_three = hidden_three.astype(BF16)
-    hidden_four, slope_four = gelu_parts(nn(mid_t_ref[...], hidden_three))
-    hidden_four = hidden_four.astype(BF16)
+    hidden_three, slope_three = narrow_gelu(nn(lhs_ref[...], x) + self_t)
+    hidden_four, slope_four = narrow_gelu(nn(mid_t_ref[...], hidden_three))
     branch = nn(out_t_ref[...], hidden_four)
     gain = gain_ref[...]
     offset = offset_ref[...]
@@ -154,9 +159,9 @@
     resid = jnp.concatenate(resid, axis=1) if slabs > 1 else resid[0]
     delta = resid.astype(BF16)
     gout_ref[...] += nt(hidden_four, delta)
-    delta_four = (nn(out_ref[...], delta) * slope_four).astype(BF16)
+    delta_four = (nn(out_ref[...], delta) * slope_four.astype(F32)).astype(BF16)
     gmid_ref[...] += nt(hidden_three, delta_four)
-    delta_three = nn(mid_ref[...], delta_four) * slope_three
+    delta_three = nn(mid_ref[...], delta_four) * slope_three.astype(F32)
     low = delta_three.astype(BF16)
     gin_ref[...] += nt(x, low)
     part = resid + nn(edge_ref[...], low)
@@ -409,6 +414,7 @@
 
 
 CHUNK_REFS = 10
+ROOMY = 512
 
 
 def chunk_scratch(places, depth):
@@ -432,10 +438,10 @@
     unit = grain(places)
     depth = lambda rows: -(-rows // (16 * unit)) * unit
     total = depth(early_rows)
-    size = min(-(-total // (4 * unit)) * unit, (total - unit) // (3 * unit) * unit)
+    steps = total // unit
     late = depth(late_rows)
     half = late // 2 // unit * unit
-    return [size, size, size, total - 3 * size], [half, late - half]
+    return [(steps + k) // 4 * unit for k in range(4)], [half, late - half]
 
 
 def pack(bufs, row, value):
@@ -516,11 +522,16 @@
     return r * (dh - jnp.mean(dh, axis=1, keepdims=True) - h * jnp.mean(dh * h, axis=1, keepdims=True))
 
 
-def table_rows_body(n, fetch_ref, x_ref, chain_ref, flag_ref, win_ref, mid_ref, umid_ref, uout_ref, uin_ref, gain_ref, off_ref,
+def table_rows_body(n, fetch_ref, x_ref, chain_ref, flag_ref, win_hbm, mid_hbm, umid_hbm, uout_hbm, uin_hbm, gain_ref, off_ref,
                     lhs_ref, self_ref, midt_ref, umidt_ref, uoutt_ref, uedge_ref, sel_ref, tag_ref, gaint_ref, offt_ref, far_ref,
-                    idx_out, idx_in, row_out, far, wants, asked, send_a, recv_a, send_b, recv_b):
+                    idx_out, idx_in, row_out, far, wants, asked, win_ref, mid_ref, umid_ref, uout_ref, uin_ref, send_a, recv_a, send_b, recv_b,
+                    load):
     me, peers = ring_place(n)
     greet_start(peers)
+    pairs = ((win_hbm, win_ref), (mid_hbm, mid_ref), (umid_hbm, umid_ref), (uout_hbm, uout_ref), (uin_hbm, uin_ref))
+    loads = [pltpu.make_async_copy(pairs[k][0], pairs[k][1], load.at[k]) for k in range(5)]
+    for copy in loads:
+        copy.start()
     rows, feat = x_ref.shape
     cap = fetch_ref.shape[1]
     edge_w = win_ref.shape[0] - 2 * feat
@@ -538,6 +549,7 @@
     x = x_ref[...]
     for p in range(n):
         wants[0:1, p * cap : (p + 1) * cap] = fetch_ref[p : p + 1, :]
+    loads[0].wait()
     self_ref[...] = jnp.transpose(nn(x, win_ref[:feat, :]))
 
     copies, backs = swap(n, me, peers, row_out, far, send_b, recv_b, True)
@@ -552,6 +564,8 @@
         copy.start()
     sel_ref[...] = hot
     far[me] = row_out[me]
+    for copy in loads[1:]:
+        copy.wait()
     midt_ref[...] = jnp.transpose(mid_ref[...])
     umidt_ref[...] = jnp.transpose(umid_ref[...])
     uoutt_ref[...] = jnp.transpose(uout_ref[...])
@@ -584,12 +598,12 @@
     return [pltpu.with_memory_space_constraint(a, pltpu.HBM) for a in arrays]
 
 
-def vmem_call(body, args, outs, scratch, collective, name, outside=()):
+def vmem_call(body, args, outs, scratch, collective, name, outside=(), raw=()):
     whole = pl.BlockSpec(memory_space=pltpu.VMEM)
     return pl.pallas_call(
         body,
         out_shape=[pltpu.HBM(s, d) if i in outside else jax.ShapeDtypeStruct(s, d) for i, (s, d) in enumerate(outs)],
-        in_specs=[whole] * len(args),
+        in_specs=[pl.BlockSpec(memory_space=pl.ANY) if i in raw else whole for i in range(len(args))],
         out_specs=[whole] * len(outs),
         scratch_shapes=scratch,
         compiler_params=pltpu.CompilerParams(vmem_limit_bytes=30 * 1024 * 1024, collective_id=collective, has_side_effects=True),
@@ -605,10 +619,11 @@
     outs = [((feat + 16, table_len + edge_w), BF16), ((feat, rows), F32), (mid.shape, BF16), (umid.shape, BF16), (uout.shape, BF16),
             ((edge_w, edge_w), BF16), ((rows, n * cap), BF16), ((1, rows), jnp.int32), ((edge_w, rows), F32), ((edge_w, rows), F32),
             ((n * cap, feat), BF16)]
-    sems = [pltpu.SemaphoreType.DMA((n,))] * 4
+    sems = [pltpu.SemaphoreType.DMA((n,))] * 4 + [pltpu.SemaphoreType.DMA((5,))]
     scratch = [pltpu.VMEM((n, 8, 128), jnp.int32)] * 2 + [pltpu.VMEM((n, cap, feat), BF16)] * 2 + [pltpu.VMEM((1, n * cap), jnp.int32)] * 2
+    scratch += [pltpu.VMEM(w.shape, BF16) for w in (win, mid, umid, uout, uin)]
     return vmem_call(functools.partial(table_rows_body, n), far_off(fetch, x, chain, flag, win, mid, umid, uout, uin, gain, off), outs,
-                     scratch + sems, 0, "table_rows", (10,))
+                     scratch + sems, 0, "table_rows", (10,), range(4, 9))
 
 
 def node_forward_body(n, s_ref, cnt_ref, x_ref, mout_ref, gain_ref, off_ref, exp_ref, con_ref, gain2_ref, off2_ref, sel_ref, uin_ref,
@@ -765,24 +780,24 @@
 
 
 EARLY_ORDER = (
-    ((0, 0),),
-    ((3, 0), (0, 1)),
+    ((2, 0),),
+    ((1, 0), (2, 1)),
     (),
-    ((2, 0), (3, 1), (1, 0)),
-    ((0, 2), (1, 1)),
-    ((3, 2),),
-    ((0, 3), (2, 1)),
+    ((1, 1), (0, 0)),
+    ((2, 2),),
     (),
-    ((3, 3), (1, 2)),
-    ((0, 4),),
-    ((2, 2),),
+    ((1, 2), (3, 0), (0, 1), (2, 3)),
+    (),
+    ((1, 3), (3, 1)),
+    ((2, 4),),
+    ((0, 2),),
     (),
 )
 LATE_ORDER = (
-    (1, 3), (5, 0), (0, 5), (2, 3), (5, 1), (3, 4), (4, 0), (4, 1), (5, 2), (1, 4), (0, 6), (3, 5), (4, 2), (2, 4), (1, 5),
-    (5, 3), (3, 6), (2, 5), (4, 3), (5, 4), (1, 6), (2, 6), (4, 4), (5, 5), (0, 7), (3, 7), (0, 8), (4, 5), (1, 7), (5, 6),
-    (2, 7), (4, 6), (-1, 0), (3, 8), (2, 8), (0, 9), (5, 7), (3, 9), (4, 7), (1, 8), (2, 9), (5, 8), (4, 8), (5, 9), (1, 9),
-    (4, 9),
+    (1, 4), (3, 2), (5, 0), (0, 3), (2, 5), (5, 1), (4, 0), (3, 3), (4, 1), (1, 5), (0, 4), (2, 6), (5, 2), (3, 4), (4, 2),
+    (1, 6), (5, 3), (0, 5), (4, 3), (3, 5), (5, 4), (2, 7), (0, 6), (2, 8), (1, 7), (3, 6), (4, 4), (5, 5), (4, 5), (0, 7),
+    (5, 6), (-1, 0), (0, 8), (3, 7), (4, 6), (3, 8), (1, 8), (5, 7), (1, 9), (4, 7), (0, 9), (5, 8), (2, 9), (4, 8), (5, 9),
+    (3, 9), (4, 9),
 )
 
 
@@ -867,7 +882,7 @@
     slab = lambda f: pl.BlockSpec((slabs, f, rows), lambda i: (i, 0, 0))
     anywhere = pl.BlockSpec(memory_space=pl.ANY)
     consts = (nbr, d2, mid, win, x, far_x, dfirst, sel)
-    roomy = table_len <= 512
+    roomy = table_len <= ROOMY
     place = pltpu.VMEM if roomy else pltpu.HBM
     sources = [pltpu.with_memory_space_constraint(c, place) for c in sources]
     depths = [s.shape[1] for s in sources] + list(late_depths)
@@ -882,7 +897,7 @@
         in_specs=[slab(edge_w), slab(feat), slab(feat), slab(feat), slab(edge_w), slab(1)] + [whole(a) for a in consts]
         + [anywhere] * len(sources),
         out_specs=[slab(edge_w), whole(x)] + [anywhere] * len(depths),
-        out_shape=[pltpu.HBM(e.shape, BF16), pltpu.HBM(x.shape, F32)]
+        out_shape=[place(e.shape, BF16), place(x.shape, F32)]
         + [place((16, d, LANES), BF16) for d in depths],
         scratch_shapes=scratch,
         compiler_params=pltpu.CompilerParams(vmem_limit_bytes=(42 if roomy else 58) * 1024 * 1024, collective_id=3, has_side_effects=True),
@@ -897,11 +912,7 @@
     (gwin, gmid, gmout, gexp, gcon, guin, egrad_out, grad_out, node_out, gumid, guout), refs = refs[:11], refs[11:]
     vectors_out, refs = refs[:6], refs[6:]
     held = sources
-    (swin, smid, smout, sexp, scon, suin, segrad, narrow), load, send = refs[:8], refs[8], refs[9]
-    slab = narrow.shape[0] // 4
-    edges = [pltpu.make_async_copy(egrad.at[pl.ds(b * slab, slab)], narrow.at[pl.ds(b * slab, slab)], load.at[b]) for b in range(4)]
-    for copy in edges:
-        copy.start()
+    (swin, smid, smout, sexp, scon, suin, segrad), send = refs[:7], refs[7]
     at = early_rows(feat, hidden, edge_w)
     sent = []
 
@@ -917,11 +928,6 @@
         for value, offset in unpack(bufs, row, size, LANES):
             target[top + offset : top + offset + value.shape[0], left : left + width] = value[:, lane : lane + width].astype(F32)
 
-    for b in range(4):
-        edges[b].wait()
-        for k in range(b * slab, (b + 1) * slab):
-            segrad[k] = narrow[k].astype(F32)
-        push(segrad.at[pl.ds(b * slab, slab)], egrad_out.at[pl.ds(b * slab, slab)])
     front, back = held[:early], held[early:]
     for b in range(hidden // feat):
         section(front, at["contract"] + b * feat, feat, feat, scon, top=b * feat)
@@ -946,25 +952,30 @@
     section(back, feat, edge_w, feat, swin, top=2 * feat)
     section(back, feat + edge_w, 2 * feat, feat, swin)
     push(swin, gwin)
+    slab = egrad.shape[0] // 4
+    for b in range(4):
+        for k in range(b * slab, (b + 1) * slab):
+            segrad[k] = egrad[k].astype(F32)
+        push(segrad.at[pl.ds(b * slab, slab)], egrad_out.at[pl.ds(b * slab, slab)])
     for copy in sent:
         copy.wait()
 
 
-def unpack_all(chunks, egrad, grad, node, early, feat, hidden, edge_w):
+def unpack_all(chunks, egrad, grad, node, early, feat, hidden, edge_w, roomy):
     whole, anywhere = pl.BlockSpec(memory_space=pltpu.VMEM), pl.BlockSpec(memory_space=pl.ANY)
     big = [(2 * feat + edge_w, feat), (feat, feat), (feat, feat), (feat, hidden), (hidden, feat), (edge_w, 2 * feat + edge_w), egrad.shape]
     small = [(edge_w, edge_w), (edge_w, edge_w), (feat,), (feat,), (feat,), (feat,), (edge_w,), (edge_w,)]
     shapes = [jax.ShapeDtypeStruct(s, F32) for s in big] + [jax.ShapeDtypeStruct(grad.shape, F32), jax.ShapeDtypeStruct(node.shape, BF16)]
     return pl.pallas_call(
         functools.partial(unpack_body, early, len(chunks) - early, feat, hidden, edge_w),
-        in_specs=[whole] * len(chunks) + [anywhere] * 3,
+        in_specs=[whole] * (len(chunks) + 3),
         out_specs=[anywhere] * 9 + [whole] * 8,
         out_shape=shapes + [jax.ShapeDtypeStruct(s, F32) for s in small],
         scratch_shapes=[pltpu.VMEM(s, F32) for s in big]
-        + [pltpu.VMEM(egrad.shape, BF16), pltpu.SemaphoreType.DMA((4,)), pltpu.SemaphoreType.DMA((24,))],
-        compiler_params=pltpu.CompilerParams(vmem_limit_bytes=46 * 1024 * 1024),
+        + [pltpu.SemaphoreType.DMA((24,))],
+        compiler_params=pltpu.CompilerParams(vmem_limit_bytes=(30 if roomy else 46) * 1024 * 1024),
         name="unpack_all",
-    )(*chunks, *far_off(egrad, grad, node))
+    )(*chunks, egrad, grad, node)
 
 
 def local(n, node_feats, edge_feats, node_cotan, edge_cotan, neighbour, edge_mask, fetch_rows, chain_ids, complex_flag, message_in,
@@ -1002,7 +1013,7 @@
         n, e, h1, gp1, gp2, part, keep, nbr, d2, message_mid, message_in, x, far_x, dfirst, sel, sources, late_depths, table_len, slabs
     )
     gwin, gmid, gmout, gexp, gcon, guin, egrad, ngrad, node, gumid, guout, gnode, onode, gffn, offn, gedge, oedge = unpack_all(
-        sums, egrad, ngrad, node, len(sources), feat, hidden, edge_w
+        sums, egrad, ngrad, node, len(sources), feat, hidden, edge_w, table_len <= ROOMY
     )
     native = lambda a: jnp.transpose(a, (2, 0, 1))[None]
     return (node[None], native(edge_new), ngrad[None], native(egrad), gwin, gmid, gmout, gnode, onode, gexp, gcon, gffn, offn,

time: 188 us -> 172 us (0.915)
  Pallas kernels: 186 us -> 171 us
    pallas_call x1, Pallas kernels: 14.1 us -> 7.87 us  [unpack_all(): pl.pallas_call(functools.partial(unpack_body, early, len(chunks) - early,...]
    pallas_call x1, Pallas kernels: 23.8 us -> 19.2 us  [message_forward(): pl.pallas_call(functools.partial(message_forward_body, table_len, feat, s...]
    pallas_call x1, Pallas kernels: 87.2 us -> 85.2 us  [message_backward(): pl.pallas_call(functools.partial(message_backward_body, n, table_len, sla...]
where the time goes in v4:
time: 172 us
  Pallas kernels  171 us (99%)
    pallas_call x1, Pallas kernels, message_backward(): pl.pallas_call(functools.partial(message_backward_body, n, table_len, sla...  85.2 us
    pallas_call x3, Pallas kernels, vmem_call(): pl.pallas_call(body, out_shape=[pltpu.HBM(s, d) if i in outside else jax....  37.6 us
    pallas_call x1, Pallas kernels, edge_pass(): pl.pallas_call(functools.partial(edge_body, table_len, slabs), grid=(fan...  20.8 us
    pallas_call x1, Pallas kernels, message_forward(): pl.pallas_call(functools.partial(message_forward_body, table_len, feat, s...  19.2 us
    pallas_call x1, Pallas kernels, unpack_all(): pl.pallas_call(functools.partial(unpack_body, early, len(chunks) - early,...  7.87 us

profile of v4, /device:TPU:1, one launch (start us, length us, event | category | flops | bytes accessed | tf_op | source)
XLA Modules:
  0.0 171.6 jit_solution(1917348999053672049)
XLA Ops:
  0.7 0.0 copy-start.2
  0.7 17.5 %table_rows.1 = (bf16[528,576]{1,0:T(8,128)(2,1)S(1)}, f32[512,128]{1,0:T(8,128)S(1)}, bf16[512,512]{1,0:T(8,128)(2,1)S(1)}, bf16[192,192]{1,0:T(8,128)(2,1)S(1)...) custom-call(s32[8,32]{1,0:T(8,128)} %bitcast.36, ...), custom_call_target="tpu_custom_call" | custom-call | tf_op jit(solution)/shard_map/table_rows/pallas_call | solution.py:603
  18.2 0.0 copy-start.3
  18.2 0.0 copy-start
  18.2 0.0 copy-start.1
  18.2 19.2 %message_forward.1 = (bf16[60,512,128]{2,1,0:T(8,128)(2,1)}, bf16[60,512,128]{2,1,0:T(8,128)(2,1)}, bf16[60,512,128]{2,1,0:T(8,128)(2,1)}, f32[512,128]{1,0:T(8,...) custom-call(bf16[60,192,128]{2,1,0:T(8,128)(2,1)} %bitcast.24, s32[60,128]{1,0:T(8,128)} %bitcast.31, ...), custom_call_target="tpu_custom_call" | custom-call | tf_op jit(solution)/shard_map/message_forward/pallas_call | solution.py:108
  37.5 0.0 copy-done.2
  37.5 0.0 copy-done
  37.5 0.0 copy-done.1
  37.5 7.8 %node_forward.1 = (bf16[128,512]{1,0:T(8,128)(2,1)S(1)}, bf16[192,576]{1,0:T(8,128)(2,1)S(1)}, f32[192,128]{1,0:T(8,128)S(1)}, f32[128,512]{1,0:T(8,128)S(1)}, f...) custom-call(f32[512,128]{1,0:T(8,128)S(1)} %get-tuple-element.90.s_r, ...), custom_call_target="tpu_custom_call" | custom-call | tf_op jit(solution)/shard_map/node_forward/pallas_call | solution.py:603
  45.3 20.8 %edge_pass.1 = (bf16[60,192,128]{2,1,0:T(8,128)(2,1)}, f32[60,192,128]{2,1,0:T(8,128)}, f32[192,192]{1,0:T(8,128)S(1)}, f32[192,192]{1,0:T(8,128)S(1)}, f32[576,...) custom-call(bf16[60,192,128]{2,1,0:T(8,128)(2,1)} %bitcast.25, ...), custom_call_target="tpu_custom_call" | custom-call | tf_op jit(solution)/shard_map/edge_pass/pallas_call | solution.py:186
  66.0 0.0 copy-done.3
  66.0 12.3 %node_backward.1 = (f32[128,512]{1,0:T(8,128)}, f32[512,128]{1,0:T(8,128)}, bf16[16,80,512]{2,1,0:T(8,128)(2,1)S(1)}, bf16[16,80,512]{2,1,0:T(8,128)(2,1)S(1)}, ...) custom-call(f32[576,192]{1,0:T(8,128)S(1)} %get-tuple-element.102.gin_ref, ...), custom_call_target="tpu_custom_call" | custom-call | tf_op jit(solution)/shard_map/node_backward/pallas_call | solution.py:603
  78.4 85.2 %message_backward.1 = (bf16[60,192,128]{2,1,0:T(8,128)(2,1)S(1)}, f32[128,512]{1,0:T(8,128)S(1)}, bf16[16,80,512]{2,1,0:T(8,128)(2,1)S(1)}, bf16[16,80,512]{2,1,...) custom-call(bf16[60,192,128]{2,1,0:T(8,128)(2,1)} %bitcast.26, ...), custom_call_target="tpu_custom_call" | custom-call | tf_op jit(solution)/shard_map/message_backward/pallas_call | solution.py:894
  163.6 7.9 %unpack_all.1 = (f32[1216,512]{1,0:T(8,128)}, f32[512,512]{1,0:T(8,128)}, f32[512,512]{1,0:T(8,128)}, f32[512,2048]{1,0:T(8,128)}, f32[2048,512]{1,0:T(8,128)}, ...) custom-call(bf16[16,80,512]{2,1,0:T(8,128)(2,1)S(1)} %get-tuple-elem, ...), custom_call_target="tpu_custom_call" | custom-call | tf_op jit(solution)/shard_map/unpack_all/pallas_call | solution.py:969
Async XLA Ops:
  0.7 36.8 %copy-start.2 = (bf16[1216,192]{0,1:T(8,128)(2,1)S(1)}, bf16[1216,192]{0,1:T(8,128)(2,1)}, u32[]{:S(2)}) copy-start(bf16[1216,192]{0,1:T(8,128)(2,1)} %param.41) | copy-start | bytes 1400836
  18.2 47.9 %copy-start.3 = (bf16[128,256]{1,0:T(8,128)(2,1)}, bf16[128,256]{1,0:T(8,128)(2,1)S(1)}, u32[]{:S(2)}) copy-start(bf16[128,256]{1,0:T(8,128)(2,1)S(1)} %get-tuple-element.92.sel_ref.refs_13_) | copy-start | bytes 196612
  18.2 19.3 %copy-start = (bf16[512,2048]{1,0:T(8,128)(2,1)S(1)}, bf16[512,2048]{1,0:T(8,128)(2,1)}, u32[]{:S(2)}) copy-start(bf16[512,2048]{1,0:T(8,128)(2,1)} %exp_ref.3) | copy-start | bytes 6291460
  18.2 19.3 %copy-start.1 = (bf16[2048,512]{1,0:T(8,128)(2,1)S(1)}, bf16[2048,512]{1,0:T(8,128)(2,1)}, u32[]{:S(2)}) copy-start(bf16[2048,512]{1,0:T(8,128)(2,1)} %con_ref.3) | copy-start | bytes 6291460

commit v5 on v4

--- a/solution.py
+++ b/solution.py
@@ -52,8 +52,8 @@
     columns = []
     for j in range(slabs):
         row = nbr_ref[pl.ds(base + j, 1), :]
-        ids = lax.broadcasted_iota(jnp.int32, (table_len, row.shape[1]), 0)
-        hot = jnp.where(ids == row, 1.0, 0.0).astype(BF16)
+        ids = lax.broadcasted_iota(jnp.int16, (table_len, row.shape[1]), 0)
+        hot = jnp.where(ids == jnp.broadcast_to(row, (16, row.shape[1])).astype(jnp.int16)[:1], BF16(1.0), BF16(0.0))
         columns.append(jnp.concatenate([hot, e_ref[j]], axis=0))
     return jnp.concatenate(columns, axis=1) if slabs > 1 else columns[0]
 
@@ -189,7 +189,7 @@
         in_specs=[slab, slab] + [whole(a) for a in consts],
         out_specs=[slab, slab] + [s for s, _ in sums],
         out_shape=[pltpu.HBM(e.shape, BF16), pltpu.HBM(e.shape, F32)] + [s for _, s in sums],
-        compiler_params=pltpu.CompilerParams(vmem_limit_bytes=30 * 1024 * 1024),
+        compiler_params=pltpu.CompilerParams(vmem_limit_bytes=42 * 1024 * 1024),
         name="edge_pass",
     )(e, cot, *consts)
 
@@ -434,14 +434,12 @@
         pl.semaphore_signal(barrier, inc=1, device_id={"tm": near, "res": far}, device_id_type=MESH)
 
 
-def chunk_plan(places, early_rows, late_rows):
+def chunk_plan(places, early_rows, late_first, late_second):
     unit = grain(places)
     depth = lambda rows: -(-rows // (16 * unit)) * unit
     total = depth(early_rows)
     steps = total // unit
-    late = depth(late_rows)
-    half = late // 2 // unit * unit
-    return [(steps + k) // 4 * unit for k in range(4)], [half, late - half]
+    return [(steps + k) // 4 * unit for k in range(4)], [depth(late_first), depth(late_second)]
 
 
 def pack(bufs, row, value):
@@ -706,7 +704,7 @@
 
 def node_backward_body(n, gin_ref, dself_ref, sel_ref, node_ref, cot_ref, uin_ref, h1_ref, r1_ref, h2_ref, r2_ref, acted_ref, slope_ref,
                        gain_ref, off_ref, gain2_ref, exp_ref, con_ref, s_ref, cnt_ref, mout_ref, ggain_ref, goff_ref,
-                       gumid_ref, guout_ref, dfirst_ref, d2_ref, *rest):
+                       gumid_ref, guout_ref, dfirst_ref, d2_ref, vec_ref, *rest):
     chunks, (row_out, far, send_a, recv_a) = rest[:-4], rest[-4:]
     me, peers = ring_place(n)
     rows, feat = node_ref.shape
@@ -753,13 +751,13 @@
     back = (jnp.transpose(dfirst) / jnp.maximum(cnt_ref[...], 1.0)).astype(BF16)
     d2_ref[...] = nn(mout_ref[...], back)
     pack(chunks, at["message_out"], nt(s_ref[...].astype(BF16), back))
-    pack(chunks, at["vectors"], jnp.concatenate(sums + edge_sums + [jnp.zeros((10, feat), F32)], axis=0))
+    vec_ref[...] = jnp.concatenate(sums + edge_sums + [jnp.zeros((10, feat), F32)], axis=0)
 
 
 def early_rows(feat, hidden, edge_w):
     at, row = {}, 0
     for name, count in (("contract", hidden), ("expand", hidden), ("message_out", feat), ("update_self", edge_w),
-                        ("update_neigh", edge_w), ("update_edge", edge_w), ("update_out", edge_w), ("vectors", 16)):
+                        ("update_neigh", edge_w), ("update_edge", edge_w), ("update_out", edge_w)):
         at[name] = row
         row += count
     at["end"] = row
@@ -771,12 +769,12 @@
     rows, feat = node.shape
     cap = sel.shape[1] // n
     edge_w = uin.shape[0]
-    outs = [(node.shape, F32), ((feat, rows), F32)] + [((16, d, LANES), BF16) for d in depths]
+    outs = [(node.shape, F32), ((feat, rows), F32), ((16, feat), F32)] + [((16, d, LANES), BF16) for d in depths]
     scratch = [pltpu.VMEM((n, cap, edge_w), BF16)] * 2 + [pltpu.SemaphoreType.DMA((n,))] * 2
     return vmem_call(functools.partial(node_backward_body, n),
                      [gin, dself, sel, node] + far_off(cot) + [uin, h1, r1, h2, r2, acted, slope] + far_off(gain, off, gain2)
                      + [expand, contract, s, cnt] + far_off(mout) + [ggain, goff, gumid, guout], outs, scratch, 2, "node_backward",
-                     (0, 1))
+                     (0, 1, 2))
 
 
 EARLY_ORDER = (
@@ -794,7 +792,7 @@
     (),
 )
 LATE_ORDER = (
-    (1, 4), (3, 2), (5, 0), (0, 3), (2, 5), (5, 1), (4, 0), (3, 3), (4, 1), (1, 5), (0, 4), (2, 6), (5, 2), (3, 4), (4, 2),
+    (1, 4), (3, 2), (5, 0), (0, 3), (2, 5), (5, 1), (3, 3), (4, 1), (1, 5), (0, 4), (2, 6), (5, 2), (3, 4), (4, 2),
     (1, 6), (5, 3), (0, 5), (4, 3), (3, 5), (5, 4), (2, 7), (0, 6), (2, 8), (1, 7), (3, 6), (4, 4), (5, 5), (4, 5), (0, 7),
     (5, 6), (-1, 0), (0, 8), (3, 7), (4, 6), (3, 8), (1, 8), (5, 7), (1, 9), (4, 7), (0, 9), (5, 8), (2, 9), (4, 8), (5, 9),
     (3, 9), (4, 9),
@@ -802,8 +800,8 @@
 
 
 def message_backward_body(n, table_len, slabs, early, late, *refs):
-    (e_ref, h1_ref, gp1_ref, gp2_ref, part_ref, keep_ref, nbr_ref, d2_ref, mid_ref, win_ref, x_ref, far_ref, dfirst_ref, sel_ref) = refs[:14]
-    refs = refs[14:]
+    (e_ref, h1_ref, gp1_ref, gp2_ref, part_ref, keep_ref, nbr_ref, d2_ref, mid_ref, win_ref, x_ref, far_ref, dfirst_ref, vec_ref, sel_ref) = refs[:15]
+    refs = refs[15:]
     sources, refs = refs[:early], refs[early:]
     egrad_ref, grad_ref, results, refs = refs[0], refs[1], refs[2 : 2 + early + late], refs[2 + early + late :]
     (gmid, gin, dself_sum, row_out, far, send_a, recv_a), refs = refs[:7], refs[7:]
@@ -862,7 +860,9 @@
         dself = jnp.transpose(dself_sum[...]).astype(BF16)
         near = gin[:rows, :].astype(BF16)
         beyond = gin[rows:table_len, :].astype(BF16)
-        fill(late_sources, 0, [gmid[...], gin[table_len:, :], tn(nodes, dself), tn(nodes, near) + tn(far_ref[...], beyond)])
+        fill(late_sources[:1], 0, [gmid[...], gin[table_len:, :], vec_ref[...]])
+        chunks[early].run(0)
+        fill(late_sources[1:], 0, [tn(nodes, dself), tn(nodes, near) + tn(far_ref[...], beyond)])
         me, peers = ring_place(n)
         copies = swap_back_start(n, me, peers, gin, sel_ref, row_out, far, send_a, recv_a, rows)
         for i, stage in LATE_ORDER:
@@ -873,7 +873,7 @@
                 chunks[i].run(stage)
 
 
-def message_backward(n, e, h1, gp1, gp2, part, keep, nbr, d2, mid, win, x, far_x, dfirst, sel, sources, late_depths, table_len, slabs):
+def message_backward(n, e, h1, gp1, gp2, part, keep, nbr, d2, mid, win, x, far_x, dfirst, vectors, sel, sources, late_depths, table_len, slabs):
     fan, edge_w, rows = e.shape
     feat = d2.shape[0]
     cap = sel.shape[1] // n
@@ -881,7 +881,7 @@
     whole = lambda a: pl.BlockSpec(a.shape, lambda i: (0,) * a.ndim)
     slab = lambda f: pl.BlockSpec((slabs, f, rows), lambda i: (i, 0, 0))
     anywhere = pl.BlockSpec(memory_space=pl.ANY)
-    consts = (nbr, d2, mid, win, x, far_x, dfirst, sel)
+    consts = (nbr, d2, mid, win, x, far_x, dfirst, vectors, sel)
     roomy = table_len <= ROOMY
     place = pltpu.VMEM if roomy else pltpu.HBM
     sources = [pltpu.with_memory_space_constraint(c, place) for c in sources]
@@ -943,14 +943,14 @@
     push(suin, guin)
     section(front, at["update_edge"], edge_w, edge_w, gumid, lane=256)
     section(front, at["update_out"], edge_w, edge_w, guout)
-    vectors = unpack(front, at["vectors"], 16, LANES)[0][0].astype(F32)
+    vectors = unpack(back[:1], feat + edge_w, 16, LANES)[0][0].astype(F32)
     for k in range(6):
         size = vectors_out[k].shape[0]
         vectors_out[k][...] = vectors[k : k + 1, :size].reshape(size)
-    section(back, 0, feat, feat, smid)
+    section(back[:1], 0, feat, feat, smid)
     push(smid, gmid)
-    section(back, feat, edge_w, feat, swin, top=2 * feat)
-    section(back, feat + edge_w, 2 * feat, feat, swin)
+    section(back[:1], feat, edge_w, feat, swin, top=2 * feat)
+    section(back[1:], 0, 2 * feat, feat, swin)
     push(swin, gwin)
     slab = egrad.shape[0] // 4
     for b in range(4):
@@ -994,23 +994,24 @@
         n, fetch_rows[0], x, chain_ids, complex_flag, message_in, message_mid, update_mid, update_out, uin, gain_edge, offset_edge
     )
     table_len = lhs.shape[1] - edge_w
-    slabs = next(c for c in (10, 6, 4, 2, 1) if fan % c == 0)
+    fit = lambda *options: next(c for c in options + (6, 4, 2, 1) if fan % c == 0)
+    slabs = fit(10)
     h1, gp1, gp2, s, keep, cnt = message_forward(e, nbr, mask, tag, lhs, self_t, mid_t, slabs)
     node, lhs3, self3, n1, r1, n2, r2, acted, slope = node_forward(
         n, s, cnt, x, message_out, gain_node, offset_node, expand_weight, contract_weight, gain_ffn, offset_ffn,
         sel, uin
     )
     edge_new, part, guout, gumid, gin3, dself3, ggain, goff = edge_pass(
-        e, cot, nbr, lhs3, self3, umid_t, uout_t, update_mid, update_out, uedge, gain_t, offset_t, slabs
+        e, cot, nbr, lhs3, self3, umid_t, uout_t, update_mid, update_out, uedge, gain_t, offset_t, fit(20, 10)
     )
     hidden = expand_weight.shape[1]
-    early_depths, late_depths = chunk_plan(n // 2, early_rows(feat, hidden, edge_w)["end"], 3 * feat + edge_w)
-    dfirst, d2, *sources = node_backward(
+    early_depths, late_depths = chunk_plan(n // 2, early_rows(feat, hidden, edge_w)["end"], feat + edge_w + 16, 2 * feat)
+    dfirst, d2, sums, *sources = node_backward(
         n, gin3, dself3, sel, node, node_cotan[0], uin, n1, r1, n2, r2, acted, slope, gain_node, offset_node, gain_ffn,
         expand_weight, contract_weight, s, cnt, message_out, ggain, goff, gumid, guout, early_depths
     )
     egrad, ngrad, *sums = message_backward(
-        n, e, h1, gp1, gp2, part, keep, nbr, d2, message_mid, message_in, x, far_x, dfirst, sel, sources, late_depths, table_len, slabs
+        n, e, h1, gp1, gp2, part, keep, nbr, d2, message_mid, message_in, x, far_x, dfirst, sums, sel, sources, late_depths, table_len, slabs
     )
     gwin, gmid, gmout, gexp, gcon, guin, egrad, ngrad, node, gumid, guout, gnode, onode, gffn, offn, gedge, oedge = unpack_all(
         sums, egrad, ngrad, node, len(sources), feat, hidden, edge_w, table_len <= ROOMY

time: 172 us -> 168 us (0.977)
  Pallas kernels: 171 us -> 167 us
    pallas_call x1, Pallas kernels: 85.2 us -> 82.6 us  [message_backward(): pl.pallas_call(functools.partial(message_backward_body, n, table_len, sla...]
where the time goes in v5:
time: 168 us
  Pallas kernels  167 us (99%)
    pallas_call x1, Pallas kernels, message_backward(): pl.pallas_call(functools.partial(message_backward_body, n, table_len, sla...  82.6 us
    pallas_call x3, Pallas kernels, vmem_call(): pl.pallas_call(body, out_shape=[pltpu.HBM(s, d) if i in outside else jax....  37.7 us
    pallas_call x1, Pallas kernels, edge_pass(): pl.pallas_call(functools.partial(edge_body, table_len, slabs), grid=(fan...  19.8 us
    pallas_call x1, Pallas kernels, message_forward(): pl.pallas_call(functools.partial(message_forward_body, table_len, feat, s...  19.2 us
    pallas_call x1, Pallas kernels, unpack_all(): pl.pallas_call(functools.partial(unpack_body, early, len(chunks) - early,...  7.87 us

profile of v5, /device:TPU:1, one launch (start us, length us, event | category | flops | bytes accessed | tf_op | source)
XLA Modules:
  0.0 168.0 jit_solution(14257855571233677298)
XLA Ops:
  0.7 0.0 copy-start.2
  0.7 17.5 %table_rows.1 = (bf16[528,576]{1,0:T(8,128)(2,1)S(1)}, f32[512,128]{1,0:T(8,128)S(1)}, bf16[512,512]{1,0:T(8,128)(2,1)S(1)}, bf16[192,192]{1,0:T(8,128)(2,1)S(1)...) custom-call(s32[8,32]{1,0:T(8,128)} %bitcast.36, ...), custom_call_target="tpu_custom_call" | custom-call | tf_op jit(solution)/shard_map/table_rows/pallas_call | solution.py:601
  18.2 0.0 copy-start.3
  18.2 0.0 copy-start
  18.2 0.0 copy-start.1
  18.2 19.2 %message_forward.1 = (bf16[60,512,128]{2,1,0:T(8,128)(2,1)}, bf16[60,512,128]{2,1,0:T(8,128)(2,1)}, bf16[60,512,128]{2,1,0:T(8,128)(2,1)}, f32[512,128]{1,0:T(8,...) custom-call(bf16[60,192,128]{2,1,0:T(8,128)(2,1)} %bitcast.24, s32[60,128]{1,0:T(8,128)} %bitcast.31, ...), custom_call_target="tpu_custom_call" | custom-call | tf_op jit(solution)/shard_map/message_forward/pallas_call | solution.py:108
  37.4 0.0 copy-done.2
  37.4 0.0 copy-done
  37.4 0.0 copy-done.1
  37.4 7.7 %node_forward.1 = (bf16[128,512]{1,0:T(8,128)(2,1)S(1)}, bf16[192,576]{1,0:T(8,128)(2,1)S(1)}, f32[192,128]{1,0:T(8,128)S(1)}, f32[128,512]{1,0:T(8,128)S(1)}, f...) custom-call(f32[512,128]{1,0:T(8,128)S(1)} %get-tuple-element.91.s_r, ...), custom_call_target="tpu_custom_call" | custom-call | tf_op jit(solution)/shard_map/node_forward/pallas_call | solution.py:601
  45.2 19.8 %edge_pass.1 = (bf16[60,192,128]{2,1,0:T(8,128)(2,1)}, f32[60,192,128]{2,1,0:T(8,128)}, f32[192,192]{1,0:T(8,128)S(1)}, f32[192,192]{1,0:T(8,128)S(1)}, f32[576,...) custom-call(bf16[60,192,128]{2,1,0:T(8,128)(2,1)} %bitcast.25, ...), custom_call_target="tpu_custom_call" | custom-call | tf_op jit(solution)/shard_map/edge_pass/pallas_call | solution.py:186
  65.0 0.0 copy-done.3
  65.0 12.4 %node_backward.1 = (f32[128,512]{1,0:T(8,128)}, f32[512,128]{1,0:T(8,128)}, f32[16,512]{1,0:T(8,128)}, bf16[16,80,512]{2,1,0:T(8,128)(2,1)S(1)}, bf16[16,80,512]...) custom-call(f32[576,192]{1,0:T(8,128)S(1)} %get-tuple-element.103.gin_ref, ...), custom_call_target="tpu_custom_call" | custom-call | tf_op jit(solution)/shard_map/node_backward/pallas_call | solution.py:601
  77.4 82.6 %message_backward.1 = (bf16[60,192,128]{2,1,0:T(8,128)(2,1)S(1)}, f32[128,512]{1,0:T(8,128)S(1)}, bf16[16,80,512]{2,1,0:T(8,128)(2,1)S(1)}, bf16[16,80,512]{2,1,...) custom-call(bf16[60,192,128]{2,1,0:T(8,128)(2,1)} %bitcast.26, ...), custom_call_target="tpu_custom_call" | custom-call | tf_op jit(solution)/shard_map/message_backward/pallas_call | solution.py:894
  160.0 7.9 %unpack_all.1 = (f32[1216,512]{1,0:T(8,128)}, f32[512,512]{1,0:T(8,128)}, f32[512,512]{1,0:T(8,128)}, f32[512,2048]{1,0:T(8,128)}, f32[2048,512]{1,0:T(8,128)}, ...) custom-call(bf16[16,80,512]{2,1,0:T(8,128)(2,1)S(1)} %get-tuple-elem, ...), custom_call_target="tpu_custom_call" | custom-call | tf_op jit(solution)/shard_map/unpack_all/pallas_call | solution.py:969
Async XLA Ops:
  0.7 36.7 %copy-start.2 = (bf16[1216,192]{0,1:T(8,128)(2,1)S(1)}, bf16[1216,192]{0,1:T(8,128)(2,1)}, u32[]{:S(2)}) copy-start(bf16[1216,192]{0,1:T(8,128)(2,1)} %param.41) | copy-start | bytes 1400836
  18.2 46.8 %copy-start.3 = (bf16[128,256]{1,0:T(8,128)(2,1)}, bf16[128,256]{1,0:T(8,128)(2,1)S(1)}, u32[]{:S(2)}) copy-start(bf16[128,256]{1,0:T(8,128)(2,1)S(1)} %get-tuple-element.93.sel_ref.refs_14_) | copy-start | bytes 196612
  18.2 19.2 %copy-start = (bf16[512,2048]{1,0:T(8,128)(2,1)S(1)}, bf16[512,2048]{1,0:T(8,128)(2,1)}, u32[]{:S(2)}) copy-start(bf16[512,2048]{1,0:T(8,128)(2,1)} %exp_ref.3) | copy-start | bytes 6291460
  18.2 19.2 %copy-start.1 = (bf16[2048,512]{1,0:T(8,128)(2,1)S(1)}, bf16[2048,512]{1,0:T(8,128)(2,1)}, u32[]{:S(2)}) copy-start(bf16[2048,512]{1,0:T(8,128)(2,1)} %con_ref.3) | copy-start | bytes 6291460

commit v6 on v5

--- a/solution.py
+++ b/solution.py
@@ -772,30 +772,30 @@
     outs = [(node.shape, F32), ((feat, rows), F32), ((16, feat), F32)] + [((16, d, LANES), BF16) for d in depths]
     scratch = [pltpu.VMEM((n, cap, edge_w), BF16)] * 2 + [pltpu.SemaphoreType.DMA((n,))] * 2
     return vmem_call(functools.partial(node_backward_body, n),
-                     [gin, dself, sel, node] + far_off(cot) + [uin, h1, r1, h2, r2, acted, slope] + far_off(gain, off, gain2)
-                     + [expand, contract, s, cnt] + far_off(mout) + [ggain, goff, gumid, guout], outs, scratch, 2, "node_backward",
+                     [gin, dself, sel, node, cot, uin, h1, r1, h2, r2, acted, slope] + far_off(gain, off, gain2)
+                     + [expand, contract, s, cnt, mout, ggain, goff, gumid, guout], outs, scratch, 2, "node_backward",
                      (0, 1, 2))
 
 
 EARLY_ORDER = (
-    ((2, 0),),
-    ((1, 0), (2, 1)),
+    ((0, 0),),
+    ((3, 0), (1, 0), (0, 1)),
     (),
-    ((1, 1), (0, 0)),
-    ((2, 2),),
+    ((1, 1),),
     (),
-    ((1, 2), (3, 0), (0, 1), (2, 3)),
+    ((0, 2),),
+    ((2, 0), (1, 2), (3, 1)),
+    ((0, 3),),
+    ((2, 1), (1, 3)),
     (),
-    ((1, 3), (3, 1)),
-    ((2, 4),),
-    ((0, 2),),
+    ((0, 4), (3, 2)),
     (),
 )
 LATE_ORDER = (
-    (1, 4), (3, 2), (5, 0), (0, 3), (2, 5), (5, 1), (3, 3), (4, 1), (1, 5), (0, 4), (2, 6), (5, 2), (3, 4), (4, 2),
-    (1, 6), (5, 3), (0, 5), (4, 3), (3, 5), (5, 4), (2, 7), (0, 6), (2, 8), (1, 7), (3, 6), (4, 4), (5, 5), (4, 5), (0, 7),
-    (5, 6), (-1, 0), (0, 8), (3, 7), (4, 6), (3, 8), (1, 8), (5, 7), (1, 9), (4, 7), (0, 9), (5, 8), (2, 9), (4, 8), (5, 9),
-    (3, 9), (4, 9),
+    (2, 2), (1, 4), (0, 5), (4, 1), (5, 0), (2, 3), (5, 1), (3, 3), (0, 6), (1, 5), (2, 4), (4, 2), (5, 2), (3, 4), (1, 6),
+    (2, 5), (5, 3), (3, 5), (4, 3), (2, 6), (0, 7), (5, 4), (3, 6), (4, 4), (5, 5), (2, 7), (4, 5), (5, 6), (-1, 0), (3, 7),
+    (1, 7), (4, 6), (2, 8), (0, 8), (0, 9), (1, 8), (5, 7), (3, 8), (4, 7), (5, 8), (1, 9), (3, 9), (2, 9), (4, 8), (5, 9),
+    (4, 9),
 )
 
 

time: 168 us -> 168 us (level)
  no operation moved by 1% of the time
where the time goes in v6:
time: 168 us; the launch traced here: 167 us
  Pallas kernels  167 us (99%)
    pallas_call x1, Pallas kernels, message_backward(): pl.pallas_call(functools.partial(message_backward_body, n, table_len, sla...  82.3 us
    pallas_call x3, Pallas kernels, vmem_call(): pl.pallas_call(body, out_shape=[pltpu.HBM(s, d) if i in outside else jax....  37.3 us
    pallas_call x1, Pallas kernels, edge_pass(): pl.pallas_call(functools.partial(edge_body, table_len, slabs), grid=(fan...  19.8 us
    pallas_call x1, Pallas kernels, message_forward(): pl.pallas_call(functools.partial(message_forward_body, table_len, feat, s...  19.2 us
    pallas_call x1, Pallas kernels, unpack_all(): pl.pallas_call(functools.partial(unpack_body, early, len(chunks) - early,...  7.87 us

profile of v6, /device:TPU:1, one launch (start us, length us, event | category | flops | bytes accessed | tf_op | source)
XLA Modules:
  0.0 167.5 jit_solution(18299288952641278247)
XLA Ops:
  0.7 0.0 copy-start.2
  0.7 17.5 %table_rows.1 = (bf16[528,576]{1,0:T(8,128)(2,1)S(1)}, f32[512,128]{1,0:T(8,128)S(1)}, bf16[512,512]{1,0:T(8,128)(2,1)S(1)}, bf16[192,192]{1,0:T(8,128)(2,1)S(1)...) custom-call(s32[8,32]{1,0:T(8,128)} %bitcast.36, ...), custom_call_target="tpu_custom_call" | custom-call | tf_op jit(solution)/shard_map/table_rows/pallas_call | solution.py:601
  18.2 0.0 copy-start.4
  18.2 0.0 copy-start
  18.2 0.0 copy-start.1
  18.2 19.2 %message_forward.1 = (bf16[60,512,128]{2,1,0:T(8,128)(2,1)}, bf16[60,512,128]{2,1,0:T(8,128)(2,1)}, bf16[60,512,128]{2,1,0:T(8,128)(2,1)}, f32[512,128]{1,0:T(8,...) custom-call(bf16[60,192,128]{2,1,0:T(8,128)(2,1)} %bitcast.25, s32[60,128]{1,0:T(8,128)} %bitcast.32, ...), custom_call_target="tpu_custom_call" | custom-call | tf_op jit(solution)/shard_map/message_forward/pallas_call | solution.py:108
  37.4 0.0 copy-done.2
  37.4 0.0 copy-done
  37.4 0.0 copy-done.1
  37.5 7.8 %node_forward.1 = (bf16[128,512]{1,0:T(8,128)(2,1)S(1)}, bf16[192,576]{1,0:T(8,128)(2,1)S(1)}, f32[192,128]{1,0:T(8,128)S(1)}, f32[128,512]{1,0:T(8,128)S(1)}, f...) custom-call(f32[512,128]{1,0:T(8,128)S(1)} %get-tuple-element.91.s_r, ...), custom_call_target="tpu_custom_call" | custom-call | tf_op jit(solution)/shard_map/node_forward/pallas_call | solution.py:601
  45.3 0.0 copy-start.3
  45.3 0.0 copy-start.5
  45.3 19.8 %edge_pass.1 = (bf16[60,192,128]{2,1,0:T(8,128)(2,1)}, f32[60,192,128]{2,1,0:T(8,128)}, f32[192,192]{1,0:T(8,128)S(1)}, f32[192,192]{1,0:T(8,128)S(1)}, f32[576,...) custom-call(bf16[60,192,128]{2,1,0:T(8,128)(2,1)} %bitcast.26, ...), custom_call_target="tpu_custom_call" | custom-call | tf_op jit(solution)/shard_map/edge_pass/pallas_call | solution.py:186
  65.1 0.0 copy-done.4
  65.1 0.0 copy-done.3
  65.1 0.0 copy-done.5
  65.1 12.0 %node_backward.1 = (f32[128,512]{1,0:T(8,128)}, f32[512,128]{1,0:T(8,128)}, f32[16,512]{1,0:T(8,128)}, bf16[16,80,512]{2,1,0:T(8,128)(2,1)S(1)}, bf16[16,80,512]...) custom-call(f32[576,192]{1,0:T(8,128)S(1)} %get-tuple-element.103.gin_ref, ...), custom_call_target="tpu_custom_call" | custom-call | tf_op jit(solution)/shard_map/node_backward/pallas_call | solution.py:601
  77.1 82.3 %message_backward.1 = (bf16[60,192,128]{2,1,0:T(8,128)(2,1)S(1)}, f32[128,512]{1,0:T(8,128)S(1)}, bf16[16,80,512]{2,1,0:T(8,128)(2,1)S(1)}, bf16[16,80,512]{2,1,...) custom-call(bf16[60,192,128]{2,1,0:T(8,128)(2,1)} %bitcast.27, ...), custom_call_target="tpu_custom_call" | custom-call | tf_op jit(solution)/shard_map/message_backward/pallas_call | solution.py:894
  159.5 7.9 %unpack_all.1 = (f32[1216,512]{1,0:T(8,128)}, f32[512,512]{1,0:T(8,128)}, f32[512,512]{1,0:T(8,128)}, f32[512,2048]{1,0:T(8,128)}, f32[2048,512]{1,0:T(8,128)}, ...) custom-call(bf16[16,80,512]{2,1,0:T(8,128)(2,1)S(1)} %get-tuple-elem, ...), custom_call_target="tpu_custom_call" | custom-call | tf_op jit(solution)/shard_map/unpack_all/pallas_call | solution.py:969
Async XLA Ops:
  0.7 36.8 %copy-start.2 = (bf16[1216,192]{0,1:T(8,128)(2,1)S(1)}, bf16[1216,192]{0,1:T(8,128)(2,1)}, u32[]{:S(2)}) copy-start(bf16[1216,192]{0,1:T(8,128)(2,1)} %param.41) | copy-start | bytes 1400836
  18.2 46.9 %copy-start.4 = (bf16[128,256]{1,0:T(8,128)(2,1)}, bf16[128,256]{1,0:T(8,128)(2,1)S(1)}, u32[]{:S(2)}) copy-start(bf16[128,256]{1,0:T(8,128)(2,1)S(1)} %get-tuple-element.93.sel_ref.refs_14_) | copy-start | bytes 196612
  18.2 19.2 %copy-start = (bf16[512,2048]{1,0:T(8,128)(2,1)S(1)}, bf16[512,2048]{1,0:T(8,128)(2,1)}, u32[]{:S(2)}) copy-start(bf16[512,2048]{1,0:T(8,128)(2,1)} %exp_ref.3) | copy-start | bytes 6291460
  18.2 19.2 %copy-start.1 = (bf16[2048,512]{1,0:T(8,128)(2,1)S(1)}, bf16[2048,512]{1,0:T(8,128)(2,1)}, u32[]{:S(2)}) copy-start(bf16[2048,512]{1,0:T(8,128)(2,1)} %con_ref.3) | copy-start | bytes 6291460
  45.3 19.8 %copy-start.3 = (bf16[512,512]{1,0:T(8,128)(2,1)S(1)}, bf16[512,512]{1,0:T(8,128)(2,1)}, u32[]{:S(2)}) copy-start(bf16[512,512]{1,0:T(8,128)(2,1)} %mout_ref.3) | copy-start | bytes 1572868
  45.3 19.8 %copy-start.5 = (bf16[1,128,512]{2,1,0:T(8,128)(2,1)S(1)}, bf16[1,128,512]{2,1,0:T(8,128)(2,1)}, u32[]{:S(2)}) copy-start(bf16[1,128,512]{2,1,0:T(8,128)(2,1)} %param.25) | copy-start | bytes 393220

commit v7 on v6

--- a/solution.py
+++ b/solution.py
@@ -168,7 +168,7 @@
     dself = dself_ref[...]
     for j in range(slabs):
         cut = slice(j * rows, (j + 1) * rows)
-        part_ref[j] = part[:, cut]
+        part_ref[j] = part[:, cut].astype(BF16)
         dself = dself + low[:, cut].astype(F32)
     dself_ref[...] = dself
 
@@ -188,7 +188,7 @@
         grid=(fan // slabs,),
         in_specs=[slab, slab] + [whole(a) for a in consts],
         out_specs=[slab, slab] + [s for s, _ in sums],
-        out_shape=[pltpu.HBM(e.shape, BF16), pltpu.HBM(e.shape, F32)] + [s for _, s in sums],
+        out_shape=[pltpu.HBM(e.shape, BF16), pltpu.HBM(e.shape, BF16)] + [s for _, s in sums],
         compiler_params=pltpu.CompilerParams(vmem_limit_bytes=42 * 1024 * 1024),
         name="edge_pass",
     )(e, cot, *consts)
@@ -849,7 +849,7 @@
     total = dself_sum[...]
     for j in range(slabs):
         cut = slice(j * rows, (j + 1) * rows)
-        egrad_ref[j] = (part_ref[j] + part[:, cut]).astype(BF16)
+        egrad_ref[j] = (part_ref[j].astype(F32) + part[:, cut]).astype(BF16)
         total = total + one[:, cut].astype(F32)
     dself_sum[...] = total
     slot(1)

time: 168 us -> 167 us (level)
  no operation moved by 1% of the time
where the time goes in v7:
time: 167 us
  Pallas kernels  166 us (99%)
    pallas_call x1, Pallas kernels, message_backward(): pl.pallas_call(functools.partial(message_backward_body, n, table_len, sla...  82.2 us
    pallas_call x3, Pallas kernels, vmem_call(): pl.pallas_call(body, out_shape=[pltpu.HBM(s, d) if i in outside else jax....  37.3 us
    pallas_call x1, Pallas kernels, edge_pass(): pl.pallas_call(functools.partial(edge_body, table_len, slabs), grid=(fan...  19.5 us
    pallas_call x1, Pallas kernels, message_forward(): pl.pallas_call(functools.partial(message_forward_body, table_len, feat, s...  19.2 us
    pallas_call x1, Pallas kernels, unpack_all(): pl.pallas_call(functools.partial(unpack_body, early, len(chunks) - early,...  7.87 us

profile of v7, /device:TPU:1, one launch (start us, length us, event | category | flops | bytes accessed | tf_op | source)
XLA Modules:
  0.0 167.0 jit_solution(11640838451273592408)
XLA Ops:
  0.7 0.0 copy-start.2
  0.7 17.5 %table_rows.1 = (bf16[528,576]{1,0:T(8,128)(2,1)S(1)}, f32[512,128]{1,0:T(8,128)S(1)}, bf16[512,512]{1,0:T(8,128)(2,1)S(1)}, bf16[192,192]{1,0:T(8,128)(2,1)S(1)...) custom-call(s32[8,32]{1,0:T(8,128)} %bitcast.36, ...), custom_call_target="tpu_custom_call" | custom-call | tf_op jit(solution)/shard_map/table_rows/pallas_call | solution.py:601
  18.2 0.0 copy-start.4
  18.2 0.0 copy-start
  18.2 0.0 copy-start.1
  18.2 19.2 %message_forward.1 = (bf16[60,512,128]{2,1,0:T(8,128)(2,1)}, bf16[60,512,128]{2,1,0:T(8,128)(2,1)}, bf16[60,512,128]{2,1,0:T(8,128)(2,1)}, f32[512,128]{1,0:T(8,...) custom-call(bf16[60,192,128]{2,1,0:T(8,128)(2,1)} %bitcast.25, s32[60,128]{1,0:T(8,128)} %bitcast.32, ...), custom_call_target="tpu_custom_call" | custom-call | tf_op jit(solution)/shard_map/message_forward/pallas_call | solution.py:108
  37.4 0.0 copy-done.2
  37.5 0.0 copy-done
  37.5 0.0 copy-done.1
  37.5 7.8 %node_forward.1 = (bf16[128,512]{1,0:T(8,128)(2,1)S(1)}, bf16[192,576]{1,0:T(8,128)(2,1)S(1)}, f32[192,128]{1,0:T(8,128)S(1)}, f32[128,512]{1,0:T(8,128)S(1)}, f...) custom-call(f32[512,128]{1,0:T(8,128)S(1)} %get-tuple-element.91.s_r, ...), custom_call_target="tpu_custom_call" | custom-call | tf_op jit(solution)/shard_map/node_forward/pallas_call | solution.py:601
  45.3 0.0 copy-start.3
  45.3 0.0 copy-start.5
  45.3 19.5 %edge_pass.1 = (bf16[60,192,128]{2,1,0:T(8,128)(2,1)}, bf16[60,192,128]{2,1,0:T(8,128)(2,1)}, f32[192,192]{1,0:T(8,128)S(1)}, f32[192,192]{1,0:T(8,128)S(1)}, f3...) custom-call(bf16[60,192,128]{2,1,0:T(8,128)(2,1)} %bitcast.26, ...), custom_call_target="tpu_custom_call" | custom-call | tf_op jit(solution)/shard_map/edge_pass/pallas_call | solution.py:186
  64.8 0.0 copy-done.4
  64.8 0.0 copy-done.3
  64.8 0.0 copy-done.5
  64.8 12.0 %node_backward.1 = (f32[128,512]{1,0:T(8,128)}, f32[512,128]{1,0:T(8,128)}, f32[16,512]{1,0:T(8,128)}, bf16[16,80,512]{2,1,0:T(8,128)(2,1)S(1)}, bf16[16,80,512]...) custom-call(f32[576,192]{1,0:T(8,128)S(1)} %get-tuple-element.103.gin_ref, ...), custom_call_target="tpu_custom_call" | custom-call | tf_op jit(solution)/shard_map/node_backward/pallas_call | solution.py:601
  76.8 82.2 %message_backward.1 = (bf16[60,192,128]{2,1,0:T(8,128)(2,1)S(1)}, f32[128,512]{1,0:T(8,128)S(1)}, bf16[16,80,512]{2,1,0:T(8,128)(2,1)S(1)}, bf16[16,80,512]{2,1,...) custom-call(bf16[60,192,128]{2,1,0:T(8,128)(2,1)} %bitcast.27, ...), custom_call_target="tpu_custom_call" | custom-call | tf_op jit(solution)/shard_map/message_backward/pallas_call | solution.py:894
  159.0 7.9 %unpack_all.1 = (f32[1216,512]{1,0:T(8,128)}, f32[512,512]{1,0:T(8,128)}, f32[512,512]{1,0:T(8,128)}, f32[512,2048]{1,0:T(8,128)}, f32[2048,512]{1,0:T(8,128)}, ...) custom-call(bf16[16,80,512]{2,1,0:T(8,128)(2,1)S(1)} %get-tuple-elem, ...), custom_call_target="tpu_custom_call" | custom-call | tf_op jit(solution)/shard_map/unpack_all/pallas_call | solution.py:969
Async XLA Ops:
  0.7 36.8 %copy-start.2 = (bf16[1216,192]{0,1:T(8,128)(2,1)S(1)}, bf16[1216,192]{0,1:T(8,128)(2,1)}, u32[]{:S(2)}) copy-start(bf16[1216,192]{0,1:T(8,128)(2,1)} %param.41) | copy-start | bytes 1400836
  18.2 46.6 %copy-start.4 = (bf16[128,256]{1,0:T(8,128)(2,1)}, bf16[128,256]{1,0:T(8,128)(2,1)S(1)}, u32[]{:S(2)}) copy-start(bf16[128,256]{1,0:T(8,128)(2,1)S(1)} %get-tuple-element.93.sel_ref.refs_14_) | copy-start | bytes 196612
  18.2 19.2 %copy-start = (bf16[512,2048]{1,0:T(8,128)(2,1)S(1)}, bf16[512,2048]{1,0:T(8,128)(2,1)}, u32[]{:S(2)}) copy-start(bf16[512,2048]{1,0:T(8,128)(2,1)} %exp_ref.3) | copy-start | bytes 6291460
  18.2 19.2 %copy-start.1 = (bf16[2048,512]{1,0:T(8,128)(2,1)S(1)}, bf16[2048,512]{1,0:T(8,128)(2,1)}, u32[]{:S(2)}) copy-start(bf16[2048,512]{1,0:T(8,128)(2,1)} %con_ref.3) | copy-start | bytes 6291460
  45.3 19.5 %copy-start.3 = (bf16[512,512]{1,0:T(8,128)(2,1)S(1)}, bf16[512,512]{1,0:T(8,128)(2,1)}, u32[]{:S(2)}) copy-start(bf16[512,512]{1,0:T(8,128)(2,1)} %mout_ref.3) | copy-start | bytes 1572868
  45.3 19.5 %copy-start.5 = (bf16[1,128,512]{2,1,0:T(8,128)(2,1)S(1)}, bf16[1,128,512]{2,1,0:T(8,128)(2,1)}, u32[]{:S(2)}) copy-start(bf16[1,128,512]{2,1,0:T(8,128)(2,1)} %param.25) | copy-start | bytes 393220
